TPU v7x, 32 devices: a whole 2x2x4 slice. The times are simulated.
32 devices in a mesh: dp: 8 (over z, y), expert: 4 (over x, core).
Axes of the slice: x: 2, y: 2, z: 4, core: 2. Of those that a mesh axis runs over, the one named last changes fastest.
Arguments:
- tokens: bfloat16 [2, 2048, 1536], P(None, ('dp', 'expert')), may hold values from -6 to 6
- cotangent: bfloat16 [2, 2048, 1536], P(None, ('dp', 'expert')), may hold values from -6 to 6
- attn_gain: bfloat16 [1536], P(('dp', 'expert')), may hold values from 0.099609375 to 1.8984375
- mlp_gain: bfloat16 [1536], P(('dp', 'expert')), may hold values from 0.099609375 to 1.8984375
- w_query: bfloat16 [1536, 1536], P(('dp', 'expert')), may hold values from -1.25 to 1.25
- w_key: bfloat16 [1536, 512], P(('dp', 'expert')), may hold values from -1.25 to 1.25
- w_value: bfloat16 [1536, 512], P(('dp', 'expert')), may hold values from -0.15625 to 0.15625
- w_out: bfloat16 [1536, 1536], P(('dp', 'expert')), may hold values from -6 to 6
- w_router: bfloat16 [1536, 20], P(('dp', 'expert')), may hold values from -0.1875 to 0.1875
- w_gate: bfloat16 [20, 1536, 512], P('expert', 'dp'), may hold values from -0.15625 to 0.15625
- w_up: bfloat16 [20, 1536, 512], P('expert', 'dp'), may hold values from -0.15625 to 0.15625
- w_down: bfloat16 [20, 512, 1536], P('expert', 'dp'), may hold values from -6 to 6
- shuffle: int32 [2, 32, 64], P(None, ('dp', 'expert')), may hold values from 0 to 63, each once within a row
- routes: int32 [2, 2048, 8], P(None, ('dp', 'expert')), may hold values from 0 to 19, all different within a row; in each aligned block of 64 rows (0 to 63, 64 to 127, ..., all dimensions but the last counted through in order) at most 32 rows name the same one
- lengths: int32 [2, 8, 1], P(None, 'dp'), may hold values from 256 to 256, as said below
Outputs:
- output: bfloat16 [2, 2048, 1536], P(None, ('dp', 'expert'))
- grad_tokens: float32 [2, 2048, 1536], P(None, ('dp', 'expert'))
- grad_attn_gain: float32 [1536], P(('dp', 'expert'))
- grad_mlp_gain: float32 [1536], P(('dp', 'expert'))
- grad_w_query: float32 [1536, 1536], P(('dp', 'expert'))
- grad_w_key: float32 [1536, 512], P(('dp', 'expert'))
- grad_w_value: float32 [1536, 512], P(('dp', 'expert'))
- grad_w_out: float32 [1536, 1536], P(('dp', 'expert'))
- grad_w_router: float32 [1536, 20], P(('dp', 'expert'))
- grad_w_gate: float32 [20, 1536, 512], P('expert', 'dp')
- grad_w_up: float32 [20, 1536, 512], P('expert', 'dp')
- grad_w_down: float32 [20, 512, 1536], P('expert', 'dp')
Inputs may be any that keep to these rules, and one draw needn't show every extreme that they name: `shuffle`: each device's entries are each number once. `routes`: each row names 8 different experts. In the dealt rows of one device (aligned blocks of 64 rows) no expert is named by more than 32 rows, a bound that some block reaches. `lengths`: A group's entries sum to 256; its documents come first, each of 256 tokens or more, and the entries after them are 0. Group 0 of every micro-batch is one document of 256 tokens.
All inputs are finite; a program needn't handle non-finite values.
Results may differ from a plain program's by a relative error of at most 0.018.
The roundings to bfloat16 on the way count: a program that leaves them out, or rounds other values in their place, can miss the bound.
Values may be sent and summed in bfloat16 or wider, within the bound.
No kernel may reach another device: no remote copies, remote signals or barrier semaphores. Data moves between devices by JAX's collectives and lax.ppermute only.
A program may use at most 192 MiB of HBM per device.

v0:
```python
import jax
import jax.numpy as jnp
from jax import lax
from jax.sharding import PartitionSpec as P

HEADS = 24
KV_HEADS = 8
HEAD_DIM = 64


EPSILON = 1e-06
ROPE_BASE = 10000.0
RESIDUAL_SCALE = 0.22
SCORE_SCALE = 1.0 / 64.0


def plain_dot(left_side, right_side):
    return jnp.dot(left_side, right_side, preferred_element_type=jnp.float32)


def inner_rows(left_side, right_side):
    return lax.dot_general(
        left_side, right_side, (((0,), (0,)), ((), ())), preferred_element_type=jnp.float32
    )


def outer_cols(left_side, right_side):
    return lax.dot_general(
        left_side, right_side, (((1,), (1,)), ((), ())), preferred_element_type=jnp.float32
    )


def rope_tables(positions):
    half_dim = HEAD_DIM // 2
    inverse = ROPE_BASE ** (-(jnp.arange(half_dim, dtype=jnp.float32) * 2.0) / HEAD_DIM)
    angles = positions.astype(jnp.float32)[:, None] * inverse[None, :]
    return (jnp.cos(angles), jnp.sin(angles))


def rotate(values, cosine_table, sine_table):
    half_dim = values.shape[-1] // 2
    first_part = values[..., :half_dim]
    second_part = values[..., half_dim:]
    cosine_part = cosine_table[:, None, :]
    sine_part = sine_table[:, None, :]
    return jnp.concatenate(
        [
            first_part * cosine_part - second_part * sine_part,
            second_part * cosine_part + first_part * sine_part,
        ],
        -1,
    )


def rotate_back(grad_values, cosine_table, sine_table):
    half_dim = grad_values.shape[-1] // 2
    first_part = grad_values[..., :half_dim]
    second_part = grad_values[..., half_dim:]
    cosine_part = cosine_table[:, None, :]
    sine_part = sine_table[:, None, :]
    return jnp.concatenate(
        [
            first_part * cosine_part + second_part * sine_part,
            second_part * cosine_part - first_part * sine_part,
        ],
        -1,
    )


def deal_rows(token_rows, order_row):
    dp_peers = lax.axis_size("dp")
    ordered = token_rows[order_row].reshape(
        dp_peers, token_rows.shape[0] // dp_peers, token_rows.shape[1]
    )
    arrived = lax.all_to_all(ordered, "dp", split_axis=0, concat_axis=0, tiled=True)
    return arrived.reshape(token_rows.shape)


def return_rows(token_rows, order_row):
    dp_peers = lax.axis_size("dp")
    arrived = lax.all_to_all(
        token_rows.reshape(dp_peers, token_rows.shape[0] // dp_peers, token_rows.shape[1]),
        "dp",
        split_axis=0,
        concat_axis=0,
        tiled=True,
    )
    inverse = (
        jnp.zeros(order_row.shape, jnp.int32)
        .at[order_row]
        .set(jnp.arange(order_row.shape[0], dtype=jnp.int32))
    )
    return arrived.reshape(token_rows.shape)[inverse]


def from_experts(slot_rows):
    return lax.all_to_all(slot_rows, "expert", split_axis=0, concat_axis=0, tiled=True)


def head_forward(query_rows, key_rows, value_rows, allowed):
    scores = outer_cols(query_rows, key_rows) * SCORE_SCALE
    scores = jnp.where(allowed, scores, -jnp.inf)
    highest = jnp.max(scores, -1, keepdims=True)
    exponent = jnp.exp(scores - highest)
    totals = jnp.sum(exponent, -1, keepdims=True)
    weights = (exponent / totals).astype(jnp.bfloat16)
    return (plain_dot(weights, value_rows), (highest + jnp.log(totals))[:, 0])


def head_backward(query_rows, key_rows, value_rows, grad_rows, logsum, allowed):
    scores = outer_cols(query_rows, key_rows) * SCORE_SCALE
    probabilities = jnp.where(allowed, jnp.exp(scores - logsum[:, None]), 0.0)
    weights = probabilities.astype(jnp.bfloat16)
    grad_probs = outer_cols(grad_rows, value_rows)
    row_delta = jnp.sum(probabilities * grad_probs, -1, keepdims=True)
    grad_scores = (probabilities * (grad_probs - row_delta) * SCORE_SCALE).astype(jnp.bfloat16)
    return (
        plain_dot(grad_scores, key_rows),
        inner_rows(grad_scores, query_rows),
        inner_rows(weights, grad_rows),
    )


def per_device(
    tokens,
    cotangent,
    attn_gain,
    mlp_gain,
    w_query,
    w_key,
    w_value,
    w_out,
    w_router,
    w_gate,
    w_up,
    w_down,
    shuffle,
    routes,
    lengths,
):
    micro_count = tokens.shape[0]
    rows_dev = tokens.shape[1]
    model_width = tokens.shape[2]
    members = lax.axis_size("expert")
    group_rows = rows_dev * members
    head_share = HEADS // KV_HEADS
    experts_all = w_router.shape[1]
    local_experts = w_gate.shape[0]
    top_count = routes.shape[2]
    capacity = (5 * rows_dev * top_count // (4 * experts_all) + 7) // 8 * 8
    assign_count = rows_dev * top_count
    first_row = lax.axis_index("expert") * rows_dev
    group_iota = jnp.arange(group_rows, dtype=jnp.int32)
    local_iota = first_row + jnp.arange(rows_dev, dtype=jnp.int32)
    expert_iota = jnp.arange(experts_all, dtype=jnp.int32)
    full_gate, full_up, full_down = (
        lax.all_gather(w_gate, "dp", axis=1, tiled=True),
        lax.all_gather(w_up, "dp", axis=1, tiled=True),
        lax.all_gather(w_down, "dp", axis=1, tiled=True),
    )
    outputs = []
    grad_list = []
    layer_sum = None
    expert_sum = None
    for step_index in range(micro_count):
        doc_lengths = lengths[step_index, 0]
        doc_ends = jnp.cumsum(doc_lengths)
        doc_starts = doc_ends - doc_lengths
        segment_all = jnp.sum((group_iota[:, None] >= doc_ends[None, :]).astype(jnp.int32), 1)
        member_of = (
            segment_all[:, None] == jnp.arange(doc_lengths.shape[0], dtype=jnp.int32)[None, :]
        )
        position_all = group_iota - jnp.sum(jnp.where(member_of, doc_starts[None, :], 0), 1)
        segment_local = lax.dynamic_slice_in_dim(segment_all, first_row, rows_dev)
        position_local = lax.dynamic_slice_in_dim(position_all, first_row, rows_dev)
        allowed_one = (segment_local[:, None] == segment_all[None, :]) & (
            group_iota[None, :] <= local_iota[:, None]
        )
        allowed = jnp.tile(allowed_one, (head_share, 1))
        gain_attn, gain_mlp, query_w, key_w, value_w, out_w, router_w = (
            lax.all_gather(attn_gain, ("dp", "expert"), axis=0, tiled=True),
            lax.all_gather(mlp_gain, ("dp", "expert"), axis=0, tiled=True),
            lax.all_gather(w_query, ("dp", "expert"), axis=0, tiled=True),
            lax.all_gather(w_key, ("dp", "expert"), axis=0, tiled=True),
            lax.all_gather(w_value, ("dp", "expert"), axis=0, tiled=True),
            lax.all_gather(w_out, ("dp", "expert"), axis=0, tiled=True),
            lax.all_gather(w_router, ("dp", "expert"), axis=0, tiled=True),
        )
        gain_first = gain_attn.astype(jnp.float32)
        gain_second = gain_mlp.astype(jnp.float32)
        inputs = tokens[step_index].astype(jnp.float32)
        inv_first = lax.rsqrt(jnp.mean(inputs * inputs, -1, keepdims=True) + EPSILON)
        unit_first = inputs * inv_first
        normed_first = (unit_first * gain_first).astype(jnp.bfloat16)
        cosine_table, sine_table = rope_tables(position_local)
        query_pre = plain_dot(normed_first, query_w).reshape(rows_dev, HEADS, HEAD_DIM)
        key_pre = plain_dot(normed_first, key_w).reshape(rows_dev, KV_HEADS, HEAD_DIM)
        value_rows = plain_dot(normed_first, value_w).astype(jnp.bfloat16)
        query_rot = rotate(query_pre, cosine_table, sine_table).astype(jnp.bfloat16)
        key_rot = (
            rotate(key_pre, cosine_table, sine_table)
            .astype(jnp.bfloat16)
            .reshape(rows_dev, KV_HEADS * HEAD_DIM)
        )
        key_group, value_group = (
            lax.all_gather(key_rot, "expert", axis=0, tiled=True),
            lax.all_gather(value_rows, "expert", axis=0, tiled=True),
        )
        query_heads = (
            query_rot.reshape(rows_dev, KV_HEADS, head_share, HEAD_DIM)
            .transpose(1, 2, 0, 3)
            .reshape(KV_HEADS, head_share * rows_dev, HEAD_DIM)
        )
        key_heads = key_group.reshape(group_rows, KV_HEADS, HEAD_DIM).transpose(1, 0, 2)
        value_heads = value_group.reshape(group_rows, KV_HEADS, HEAD_DIM).transpose(1, 0, 2)
        attended, logsum = lax.map(
            lambda head_parts: head_forward(head_parts[0], head_parts[1], head_parts[2], allowed),
            (query_heads, key_heads, value_heads),
        )
        merged = (
            attended.reshape(KV_HEADS, head_share, rows_dev, HEAD_DIM)
            .transpose(2, 0, 1, 3)
            .reshape(rows_dev, HEADS * HEAD_DIM)
            .astype(jnp.bfloat16)
        )
        attn_out = plain_dot(merged, out_w)
        hidden = inputs + RESIDUAL_SCALE * attn_out
        inv_second = lax.rsqrt(jnp.mean(hidden * hidden, -1, keepdims=True) + EPSILON)
        unit_second = hidden * inv_second
        normed_second = (unit_second * gain_second).astype(jnp.bfloat16)
        order_row = shuffle[step_index, 0]
        dealt_rows = deal_rows(normed_second, order_row)
        logits = plain_dot(dealt_rows, router_w)
        route_rows = routes[step_index]
        chosen = route_rows[:, :, None] == expert_iota[None, None, :]
        picked = jnp.sum(jnp.where(chosen, logits[:, None, :], 0.0), -1)
        gate_weights = jax.nn.softmax(picked, -1)
        flat_route = route_rows.reshape(-1)
        flat_hot = (flat_route[:, None] == expert_iota[None, :]).astype(jnp.int32)
        earlier = jnp.cumsum(flat_hot, 0) - flat_hot
        slot_index = jnp.sum(earlier * flat_hot, 1)
        position = flat_route * capacity + slot_index
        slot_owner = (
            jnp.full((experts_all * capacity,), assign_count, jnp.int32)
            .at[position]
            .set(jnp.arange(assign_count, dtype=jnp.int32))
        )
        slot_token = slot_owner // top_count
        dealt_pad = jnp.concatenate([dealt_rows, jnp.zeros((1, model_width), jnp.bfloat16)], 0)
        send_rows = dealt_pad[slot_token].reshape(members, local_experts, capacity, model_width)
        received = lax.all_to_all(send_rows, "expert", split_axis=0, concat_axis=0, tiled=True)
        gate_pre = jnp.einsum(
            "slcd,ldf->slcf", received, full_gate, preferred_element_type=jnp.float32
        )
        up_pre = jnp.einsum("slcd,ldf->slcf", received, full_up, preferred_element_type=jnp.float32)
        activated = (jax.nn.silu(gate_pre) * up_pre).astype(jnp.bfloat16)
        expert_out = jnp.einsum(
            "slcf,lfd->slcd", activated, full_down, preferred_element_type=jnp.float32
        ).astype(jnp.bfloat16)
        returned = from_experts(expert_out).reshape(experts_all * capacity, model_width)
        route_out = returned[position].reshape(rows_dev, top_count, model_width)
        combined = jnp.sum(route_out.astype(jnp.float32) * gate_weights[:, :, None], 1).astype(
            jnp.bfloat16
        )
        moe_rows = return_rows(combined, order_row)
        result = hidden + RESIDUAL_SCALE * moe_rows.astype(jnp.float32)
        outputs.append(result.astype(jnp.bfloat16))
        grad_result = cotangent[step_index].astype(jnp.float32)
        grad_moe = deal_rows((RESIDUAL_SCALE * grad_result).astype(jnp.bfloat16), order_row)
        grad_gates = jnp.sum(
            grad_moe[:, None, :].astype(jnp.float32) * route_out.astype(jnp.float32), -1
        )
        grad_picked = gate_weights * (
            grad_gates - jnp.sum(gate_weights * grad_gates, -1, keepdims=True)
        )
        grad_logits = jnp.sum(jnp.where(chosen, grad_picked[:, :, None], 0.0), 1).astype(
            jnp.bfloat16
        )
        router_grad = inner_rows(dealt_rows, grad_logits)
        grad_dealt_router = outer_cols(grad_logits, router_w)
        gate_pad = jnp.concatenate([gate_weights.reshape(-1), jnp.zeros((1,), jnp.float32)], 0)
        grad_moe_pad = jnp.concatenate([grad_moe, jnp.zeros((1, model_width), jnp.bfloat16)], 0)
        grad_send = (
            (grad_moe_pad[slot_token].astype(jnp.float32) * gate_pad[slot_owner][:, None])
            .astype(jnp.bfloat16)
            .reshape(members, local_experts, capacity, model_width)
        )
        grad_received = lax.all_to_all(grad_send, "expert", split_axis=0, concat_axis=0, tiled=True)
        grad_act = jnp.einsum(
            "slcd,lfd->slcf", grad_received, full_down, preferred_element_type=jnp.float32
        )
        down_grad = jnp.einsum(
            "slcf,slcd->lfd", activated, grad_received, preferred_element_type=jnp.float32
        )
        sigmoid_gate = jax.nn.sigmoid(gate_pre)
        silu_gate = gate_pre * sigmoid_gate
        grad_gate_pre = (
            grad_act * up_pre * sigmoid_gate * (1.0 + gate_pre * (1.0 - sigmoid_gate))
        ).astype(jnp.bfloat16)
        grad_up_pre = (grad_act * silu_gate).astype(jnp.bfloat16)
        gate_grad = jnp.einsum(
            "slcd,slcf->ldf", received, grad_gate_pre, preferred_element_type=jnp.float32
        )
        up_grad = jnp.einsum(
            "slcd,slcf->ldf", received, grad_up_pre, preferred_element_type=jnp.float32
        )
        grad_slots = (
            jnp.einsum(
                "slcf,ldf->slcd", grad_gate_pre, full_gate, preferred_element_type=jnp.float32
            )
            + jnp.einsum("slcf,ldf->slcd", grad_up_pre, full_up, preferred_element_type=jnp.float32)
        ).astype(jnp.bfloat16)
        grad_back = from_experts(grad_slots).reshape(experts_all * capacity, model_width)
        grad_dealt = (
            jnp.sum(
                grad_back[position].reshape(rows_dev, top_count, model_width).astype(jnp.float32), 1
            )
            + grad_dealt_router
        )
        grad_normed_second = return_rows(grad_dealt.astype(jnp.bfloat16), order_row).astype(
            jnp.float32
        )
        scaled_second = grad_normed_second * gain_second
        grad_hidden = grad_result + inv_second * (
            scaled_second - unit_second * jnp.mean(scaled_second * unit_second, -1, keepdims=True)
        )
        mlp_gain_grad = jnp.sum(grad_normed_second * unit_second, 0)
        grad_attn = (RESIDUAL_SCALE * grad_hidden).astype(jnp.bfloat16)
        out_grad = inner_rows(merged, grad_attn)
        grad_merged = outer_cols(grad_attn, out_w).astype(jnp.bfloat16)
        grad_heads = (
            grad_merged.reshape(rows_dev, KV_HEADS, head_share, HEAD_DIM)
            .transpose(1, 2, 0, 3)
            .reshape(KV_HEADS, head_share * rows_dev, HEAD_DIM)
        )
        grad_query_heads, grad_key_heads, grad_value_heads = lax.map(
            lambda head_parts: head_backward(
                head_parts[0], head_parts[1], head_parts[2], head_parts[3], head_parts[4], allowed
            ),
            (query_heads, key_heads, value_heads, grad_heads, logsum),
        )
        key_total = grad_key_heads.transpose(1, 0, 2).reshape(group_rows, KV_HEADS * HEAD_DIM)
        value_total = grad_value_heads.transpose(1, 0, 2).reshape(group_rows, KV_HEADS * HEAD_DIM)
        key_share, value_share = (
            lax.psum_scatter(
                key_total.astype(jnp.bfloat16), "expert", scatter_dimension=0, tiled=True
            ).astype(jnp.float32),
            lax.psum_scatter(
                value_total.astype(jnp.bfloat16), "expert", scatter_dimension=0, tiled=True
            ).astype(jnp.float32),
        )
        grad_value_rows = value_share.astype(jnp.bfloat16)
        grad_key_rows = (
            rotate_back(key_share.reshape(rows_dev, KV_HEADS, HEAD_DIM), cosine_table, sine_table)
            .reshape(rows_dev, KV_HEADS * HEAD_DIM)
            .astype(jnp.bfloat16)
        )
        grad_query_rot = (
            grad_query_heads.reshape(KV_HEADS, head_share, rows_dev, HEAD_DIM)
            .transpose(2, 0, 1, 3)
            .reshape(rows_dev, HEADS, HEAD_DIM)
        )
        grad_query_rows = (
            rotate_back(grad_query_rot, cosine_table, sine_table)
            .reshape(rows_dev, HEADS * HEAD_DIM)
            .astype(jnp.bfloat16)
        )
        query_grad = inner_rows(normed_first, grad_query_rows)
        key_grad = inner_rows(normed_first, grad_key_rows)
        value_grad = inner_rows(normed_first, grad_value_rows)
        grad_normed_first = (
            outer_cols(grad_query_rows, query_w)
            + outer_cols(grad_key_rows, key_w)
            + outer_cols(grad_value_rows, value_w)
        )
        scaled_first = grad_normed_first * gain_first
        grad_inputs = grad_hidden + inv_first * (
            scaled_first - unit_first * jnp.mean(scaled_first * unit_first, -1, keepdims=True)
        )
        attn_gain_grad = jnp.sum(grad_normed_first * unit_first, 0)
        grad_list.append(grad_inputs)
        layer_terms = (
            attn_gain_grad,
            mlp_gain_grad,
            query_grad,
            key_grad,
            value_grad,
            out_grad,
            router_grad,
        )
        expert_terms = (gate_grad, up_grad, down_grad)
        layer_terms = (
            lax.psum_scatter(attn_gain_grad, ("dp", "expert"), scatter_dimension=0, tiled=True),
            lax.psum_scatter(mlp_gain_grad, ("dp", "expert"), scatter_dimension=0, tiled=True),
            lax.psum_scatter(query_grad, ("dp", "expert"), scatter_dimension=0, tiled=True),
            lax.psum_scatter(key_grad, ("dp", "expert"), scatter_dimension=0, tiled=True),
            lax.psum_scatter(value_grad, ("dp", "expert"), scatter_dimension=0, tiled=True),
            lax.psum_scatter(out_grad, ("dp", "expert"), scatter_dimension=0, tiled=True),
            lax.psum_scatter(router_grad, ("dp", "expert"), scatter_dimension=0, tiled=True),
        )
        expert_terms = (
            lax.psum_scatter(
                gate_grad.astype(jnp.bfloat16), "dp", scatter_dimension=1, tiled=True
            ).astype(jnp.float32),
            lax.psum_scatter(
                up_grad.astype(jnp.bfloat16), "dp", scatter_dimension=1, tiled=True
            ).astype(jnp.float32),
            lax.psum_scatter(
                down_grad.astype(jnp.bfloat16), "dp", scatter_dimension=1, tiled=True
            ).astype(jnp.float32),
        )
        layer_sum = (
            layer_terms if layer_sum is None else jax.tree.map(jnp.add, layer_sum, layer_terms)
        )
        expert_sum = (
            expert_terms if expert_sum is None else jax.tree.map(jnp.add, expert_sum, expert_terms)
        )
    return (
        jnp.stack(outputs),
        jnp.stack(grad_list),
        layer_sum[0],
        layer_sum[1],
        layer_sum[2],
        layer_sum[3],
        layer_sum[4],
        layer_sum[5],
        layer_sum[6],
        expert_sum[0],
        expert_sum[1],
        expert_sum[2],
    )


def solution(mesh):
    placed = (
        P(None, ("dp", "expert"), None),
        P(None, ("dp", "expert"), None),
        P(("dp", "expert")),
        P(("dp", "expert")),
        P(("dp", "expert"), None),
        P(("dp", "expert"), None),
        P(("dp", "expert"), None),
        P(("dp", "expert"), None),
        P(("dp", "expert"), None),
        P("expert", "dp", None),
        P("expert", "dp", None),
        P("expert", "dp", None),
        P(None, ("dp", "expert"), None),
        P(None, ("dp", "expert"), None),
        P(None, "dp", None),
    )
    return jax.shard_map(
        per_device,
        mesh=mesh,
        in_specs=placed,
        out_specs=(
            P(None, ("dp", "expert"), None),
            P(None, ("dp", "expert"), None),
            P(("dp", "expert")),
            P(("dp", "expert")),
            P(("dp", "expert"), None),
            P(("dp", "expert"), None),
            P(("dp", "expert"), None),
            P(("dp", "expert"), None),
            P(("dp", "expert"), None),
            P("expert", "dp", None),
            P("expert", "dp", None),
            P("expert", "dp", None),
        ),
        check_vma=False,
    )
```

profile of v0, /device:TPU:3, one launch (start us, length us, event | category | flops | bytes accessed | tf_op | source)
XLA Modules:
  0.0 2573.7 jit_solution(1871766105182150165)
XLA Ops:
  22.5 39.0 %all-gather = bf16[32,48,20]{1,2,0:T(8,128)(2,1)S(1)} all-gather(bf16[1,48,20]{1,2,0:T(8,128)(2,1)S(1)} %bitcast.697), channel_id=1, replica_groups=mesh['dp'=8,'expert'=4] {'dp','expert'}, dimensions={0}, use_global_device_ids=true | all-gather | bytes 63360 | tf_op jit(solution)/shard_map/all_gather | solution.py:187
  62.3 39.9 %all-reduce.9 = (bf16[1536]{0:T(1024)(128)(2,1)S(1)}, bf16[1536]{0:T(1024)(128)(2,1)S(1)}) all-reduce(bf16[1536]{0:T(1024)(128)(2,1)S(1)} %dynamic-update-slice, bf16[1536]{0:T(1024)(128)(2,1)S(1)} %dynamic-update-slice.1), channel_id=1, replica_groups=mesh['dp'=8,'expert'=4] {'dp','expert'}, use_global_device_ids=true, to_apply=%add.4 | all-reduce | flops 3072 | bytes 12288
  133.6 56.9 %all-gather.9.cloned.1.call-done = bf16[1536,1536]{1,0:T(8,128)(2,1)} async-done(((bf16[48,1536]{1,0:T(8,128)(2,1)}), bf16[1536,1536]{1,0:T(8,128)(2,1)}) %all-gather.9.cloned.1.call-update) | async-done | bytes 4718608 | tf_op jit(solution)/shard_map/all_gather | solution.py:183
  213.0 42.7 %all-gather.15.cloned.1.call-done = bf16[1536,1536]{1,0:T(8,128)(2,1)} async-done(((bf16[48,1536]{1,0:T(8,128)(2,1)}), bf16[1536,1536]{1,0:T(8,128)(2,1)}) %all-gather.15.cloned.1.call-update) | async-done | bytes 4718608 | tf_op jit(solution)/shard_map/all_gather | solution.py:186
  326.0 51.5 %all-gather.21.cloned.1.call-done = bf16[5,512,1536]{2,1,0:T(8,128)(2,1)} async-done(((bf16[5,64,1536]{2,1,0:T(8,128)(2,1)}), bf16[5,512,1536]{2,1,0:T(8,128)(2,1)}) %all-gather.21.cloned.1.call-update) | async-done | bytes 7864336 | tf_op jit(solution)/shard_map/all_gather | solution.py:159
  384.0 112.2 %all-gather.19.cloned.1.call-done = bf16[5,1536,512]{2,1,0:T(8,128)(2,1)} async-done(((bf16[5,192,512]{2,1,0:T(8,128)(2,1)}), bf16[5,1536,512]{2,1,0:T(8,128)(2,1)}) %all-gather.19.cloned.1.call-update) | async-done | bytes 7864336 | tf_op jit(solution)/shard_map/all_gather | solution.py:158
  502.2 112.7 %all-gather.17.cloned.1.call-done = bf16[5,1536,512]{2,1,0:T(8,128)(2,1)} async-done(((bf16[5,192,512]{2,1,0:T(8,128)(2,1)}), bf16[5,1536,512]{2,1,0:T(8,128)(2,1)}) %all-gather.17.cloned.1.call-update) | async-done | bytes 7864336 | tf_op jit(solution)/shard_map/all_gather | solution.py:157
  635.3 24.2 all_gather.61
  690.0 34.8 %while.57 = (s32[]{:T(128)}, bf16[8,192,64]{1,2,0:T(8,128)(2,1)}, f32[8,192]{1,0:T(8,128)}, bf16[8,192,64]{2,1,0:T(8,128)(2,1)}, bf16[8,256,64]{2,1,0:T(8,128)(2...) while((s32[]{:T(128)}, bf16[8,192,64]{1,2,0:T(8,128)(2,1)}, ...), condition=%wide.region_19.20_spmd.clone, body=%wide.region_16.19_spmd.clone.sunk | while | flops 12975938 | bytes 960105 | solution.py:216
  797.3 18.8 all-to-all-done.13
  956.8 42.5 %while.58 = (s32[]{:T(128)}, f32[8,192,64]{1,2,0:T(8,128)S(1)}, bf16[8,256,64]{1,2,0:T(8,128)(2,1)S(1)}, bf16[8,256,64]{1,2,0:T(8,128)(2,1)S(1)}, bf16[8,192,64]...) while((s32[]{:T(128)}, f32[8,192,64]{1,2,0:T(8,128)S(1)}, ...), condition=%wide.region_37.38_spmd.clone, body=%wide.region_35.37_spmd.clone.sunk | while | flops 31948608 | bytes 2188153 | solution.py:336
  1005.7 42.6 %while.59 = (s32[]{:T(128)}, f32[8,192,64]{1,2,0:T(8,128)S(1)}, bf16[8,256,64]{1,2,0:T(8,128)(2,1)S(1)}, bf16[8,256,64]{1,2,0:T(8,128)(2,1)S(1)}, bf16[8,192,64]...) while((s32[]{:T(128)}, f32[8,192,64]{1,2,0:T(8,128)S(1)}, ...), condition=%wide.region_48.49_spmd.clone, body=%wide.region_46.48_spmd.clone.sunk | while | flops 31948608 | bytes 2188153 | solution.py:336
  1134.7 79.3 %reduce-scatter.54.cloned.1.call-done = f32[48,20]{1,0:T(8,128)} async-done(((f32[1536,20]{1,0:T(8,128)}), f32[48,20]{1,0:T(8,128)}) %reduce-scatter.54.cloned.1.call-update) | async-done | bytes 3856
  1227.5 44.1 %all-reduce.8 = (f32[1536]{0:T(1024)S(1)}, f32[1536]{0:T(1024)S(1)}) all-reduce(f32[1536]{0:T(1024)S(1)} %add.418, f32[1536]{0:T(1024)S(1)} %add.419), channel_id=13, replica_groups=mesh['dp'=8,'expert'=4] {'dp','expert'}, use_global_device_ids=true, to_apply=%region_53.54.clone | all-reduce | flops 3072 | bytes 24576
  1274.0 85.1 %reduce-scatter.26.cloned.1.call-done = bf16[5,192,512]{2,1,0:T(8,128)(2,1)} async-done(((bf16[5,1536,512]{2,1,0:T(8,128)(2,1)}), bf16[5,192,512]{2,1,0:T(8,128)(2,1)}) %reduce-scatter.26.cloned.1.call-update) | async-done | bytes 983056 | tf_op jit(solution)/shard_map/reduce_scatter | solution.py:402
  1359.1 142.6 %reduce-scatter.28.cloned.1.call-done = bf16[5,192,512]{2,1,0:T(8,128)(2,1)} async-done(((bf16[5,1536,512]{2,1,0:T(8,128)(2,1)}), bf16[5,192,512]{2,1,0:T(8,128)(2,1)}) %reduce-scatter.28.cloned.1.call-update) | async-done | bytes 983056 | tf_op jit(solution)/shard_map/reduce_scatter | solution.py:402
  1504.8 139.5 %reduce-scatter.30.cloned.1.call-done = bf16[5,192,512]{2,1,0:T(8,128)(2,1)} async-done(((bf16[5,1536,512]{2,1,0:T(8,128)(2,1)}), bf16[5,192,512]{2,1,0:T(8,128)(2,1)}) %reduce-scatter.30.cloned.1.call-update) | async-done | bytes 983056 | tf_op jit(solution)/shard_map/reduce_scatter | solution.py:405
  1644.3 142.6 %reduce-scatter.32.cloned.1.call-done = bf16[5,192,512]{2,1,0:T(8,128)(2,1)} async-done(((bf16[5,1536,512]{2,1,0:T(8,128)(2,1)}), bf16[5,192,512]{2,1,0:T(8,128)(2,1)}) %reduce-scatter.32.cloned.1.call-update) | async-done | bytes 983056 | tf_op jit(solution)/shard_map/reduce_scatter | solution.py:405
  1790.0 139.5 %reduce-scatter.34.cloned.1.call-done = bf16[5,64,1536]{2,1,0:T(8,128)(2,1)} async-done(((bf16[5,512,1536]{2,1,0:T(8,128)(2,1)}), bf16[5,64,1536]{2,1,0:T(8,128)(2,1)}) %reduce-scatter.34.cloned.1.call-update) | async-done | bytes 983056 | tf_op jit(solution)/shard_map/reduce_scatter | solution.py:408
  1929.5 142.6 %reduce-scatter.36.cloned.1.call-done = bf16[5,64,1536]{2,1,0:T(8,128)(2,1)} async-done(((bf16[5,512,1536]{2,1,0:T(8,128)(2,1)}), bf16[5,64,1536]{2,1,0:T(8,128)(2,1)}) %reduce-scatter.36.cloned.1.call-update) | async-done | bytes 983056 | tf_op jit(solution)/shard_map/reduce_scatter | solution.py:408
  2075.1 101.9 %reduce-scatter.40.cloned.1.call-done = f32[48,512]{1,0:T(8,128)} async-done(((f32[1536,512]{1,0:T(8,128)}), f32[48,512]{1,0:T(8,128)}) %reduce-scatter.40.cloned.1.call-update) | async-done | bytes 98320 | tf_op jit(solution)/shard_map/reduce_scatter | solution.py:396
  2177.0 106.4 %reduce-scatter.42.cloned.1.call-done = f32[48,512]{1,0:T(8,128)} async-done(((f32[1536,512]{1,0:T(8,128)}), f32[48,512]{1,0:T(8,128)}) %reduce-scatter.42.cloned.1.call-update) | async-done | bytes 98320 | tf_op jit(solution)/shard_map/reduce_scatter | solution.py:397
  2283.4 140.8 %reduce-scatter.38.cloned.1.call-done = f32[48,1536]{1,0:T(8,128)} async-done(((f32[1536,1536]{1,0:T(8,128)}), f32[48,1536]{1,0:T(8,128)}) %reduce-scatter.38.cloned.1.call-update) | async-done | bytes 294928 | tf_op jit(solution)/shard_map/reduce_scatter | solution.py:395
  2424.3 142.1 %reduce-scatter.44.cloned.1.call-done = f32[48,1536]{1,0:T(8,128)} async-done(((f32[1536,1536]{1,0:T(8,128)}), f32[48,1536]{1,0:T(8,128)}) %reduce-scatter.44.cloned.1.call-update) | async-done | bytes 294928 | tf_op jit(solution)/shard_map/reduce_scatter | solution.py:398
  (805 shorter events, 657.9 us)
Async XLA Ops:
  7.2 101.3 %all-gather.11.cloned.1.call-start = ((), (), s32[]{:S(2)}) async-start(), calls=%async_computation.32 | async-start | bytes 1622016 | tf_op jit(solution)/shard_map/all_gather | solution.py:184
  7.9 117.0 %all-gather.13.cloned.1.call-start = ((), (), s32[]{:S(2)}) async-start(), calls=%async_computation.33 | async-start | bytes 1622016 | tf_op jit(solution)/shard_map/all_gather | solution.py:185
  8.7 181.7 %all-gather.9.cloned.1.call-start = ((), (), s32[]{:S(2)}) async-start(), calls=%async_computation.31 | async-start | bytes 4866048 | tf_op jit(solution)/shard_map/all_gather | solution.py:183
  9.4 246.3 %all-gather.15.cloned.1.call-start = ((), (), s32[]{:S(2)}) async-start(), calls=%async_computation.34 | async-start | bytes 4866048 | tf_op jit(solution)/shard_map/all_gather | solution.py:186
  10.0 367.5 %all-gather.21.cloned.1.call-start = ((), (), s32[]{:S(2)}) async-start(), calls=%async_computation.37 | async-start | bytes 8847360 | tf_op jit(solution)/shard_map/all_gather | solution.py:159
  10.6 485.6 %all-gather.19.cloned.1.call-start = ((), (), s32[]{:S(2)}) async-start(), calls=%async_computation.36 | async-start | bytes 8847360 | tf_op jit(solution)/shard_map/all_gather | solution.py:158
  13.3 247.4 %all-to-all-start.8 = ((bf16[8,8,1536]{2,1,0:T(8,128)(2,1)}), bf16[8,8,1536]{2,1,0:T(8,128)(2,1)S(1)}, u32[]{:S(2)}, u32[]{:S(2)}) async-start(bf16[8,8,1536]{2,1,0:T(8,128)(2,1)} %bitcast.82), calls=%async_computation.8 | async-start | bytes 393216 | tf_op jit(solution)/shard_map/all_to_all | solution.py:75
  19.0 596.0 %all-gather.17.cloned.1.call-start = ((), (), s32[]{:S(2)}) async-start(), calls=%async_computation.35 | async-start | bytes 8847360 | tf_op jit(solution)/shard_map/all_gather | solution.py:157
  312.8 71.1 %all-to-all-start.1 = ((bf16[4,5,32,1536]{3,2,1,0:T(8,128)(2,1)}), bf16[4,5,32,1536]{3,2,1,0:T(8,128)(2,1)}, u32[]{:S(2)}, u32[]{:S(2)}) async-start(bf16[4,5,32,1536]{3,2,1,0:T(8,128)(2,1)} %bitcast.634), calls=%async_computation.1 | async-start | bytes 3932160 | tf_op jit(solution)/shard_map/all_to_all | solution.py:251
  629.5 54.0 %all-to-all-start.10 = ((bf16[4,5,32,1536]{3,2,1,0:T(8,128)(2,1)}), bf16[4,5,32,1536]{3,2,1,0:T(8,128)(2,1)S(1)}, u32[]{:S(2)}, u32[]{:S(2)}) async-start(bf16[4,5,32,1536]{3,2,1,0:T(8,128)(2,1)} %copy.284), calls=%async_computation.10 | async-start | bytes 3932160 | tf_op jit(solution)/shard_map/all_to_all | solution.py:97
  943.0 154.2 %reduce-scatter.46.cloned.1.call-start = ((), (), s32[]{:S(2)}) async-start(), calls=%async_computation.48 | async-start | bytes 327680
  1005.5 92.8 %reduce-scatter.50.cloned.1.call-start = ((), (), s32[]{:S(2)}) async-start(), calls=%async_computation.50 | async-start | bytes 327680
  1050.1 63.4 %reduce-scatter.52.cloned.1.call-start = ((), (), s32[]{:S(2)}) async-start(), calls=%async_computation.51 | async-start | bytes 327680
  1051.0 162.9 %reduce-scatter.54.cloned.1.call-start = ((), (), s32[]{:S(2)}) async-start(), calls=%async_computation.52 | async-start | bytes 811008
  1052.6 306.5 %reduce-scatter.26.cloned.1.call-start = ((), (), s32[]{:S(2)}) async-start(), calls=%async_computation.38 | async-start | bytes 8847360 | tf_op jit(solution)/shard_map/reduce_scatter | solution.py:402
  1059.7 442.1 %reduce-scatter.28.cloned.1.call-start = ((), (), s32[]{:S(2)}) async-start(), calls=%async_computation.39 | async-start | bytes 8847360 | tf_op jit(solution)/shard_map/reduce_scatter | solution.py:402
  1067.6 576.7 %reduce-scatter.30.cloned.1.call-start = ((), (), s32[]{:S(2)}) async-start(), calls=%async_computation.40 | async-start | bytes 8847360 | tf_op jit(solution)/shard_map/reduce_scatter | solution.py:405
  1074.7 712.1 %reduce-scatter.32.cloned.1.call-start = ((), (), s32[]{:S(2)}) async-start(), calls=%async_computation.41 | async-start | bytes 8847360 | tf_op jit(solution)/shard_map/reduce_scatter | solution.py:405
  1081.3 848.2 %reduce-scatter.34.cloned.1.call-start = ((), (), s32[]{:S(2)}) async-start(), calls=%async_computation.42 | async-start | bytes 8847360 | tf_op jit(solution)/shard_map/reduce_scatter | solution.py:408
  1089.2 982.8 %reduce-scatter.36.cloned.1.call-start = ((), (), s32[]{:S(2)}) async-start(), calls=%async_computation.43 | async-start | bytes 8847360 | tf_op jit(solution)/shard_map/reduce_scatter | solution.py:408
  1097.2 1079.8 %reduce-scatter.40.cloned.1.call-start = ((), (), s32[]{:S(2)}) async-start(), calls=%async_computation.45 | async-start | bytes 3244032 | tf_op jit(solution)/shard_map/reduce_scatter | solution.py:396
  1102.5 1180.9 %reduce-scatter.42.cloned.1.call-start = ((), (), s32[]{:S(2)}) async-start(), calls=%async_computation.46 | async-start | bytes 3244032 | tf_op jit(solution)/shard_map/reduce_scatter | solution.py:397
  1117.8 1306.4 %reduce-scatter.38.cloned.1.call-start = ((), (), s32[]{:S(2)}) async-start(), calls=%async_computation.44 | async-start | bytes 9732096 | tf_op jit(solution)/shard_map/reduce_scatter | solution.py:395
  1127.2 1439.2 %reduce-scatter.44.cloned.1.call-start = ((), (), s32[]{:S(2)}) async-start(), calls=%async_computation.47 | async-start | bytes 9732096 | tf_op jit(solution)/shard_map/reduce_scatter | solution.py:398
  (132 other events, 3735.8 us)
Sparse Core Ops, SparseCore 0:
  10.9 57.0 all-gather.10
  70.9 54.0 all-gather.12
  127.9 62.5 all-gather.8
  193.2 62.4 all-gather.14
  257.7 119.7 all-gather.20
  379.5 116.5 all-gather.18
  498.4 116.5 all-gather.16
  1005.7 19.2 reduce-scatter.45
  1049.3 19.1 reduce-scatter.49
  1070.8 19.9 reduce-scatter.47
  1093.4 20.0 reduce-scatter.51
  1119.0 94.8 reduce-scatter.53
  1217.6 141.4 reduce-scatter.25
  1362.6 139.0 reduce-scatter.27
  1505.2 139.0 reduce-scatter.29
  1647.8 139.0 reduce-scatter.31
  1790.4 139.0 reduce-scatter.33
  1933.0 139.0 reduce-scatter.35
  2078.1 98.9 reduce-scatter.39
  2182.9 100.5 reduce-scatter.41
  2289.9 134.3 reduce-scatter.37
  2431.7 134.6 reduce-scatter.43
where the time goes:
time: 2590 us; the launch traced here: 2570 us
  waiting for transfers between devices  1840 us (71%)
  matrix products  264 us (10%)
  blocking collectives  168 us (6%)
  local copies, waits for them, and re-layouts  139 us (5%)
  starting transfers between devices  87.3 us (3%)
  other arithmetic  53.5 us (2%)
    reduce_scatter x2, waiting for transfers between devices, per_device(): lax.psum_scatter(up_grad.astype(jnp.bfloat16), 'dp', scatter_dimension=1,...  282 us
    reduce_scatter x2, waiting for transfers between devices, per_device(): lax.psum_scatter(down_grad.astype(jnp.bfloat16), 'dp', scatter_dimension=...  282 us
    reduce_scatter x2, waiting for transfers between devices, per_device(): lax.psum_scatter(gate_grad.astype(jnp.bfloat16), 'dp', scatter_dimension=...  228 us
    reduce_scatter x1, waiting for transfers between devices, per_device(): lax.psum_scatter(out_grad, ('dp', 'expert'), scatter_dimension=0, tiled=T...  142 us
    reduce_scatter x1, waiting for transfers between devices, per_device(): lax.psum_scatter(query_grad, ('dp', 'expert'), scatter_dimension=0, tiled...  141 us
    all_gather x1, waiting for transfers between devices, per_device(): lax.all_gather(w_gate, 'dp', axis=1, tiled=True)  113 us
    all_gather x1, waiting for transfers between devices, per_device(): lax.all_gather(w_up, 'dp', axis=1, tiled=True)  112 us
    reduce_scatter x1, waiting for transfers between devices, per_device(): lax.psum_scatter(value_grad, ('dp', 'expert'), scatter_dimension=0, tiled...  106 us
  transfers between devices with their start and end apart: 38, of which 29 were waited for; matrix products, arithmetic and copies ran while one was open for 13% of the time, Pallas kernels for 0%

commit v1 on v0

v1 whole, which is shorter than its diff:
```python
import functools

import jax
import jax.numpy as jnp
from jax import lax
from jax.experimental import pallas as pl
from jax.experimental.pallas import tpu as pltpu
from jax.sharding import PartitionSpec as P

HEADS = 24
KV_HEADS = 8
HEAD_DIM = 64

EPSILON = 1e-06
ROPE_BASE = 10000.0
RESIDUAL_SCALE = 0.22
SCORE_SCALE = 1.0 / 64.0
NEGATIVE = -1e30
LANES = 128

BF16 = jnp.bfloat16
F32 = jnp.float32
ALL = ("dp", "expert")


def dot(a, b, dims=((1,), (0,))):
    return lax.dot_general(a, b, (dims, ((), ())), preferred_element_type=F32)


class Rings:
    def __init__(self, dp_count, expert_count):
        y_count = 1
        while dp_count % (2 * y_count) == 0 and 8 * y_count * y_count <= dp_count:
            y_count *= 2
        self.y, self.z = y_count, dp_count // y_count
        self.core = 2 if expert_count % 2 == 0 else 1
        self.x = expert_count // self.core
        zs, ys, xs, cs = range(self.z), range(self.y), range(self.x), range(self.core)
        self.z_groups = [[z * self.y + y for z in zs] for y in ys]
        self.table = {
            "z": ("dp", self.z, [(z * self.y + y, (z + 1) % self.z * self.y + y) for z in zs for y in ys]),
            "y": ("dp", self.y, [(z * self.y + y, z * self.y + (y + 1) % self.y) for z in zs for y in ys]),
            "x": (
                "expert",
                self.x,
                [(x * self.core + c, (x + 1) % self.x * self.core + c) for x in xs for c in cs],
            ),
            "c": (
                "expert",
                self.core,
                [(x * self.core + c, x * self.core + (c + 1) % self.core) for x in xs for c in cs],
            ),
        }
        d, e = lax.axis_index("dp"), lax.axis_index("expert")
        self.at = {"z": d // self.y, "y": d % self.y, "x": e // self.core, "c": e % self.core}

    def count(self, ring):
        return self.table[ring][1]

    def step(self, value, ring):
        axis, _, pairs = self.table[ring]
        return lax.ppermute(value, axis, pairs)

    def origin(self, ring, slot):
        return lax.rem(self.at[ring] + (self.count(ring) - slot), self.count(ring))

    def gather(self, value, ring):
        slots = [value]
        for _ in range(self.count(ring) - 1):
            slots.append(self.step(slots[-1], ring))
        return slots

    def reduce(self, parts, ring, wire=BF16):
        running = None
        for slot in range(1, self.count(ring)):
            term = parts[slot]
            if running is not None:
                term = term.astype(F32) + running.astype(F32)
            running = self.step(term.astype(wire), ring)
        own = parts[0].astype(F32)
        return own if running is None else own + running.astype(F32)

    def gather_two(self, value, first, second):
        columns = [self.gather(slot, second) for slot in self.gather(value, first)]
        return [[column[s] for column in columns] for s in range(self.count(second))]

    def reduce_two(self, parts, first, second, wire=BF16):
        partial = [
            self.reduce([parts[s][t] for s in range(self.count(second))], second, wire)
            for t in range(self.count(first))
        ]
        return self.reduce(partial, first, wire)


def in_order(slots, position_of, count):
    stacked = jnp.stack(slots)
    return [
        lax.dynamic_index_in_dim(stacked, lax.rem(position_of + (count - i), count), 0, False)
        for i in range(count)
    ]


def rotate_pairs(values, cosine, sine, direction):
    lane = lax.broadcasted_iota(jnp.int32, (values.shape[0], LANES), 1)
    low = (lane & (HEAD_DIM - 1)) < HEAD_DIM // 2
    pieces = []
    for start in range(0, values.shape[1], LANES):
        piece = values[:, start : start + LANES]
        partner = jnp.where(
            low,
            pltpu.roll(piece, LANES - HEAD_DIM // 2, 1),
            pltpu.roll(piece, HEAD_DIM // 2, 1),
        )
        turned = partner * sine
        pieces.append(piece * cosine + turned if direction > 0 else piece * cosine - turned)
    return jnp.concatenate(pieces, 1)


def attention_forward_kernel(
    heads, kv_heads, n1_ref, w_ref, wo_ref, cos_ref, sin_ref, bias_ref, out_ref, qkv_ref, merged_ref, lse_ref
):
    share = heads // kv_heads
    rotated = (heads + kv_heads) * HEAD_DIM
    pre = dot(n1_ref[0], w_ref[...])
    turned = rotate_pairs(pre[:, :rotated], cos_ref[0], sin_ref[0], 1)
    qkv_ref[0, :, :rotated] = turned.astype(BF16)
    qkv_ref[0, :, rotated:] = pre[:, rotated:].astype(BF16)
    bias = bias_ref[0]
    lane = lax.broadcasted_iota(jnp.int32, (pre.shape[0], LANES), 1)
    sums = jnp.zeros((pre.shape[0], LANES), F32)
    for head in range(heads):
        group = head // share
        key_at = (heads + group) * HEAD_DIM
        value_at = rotated + group * HEAD_DIM
        query = qkv_ref[0, :, head * HEAD_DIM : (head + 1) * HEAD_DIM]
        key = qkv_ref[0, :, key_at : key_at + HEAD_DIM]
        value = qkv_ref[0, :, value_at : value_at + HEAD_DIM]
        scores = dot(query, key, ((1,), (1,))) * SCORE_SCALE + bias
        highest = jnp.max(scores, -1, keepdims=True)
        exponent = jnp.exp(scores - highest)
        total = jnp.sum(exponent, -1, keepdims=True)
        weights = (exponent / total).astype(BF16)
        merged_ref[0, :, head * HEAD_DIM : (head + 1) * HEAD_DIM] = dot(weights, value).astype(BF16)
        sums = jnp.where(lane == head, highest + jnp.log(total), sums)
    lse_ref[0] = sums
    out_ref[0] = dot(merged_ref[0], wo_ref[...]).astype(BF16)


def attention_backward_kernel(
    heads,
    kv_heads,
    ga_ref,
    w_ref,
    wo_ref,
    cos_ref,
    sin_ref,
    bias_ref,
    qkv_ref,
    lse_ref,
    out_ref,
    dqkv_ref,
    turned_ref,
):
    share = heads // kv_heads
    rotated = (heads + kv_heads) * HEAD_DIM
    grad_merged = dot(ga_ref[0], wo_ref[...], ((1,), (1,))).astype(BF16)
    bias = bias_ref[0]
    for group in range(kv_heads):
        key_at = (heads + group) * HEAD_DIM
        value_at = rotated + group * HEAD_DIM
        key = qkv_ref[0, :, key_at : key_at + HEAD_DIM]
        value = qkv_ref[0, :, value_at : value_at + HEAD_DIM]
        grad_key, grad_value = None, None
        for head in range(group * share, (group + 1) * share):
            query = qkv_ref[0, :, head * HEAD_DIM : (head + 1) * HEAD_DIM]
            grad_rows = grad_merged[:, head * HEAD_DIM : (head + 1) * HEAD_DIM]
            scores = dot(query, key, ((1,), (1,))) * SCORE_SCALE + bias
            chance = jnp.exp(scores - lse_ref[0, :, head : head + 1])
            weights = chance.astype(BF16)
            grad_chance = dot(grad_rows, value, ((1,), (1,)))
            delta = jnp.sum(chance * grad_chance, -1, keepdims=True)
            grad_raw = (chance * (grad_chance - delta) * SCORE_SCALE).astype(BF16)
            turned_ref[:, head * HEAD_DIM : (head + 1) * HEAD_DIM] = dot(grad_raw, key)
            key_part = dot(grad_raw, query, ((0,), (0,)))
            value_part = dot(weights, grad_rows, ((0,), (0,)))
            grad_key = key_part if grad_key is None else grad_key + key_part
            grad_value = value_part if grad_value is None else grad_value + value_part
        turned_ref[:, key_at : key_at + HEAD_DIM] = grad_key
        dqkv_ref[0, :, value_at : value_at + HEAD_DIM] = grad_value.astype(BF16)
    back = rotate_pairs(turned_ref[...], cos_ref[0], sin_ref[0], -1)
    dqkv_ref[0, :, :rotated] = back.astype(BF16)
    out_ref[0] = dot(dqkv_ref[0], w_ref[...], ((1,), (1,))).astype(BF16)


def per_micro(shape):
    return pl.BlockSpec((1,) + tuple(shape[1:]), lambda m: (m,) + (0,) * (len(shape) - 1))


def whole(shape):
    return pl.BlockSpec(tuple(shape), lambda m: (0,) * len(shape))


def attention_forward(n1, w, wo, cosine, sine, bias, heads, kv_heads):
    micros, rows, width = n1.shape
    outs = [
        jax.ShapeDtypeStruct((micros, rows, width), BF16),
        jax.ShapeDtypeStruct((micros, rows, w.shape[1]), BF16),
        jax.ShapeDtypeStruct((micros, rows, heads * HEAD_DIM), BF16),
        jax.ShapeDtypeStruct((micros, rows, LANES), F32),
    ]
    return pl.pallas_call(
        functools.partial(attention_forward_kernel, heads, kv_heads),
        grid=(micros,),
        in_specs=[
            per_micro(n1.shape),
            whole(w.shape),
            whole(wo.shape),
            per_micro(cosine.shape),
            per_micro(sine.shape),
            per_micro(bias.shape),
        ],
        out_specs=[per_micro(o.shape) for o in outs],
        out_shape=outs,
        name="attention_forward",
    )(n1, w, wo, cosine, sine, bias)


def attention_backward(ga, w, wo, cosine, sine, bias, qkv, lse, heads, kv_heads):
    micros, rows, width = ga.shape
    outs = [
        jax.ShapeDtypeStruct((micros, rows, width), BF16),
        jax.ShapeDtypeStruct((micros, rows, w.shape[1]), BF16),
    ]
    return pl.pallas_call(
        functools.partial(attention_backward_kernel, heads, kv_heads),
        grid=(micros,),
        in_specs=[
            per_micro(ga.shape),
            whole(w.shape),
            whole(wo.shape),
            per_micro(cosine.shape),
            per_micro(sine.shape),
            per_micro(bias.shape),
            per_micro(qkv.shape),
            per_micro(lse.shape),
        ],
        out_specs=[per_micro(o.shape) for o in outs],
        out_shape=outs,
        scratch_shapes=[pltpu.VMEM((rows, (heads + kv_heads) * HEAD_DIM), F32)],
        name="attention_backward",
    )(ga, w, wo, cosine, sine, bias, qkv, lse)


def experts_kernel(
    experts_all,
    ids_ref,
    x_ref,
    gm_ref,
    mask_ref,
    wr_ref,
    wgu_ref,
    wd_ref,
    mixed_ref,
    dx_ref,
    gate_ref,
    gg_ref,
    act_ref,
    dgu_ref,
    mixed_acc,
    dx_acc,
):
    step = pl.program_id(1)
    rows = x_ref.shape[0]
    per_step, hidden = wd_ref.shape[0], wd_ref.shape[1]
    lane = lax.broadcasted_iota(jnp.int32, (rows, LANES), 1)

    @pl.when(step == 0)
    def _():
        named = mask_ref[...].astype(F32) > 0.5
        logits = jnp.where(named, dot(x_ref[...], wr_ref[...]), NEGATIVE)
        highest = jnp.max(logits, -1, keepdims=True)
        exponent = jnp.where(named, jnp.exp(logits - highest), 0.0)
        gate_ref[...] = exponent / jnp.sum(exponent, -1, keepdims=True)
        gg_ref[...] = jnp.zeros_like(gg_ref)
        mixed_acc[...] = jnp.zeros_like(mixed_acc)
        dx_acc[...] = jnp.zeros_like(dx_acc)

    x = x_ref[...]
    down = wd_ref[...].reshape(per_step * hidden, wd_ref.shape[2])
    grad_act = dot(gm_ref[...], down, ((1,), (1,)))
    gates = gate_ref[...]
    for i in range(per_step):
        mine = lane == ids_ref[step * per_step + i]
        gate = jnp.sum(jnp.where(mine, gates, 0.0), -1, keepdims=True)
        pre = dot(x, wgu_ref[i])
        gate_pre, up_pre = pre[:, :hidden], pre[:, hidden:]
        sig = jax.nn.sigmoid(gate_pre)
        silu = gate_pre * sig
        activated = (silu * up_pre).astype(BF16).astype(F32)
        grad_one = grad_act[:, i * hidden : (i + 1) * hidden]
        picked = jnp.sum(activated * grad_one, -1, keepdims=True)
        gg_ref[...] += jnp.where(mine, picked, 0.0)
        act_ref[:, i * hidden : (i + 1) * hidden] = (activated * gate).astype(BF16)
        grad_one = grad_one * gate
        grad_gate_pre = (grad_one * up_pre * sig * (1.0 + gate_pre * (1.0 - sig))).astype(BF16)
        grad_up_pre = (grad_one * silu).astype(BF16)
        base = 2 * hidden * i
        dgu_ref[:, base : base + hidden] = grad_gate_pre
        dgu_ref[:, base + hidden : base + 2 * hidden] = grad_up_pre
        dx_acc[...] += dot(dgu_ref[:, base : base + 2 * hidden], wgu_ref[i], ((1,), (1,)))
    mixed_acc[...] += dot(act_ref[...], down)

    @pl.when(step == pl.num_programs(1) - 1)
    def _():
        mixed_ref[...] = mixed_acc[...].astype(BF16)
        dx_ref[...] = dx_acc[...].astype(BF16)


def run_experts(ids, x, gm_mask, wr, wgu, wd, experts_all):
    rows, width = x.shape
    local, hidden = wd.shape[0], wd.shape[1]
    per_step = 2 if local % 2 == 0 else 1
    block = min(rows, 1024)
    outs = [
        jax.ShapeDtypeStruct((rows, width), BF16),
        jax.ShapeDtypeStruct((rows, width), BF16),
        jax.ShapeDtypeStruct((rows, LANES), F32),
        jax.ShapeDtypeStruct((rows, LANES), F32),
        jax.ShapeDtypeStruct((rows, local * hidden), BF16),
        jax.ShapeDtypeStruct((rows, 2 * local * hidden), BF16),
    ]
    once = pl.Buffered(1)
    return pl.pallas_call(
        functools.partial(experts_kernel, experts_all),
        grid_spec=pltpu.PrefetchScalarGridSpec(
            num_scalar_prefetch=1,
            grid=(rows // block, local // per_step),
            in_specs=[
                pl.BlockSpec((block, width), lambda r, s, ids: (r, 0)),
                pl.BlockSpec((block, width), lambda r, s, ids: (r, 0)),
                pl.BlockSpec((block, LANES), lambda r, s, ids: (r, width // LANES)),
                pl.BlockSpec((width, LANES), lambda r, s, ids: (0, 0), pipeline_mode=once),
                pl.BlockSpec((per_step, width, 2 * hidden), lambda r, s, ids: (s, 0, 0)),
                pl.BlockSpec((per_step, hidden, width), lambda r, s, ids: (s, 0, 0)),
            ],
            out_specs=[
                pl.BlockSpec((block, width), lambda r, s, ids: (r, 0)),
                pl.BlockSpec((block, width), lambda r, s, ids: (r, 0)),
                pl.BlockSpec((block, LANES), lambda r, s, ids: (r, 0)),
                pl.BlockSpec((block, LANES), lambda r, s, ids: (r, 0)),
                pl.BlockSpec((block, per_step * hidden), lambda r, s, ids: (r, s)),
                pl.BlockSpec((block, 2 * per_step * hidden), lambda r, s, ids: (r, s)),
            ],
            scratch_shapes=[pltpu.VMEM((block, width), F32), pltpu.VMEM((block, width), F32)],
        ),
        out_shape=outs,
        compiler_params=pltpu.CompilerParams(vmem_limit_bytes=60 << 20),
        name="experts",
    )(ids, x, gm_mask, gm_mask, wr, wgu, wd)


def per_device(
    tokens,
    cotangent,
    attn_gain,
    mlp_gain,
    w_query,
    w_key,
    w_value,
    w_out,
    w_router,
    w_gate,
    w_up,
    w_down,
    shuffle,
    routes,
    lengths,
):
    micros, rows, width = tokens.shape
    dp_count, members = lax.axis_size("dp"), lax.axis_size("expert")
    devices = dp_count * members
    rings = Rings(dp_count, members)
    zn, yn, xn, cn = rings.z, rings.y, rings.x, rings.core
    group_rows = rows * members
    experts_all = w_router.shape[1]
    own_experts, model_part, hidden_all = w_gate.shape
    hidden_part = hidden_all // zn
    heads, kv_heads = HEADS // members, KV_HEADS // members
    weight_rows = w_query.shape[0]
    home_rows = micros * rows

    small = jnp.concatenate([w_router.T, attn_gain[None], mlp_gain[None]], 0)
    small = lax.all_to_all(jnp.broadcast_to(small[None], (devices,) + small.shape), ALL, 0, 0)
    small = small.transpose(1, 0, 2).reshape(experts_all + 2, width)
    gain_first = small[experts_all].astype(F32)
    gain_second = small[experts_all + 1].astype(F32)
    router_rows = jnp.pad(small[:experts_all], ((0, LANES - experts_all), (0, 0)))
    router_cols = router_rows.T

    def by_member(w):
        return w.reshape(weight_rows, members, w.shape[1] // members)

    mine = jnp.concatenate([by_member(w_query), by_member(w_key), by_member(w_value)], 2)
    mine = lax.all_to_all(mine.transpose(1, 0, 2), "expert", 0, 0)
    qkv_cols = mine.shape[2]
    mine = mine.reshape(members * weight_rows, qkv_cols)
    to_heads = [(s, (s % dp_count) * members + s // dp_count) for s in range(devices)]
    to_home = [(t, s) for s, t in to_heads]
    out_mine = lax.ppermute(w_out, ALL, to_heads)
    merged_cols = width // members
    pack = out_mine.reshape(weight_rows, members, merged_cols).transpose(1, 0, 2)
    pack = jnp.concatenate([mine, pack.reshape(members * weight_rows, merged_cols)], 1)
    packs = rings.gather_two(pack, "z", "y")
    packs = [in_order(column, rings.at["z"], zn) for column in packs]
    packs = [in_order([packs[s][z] for s in range(yn)], rings.at["y"], yn) for z in range(zn)]
    packs = jnp.stack([packs[z][y] for z in range(zn) for y in range(yn)])
    w_qkv = packs[:, :, :qkv_cols].reshape(width, qkv_cols)
    w_merge = packs[:, :, qkv_cols:].reshape(dp_count, members, weight_rows, merged_cols)
    w_merge = w_merge.transpose(0, 2, 1, 3).reshape(dp_count * weight_rows, width)

    dealt = lax.all_to_all(
        routes.reshape(micros, dp_count, rows // dp_count, routes.shape[2]), "dp", 1, 1
    ).reshape(micros, rows, routes.shape[2])
    lane_ids = jnp.arange(LANES, dtype=jnp.int32)
    hot = jnp.sum((dealt[:, :, :, None] == lane_ids).astype(F32), 2).astype(BF16)
    place = (shuffle[:, 0, :, None] == jnp.arange(rows, dtype=jnp.int32)).astype(BF16)
    named = jnp.einsum("mir,mix->mrx", place, hot, preferred_element_type=F32).astype(BF16)

    grad_result = cotangent.astype(F32)
    grad_moe = (RESIDUAL_SCALE * grad_result).astype(BF16)
    beside = jnp.concatenate([grad_moe, named], 2).reshape(home_rows, width + LANES)
    beside = rings.gather_two(beside, "z", "x")
    gm_mask = jnp.concatenate([slot for column in beside for slot in column], 0)

    def to_z(w):
        w = w.reshape(own_experts, model_part, zn, hidden_part)
        return w.transpose(2, 0, 1, 3)

    gate_up = jnp.concatenate([to_z(w_gate), to_z(w_up)], 3)
    gate_up = lax.all_to_all(gate_up, "dp", 0, 0, axis_index_groups=rings.z_groups)
    gate_up = in_order(rings.gather(gate_up, "y"), rings.at["y"], yn)
    gate_up = jnp.stack(gate_up, 1).transpose(2, 0, 1, 3, 4)
    gate_up = gate_up.reshape(own_experts, width, 2 * hidden_part)
    down = in_order(rings.gather(w_down, "y"), rings.at["y"], yn)
    down = jnp.concatenate(down, 1)
    w_gu = jnp.concatenate(rings.gather(gate_up, "c"), 0)
    w_dn = jnp.concatenate(rings.gather(down, "c"), 0)
    ids = jnp.concatenate(
        [
            (rings.at["x"] * cn + rings.origin("c", s)) * own_experts
            + jnp.arange(own_experts, dtype=jnp.int32)
            for s in range(cn)
        ]
    )

    group_iota = jnp.arange(group_rows, dtype=jnp.int32)
    row_at = jnp.concatenate(
        [
            (rings.origin("x", s) * cn + rings.origin("c", t)) * rows
            + jnp.arange(rows, dtype=jnp.int32)
            for s in range(xn)
            for t in range(cn)
        ]
    )
    half = HEAD_DIM // 2
    lane = jnp.arange(LANES, dtype=jnp.int32)
    inverse = ROPE_BASE ** (-((lane % half).astype(F32) * 2.0) / HEAD_DIM)
    sign = jnp.where(lane % HEAD_DIM < half, -1.0, 1.0)
    cosine, sine, bias = [], [], []
    for m in range(micros):
        doc_lengths = lengths[m, 0]
        doc_ends = jnp.cumsum(doc_lengths)
        doc_starts = doc_ends - doc_lengths
        segment = jnp.sum((row_at[:, None] >= doc_ends[None, :]).astype(jnp.int32), 1)
        member_of = segment[:, None] == jnp.arange(doc_lengths.shape[0], dtype=jnp.int32)[None, :]
        position = row_at - jnp.sum(jnp.where(member_of, doc_starts[None, :], 0), 1)
        angles = position.astype(F32)[:, None] * inverse[None, :]
        cosine.append(jnp.cos(angles))
        sine.append(jnp.sin(angles) * sign)
        allowed = (segment[:, None] == segment[None, :]) & (row_at[None, :] <= row_at[:, None])
        bias.append(jnp.where(allowed, 0.0, NEGATIVE))
    cosine, sine, bias = jnp.stack(cosine), jnp.stack(sine), jnp.stack(bias)

    def over_members(value):
        both = jnp.concatenate(rings.gather(value, "c"), 1)
        return jnp.concatenate(rings.gather(both, "x"), 1)

    def sum_members(value):
        parts = value.reshape(micros, xn, cn, rows, width)
        parts = rings.reduce([parts[:, :, t] for t in range(cn)], "c")
        return rings.reduce([parts[:, s] for s in range(xn)], "x")

    inputs = tokens.astype(F32)
    inv_first = lax.rsqrt(jnp.mean(inputs * inputs, -1, keepdims=True) + EPSILON)
    unit_first = inputs * inv_first
    normed_first = over_members((unit_first * gain_first).astype(BF16))
    attn_part, qkv, merged, lse = attention_forward(
        normed_first, w_qkv, w_merge, cosine, sine, bias, heads, kv_heads
    )
    hidden = inputs + RESIDUAL_SCALE * sum_members(attn_part)
    inv_second = lax.rsqrt(jnp.mean(hidden * hidden, -1, keepdims=True) + EPSILON)
    unit_second = hidden * inv_second
    normed_second = (unit_second * gain_second).astype(BF16).reshape(home_rows, width)

    group_x = rings.gather_two(normed_second, "z", "x")
    group_x = jnp.concatenate([slot for column in group_x for slot in column], 0)
    mixed, dx, gates, grad_gates, act, dgu = run_experts(
        ids, group_x, gm_mask, router_cols, w_gu, w_dn, experts_all
    )

    def to_owner(value, wire):
        parts = value.reshape(xn, zn, home_rows, value.shape[1])
        return rings.reduce_two([[parts[s, t] for t in range(zn)] for s in range(xn)], "z", "x", wire)

    grad_gates = to_owner(grad_gates, F32)
    grad_dealt = to_owner(dx, BF16)
    own_gates = gates[:home_rows]
    grad_picked = own_gates * (grad_gates - jnp.sum(own_gates * grad_gates, -1, keepdims=True))
    grad_logits = grad_picked.astype(BF16)
    router_grad = dot(grad_logits, normed_second, ((0,), (0,)))[:experts_all]
    grad_dealt = (grad_dealt + dot(grad_logits, router_rows)).astype(BF16)
    grad_normed_second = grad_dealt.astype(F32).reshape(micros, rows, width)
    scaled_second = grad_normed_second * gain_second
    grad_hidden = grad_result + inv_second * (
        scaled_second - unit_second * jnp.mean(scaled_second * unit_second, -1, keepdims=True)
    )
    mlp_gain_grad = jnp.sum(grad_normed_second * unit_second, (0, 1))
    grad_attn = over_members((RESIDUAL_SCALE * grad_hidden).astype(BF16))

    moe_rows = to_owner(mixed, BF16).astype(BF16).reshape(micros, rows, width)
    output = (hidden + RESIDUAL_SCALE * moe_rows.astype(F32)).astype(BF16)

    first_part, dqkv = attention_backward(
        grad_attn, w_qkv, w_merge, cosine, sine, bias, qkv, lse, heads, kv_heads
    )
    grad_normed_first = sum_members(first_part)
    scaled_first = grad_normed_first * gain_first
    grad_tokens = grad_hidden + inv_first * (
        scaled_first - unit_first * jnp.mean(scaled_first * unit_first, -1, keepdims=True)
    )
    attn_gain_grad = jnp.sum(grad_normed_first * unit_first, (0, 1))

    small = jnp.concatenate([router_grad, mlp_gain_grad[None]], 0)
    small = small.reshape(experts_all + 1, devices, weight_rows).transpose(1, 0, 2)
    small = jnp.sum(lax.all_to_all(small, ALL, 0, 0), 0)
    grad_w_router, grad_mlp_gain = small[:experts_all].T, small[experts_all]
    grad_attn_gain = jnp.sum(
        lax.all_to_all(attn_gain_grad.reshape(devices, 1, weight_rows), ALL, 0, 0), (0, 1)
    )

    model_parts = zn * yn
    grad_gu = dot(group_x, dgu, ((0,), (0,))).astype(BF16)
    grad_gu = grad_gu.reshape(width, cn, own_experts * 2 * hidden_part)
    grad_gu = rings.reduce([grad_gu[:, s] for s in range(cn)], "c").astype(BF16)
    grad_gu = grad_gu.reshape(zn, yn, model_part, own_experts * 2 * hidden_part)
    grad_gu = rings.reduce(
        [lax.dynamic_index_in_dim(grad_gu, rings.origin("y", s), 1, False) for s in range(yn)], "y"
    ).astype(BF16)
    grad_gu = lax.all_to_all(grad_gu, "dp", 0, 0, axis_index_groups=rings.z_groups)
    grad_gu = grad_gu.reshape(zn, model_part, own_experts, 2, hidden_part).astype(F32)
    grad_gu = grad_gu.transpose(3, 2, 1, 0, 4).reshape(2, own_experts, model_part, hidden_all)
    grad_dn = dot(act, gm_mask[:, :width], ((0,), (0,))).astype(BF16)
    grad_dn = grad_dn.reshape(cn, own_experts, hidden_part, width)
    grad_dn = rings.reduce([grad_dn[s] for s in range(cn)], "c").astype(BF16)
    grad_dn = grad_dn.reshape(own_experts, yn, hidden_part // yn, width)
    grad_dn = rings.reduce(
        [lax.dynamic_index_in_dim(grad_dn, rings.origin("y", s), 1, False) for s in range(yn)], "y"
    )

    flat = micros * group_rows
    grad_qkv = dot(
        normed_first.reshape(flat, width), dqkv.reshape(flat, qkv_cols), ((0,), (0,))
    ).astype(BF16)
    grad_out = dot(
        merged.reshape(flat, heads * HEAD_DIM), grad_attn.reshape(flat, width), ((0,), (0,))
    ).astype(BF16)
    grad_out = grad_out.reshape(dp_count, weight_rows, members, merged_cols).transpose(0, 2, 1, 3)
    both = jnp.concatenate(
        [
            grad_qkv.reshape(dp_count, members * weight_rows, qkv_cols),
            grad_out.reshape(dp_count, members * weight_rows, merged_cols),
        ],
        2,
    )
    parts = [
        [
            lax.dynamic_index_in_dim(both, rings.origin("z", t) * yn + rings.origin("y", s), 0, False)
            for t in range(zn)
        ]
        for s in range(yn)
    ]
    both = rings.reduce_two(parts, "z", "y")
    grad_out = both[:, qkv_cols:].reshape(members, weight_rows, merged_cols).transpose(1, 0, 2)
    grad_out = lax.ppermute(grad_out.reshape(weight_rows, width), ALL, to_home)
    home = lax.all_to_all(both[:, :qkv_cols].reshape(members, weight_rows, qkv_cols), "expert", 0, 0)
    home = home.transpose(1, 0, 2)
    query_cols, key_cols = heads * HEAD_DIM, kv_heads * HEAD_DIM
    grad_query = home[:, :, :query_cols].reshape(weight_rows, -1)
    grad_key = home[:, :, query_cols : query_cols + key_cols].reshape(weight_rows, -1)
    grad_value = home[:, :, query_cols + key_cols :].reshape(weight_rows, -1)

    return (
        output,
        grad_tokens,
        grad_attn_gain,
        grad_mlp_gain,
        grad_query,
        grad_key,
        grad_value,
        grad_out,
        grad_w_router,
        grad_gu[0],
        grad_gu[1],
        grad_dn,
    )


def solution(mesh):
    rows = P(None, ALL, None)
    placed = (rows, rows, P(ALL), P(ALL)) + (P(ALL, None),) * 5
    placed += (P("expert", "dp", None),) * 3 + (rows, rows, P(None, "dp", None))
    results = (rows, rows, P(ALL), P(ALL)) + (P(ALL, None),) * 5
    results += (P("expert", "dp", None),) * 3
    return jax.shard_map(per_device, mesh=mesh, in_specs=placed, out_specs=results, check_vma=False)
```

time: 2590 us -> 679 us (0.26)
  the two profiles are of different devices: /device:TPU:3 before, /device:TPU:4 now
where the time goes in v1:
time: 679 us; the launch traced here: 670 us
  waiting for transfers between devices  242 us (36%)
  starting transfers between devices  134 us (20%)
  local copies, waits for them, and re-layouts  122 us (18%)
  other arithmetic  79.6 us (12%)
  Pallas kernels  66.1 us (10%)
  matrix products  24.8 us (4%)
    ppermute x65, waiting for transfers between devices, step(): return lax.ppermute(value, axis, pairs)  204 us
    ppermute x65, starting transfers between devices, step(): return lax.ppermute(value, axis, pairs)  89.6 us
    pallas_call x1, Pallas kernels, run_experts(): pl.pallas_call(functools.partial(experts_kernel, experts_all), grid_spec=...  45.1 us
    unnamed x122, local copies, waits for them, and re-layouts  29.5 us
    ppermute x1, waiting for transfers between devices, per_device(): grad_out = lax.ppermute(grad_out.reshape(weight_rows, width), ALL, to_home)  26 us
    dot_general x6, matrix products, dot(): return lax.dot_general(a, b, (dims, ((), ())), preferred_element_type=F32)  24.7 us
    reshape x1, local copies, waits for them, and re-layouts, per_device(): grad_gu = grad_gu.reshape(width, cn, own_experts * 2 * hidden_part)  17 us
    slice x1, local copies, waits for them, and re-layouts, per_device(): grad_gu = rings.reduce([grad_gu[:, s] for s in range(cn)], 'c').astype(BF16)  16.7 us
  transfers between devices with their start and end apart: 75, of which 26 were waited for; matrix products, arithmetic and copies ran while one was open for 29% of the time, Pallas kernels for 3%

profile of v1, /device:TPU:4, one launch (start us, length us, event | category | flops | bytes accessed | tf_op | source)
XLA Modules:
  0.0 670.2 jit_solution(13724086501420603342)
XLA Ops:
  31.0 6.8 %all-to-all-start = ((bf16[32,2,528]{2,1,0:T(2,128)(2,1)}), bf16[32,2,528]{2,1,0:T(2,128)(2,1)S(1)}, u32[]{:S(2)}, u32[]{:S(2)}) async-start(bf16[32,2,528]{2,1,0:T(2,128)(2,1)} %reshape.998), calls=%async_computation | async-start | bytes 163840 | tf_op jit(solution)/shard_map/all_to_all | solution.py:393
  64.4 39.4 %collective-permute-done.3 = bf16[192,1024]{1,0:T(8,128)(2,1)} collective-permute-done((bf16[192,1024]{1,0:T(8,128)(2,1)S(1)}, bf16[192,1024]{1,0:T(8,128)(2,1)}, u32[]{:S(2)}, u32[]{:S(2)}) %collective-permute-start.3) | collective-permute-done | bytes 393248 | tf_op jit(solution)/shard_map/ppermute | solution.py:62
  103.8 8.1 %collective-permute-start.4 = (bf16[192,1024]{1,0:T(8,128)(2,1)}, bf16[192,1024]{1,0:T(8,128)(2,1)}, u32[]{:S(2)}, u32[]{:S(2)}) collective-permute-start(bf16[192,1024]{1,0:T(8,128)(2,1)} %collective-permute-done.3), channel_id=1, source_target_pairs={{0,8},{4,12},{8,16},{12,20},{16,24},{20,28},{24,0},{28,4},{1,9},{5... | collective-permute-start | bytes 1179656 | tf_op jit(solution)/shard_map/ppermute | solution.py:62
  114.9 6.2 collective-permute-start.20
  145.0 6.3 collective-permute-done.8
  151.3 8.2 %collective-permute-start.21 = (bf16[128,1664]{1,0:T(8,128)(2,1)}, bf16[128,1664]{1,0:T(8,128)(2,1)}, u32[]{:S(2)}, u32[]{:S(2)}) collective-permute-start(bf16[128,1664]{1,0:T(8,128)(2,1)} %collective-permute-done.20), channel_id=1, source_target_pairs={{0,8},{4,12},{8,16},{12,20},{16,24},{20,28},{24,0},{28,4},{1,9},{5... | collective-permute-start | bytes 1277960 | tf_op jit(solution)/shard_map/ppermute | solution.py:62
  165.2 9.4 %attention_forward.1 = (bf16[2,256,1536]{2,1,0:T(8,128)(2,1)}, bf16[2,256,640]{2,1,0:T(8,128)(2,1)}, bf16[2,256,384]{2,1,0:T(8,128)(2,1)}, f32[2,256,128]{2,1,0:T(8,128)}) custom-call(bf16[2,256,1536]{2,1,0:T(8,128)(2,1)} %pad_maximum_fusion.4.n1_ref, bf16[1536,640]{1,0:T(8,128)(2,1)} %bitcast.316, bf16[384,1536]{1,0:T(8,128)(2,1)} %bitcast.323, ...), custom_call_target="tpu_custom_call" | custom-call | tf_op jit(solution)/shard_map/attention_forward/pallas_call | solution.py:211
  187.5 35.8 %collective-permute-done.26 = bf16[4,5,192,256]{3,2,1,0:T(8,128)(2,1)S(1)} collective-permute-done((bf16[4,5,192,256]{3,2,1,0:T(8,128)(2,1)}, bf16[4,5,192,256]{3,2,1,0:T(8,128)(2,1)S(1)}, u32[]{:S(2)}, u32[]{:S(2)}) %collective-permute-start.26) | collective-permute-done | bytes 1966112 | tf_op jit(solution)/shard_map/ppermute | solution.py:62
  240.7 5.7 collective-permute-done.12
  260.6 7.5 %collective-permute-done.14 = bf16[128,1536]{1,0:T(8,128)(2,1)S(1)} collective-permute-done((bf16[128,1536]{1,0:T(8,128)(2,1)S(1)}, bf16[128,1536]{1,0:T(8,128)(2,1)S(1)}, u32[]{:S(2)}, u32[]{:S(2)}) %collective-permute-start.14) | collective-permute-done | bytes 393248 | tf_op jit(solution)/shard_map/ppermute | solution.py:62
  271.5 7.1 %collective-permute-done.17 = bf16[128,1536]{1,0:T(8,128)(2,1)S(1)} collective-permute-done((bf16[128,1536]{1,0:T(8,128)(2,1)S(1)}, bf16[128,1536]{1,0:T(8,128)(2,1)S(1)}, u32[]{:S(2)}, u32[]{:S(2)}) %collective-permute-start.17) | collective-permute-done | bytes 393248 | tf_op jit(solution)/shard_map/ppermute | solution.py:62
  284.3 7.2 %pad_maximum_fusion.wgu_ref = bf16[10,1536,256]{2,1,0:T(8,128)(2,1)} fusion(bf16[5,1536,256]{2,1,0:T(8,128)(2,1)} %collective-permute-done.27, bf16[5,1536,256]{2,1,0:T(8,128)(2,1)} %bitcast.320), kind=kLoop, calls=%fused_computation.1 | loop fusion | flops 3932160 | bytes 15728640 | tf_op jit(solution)/shard_map/concatenate | solution.py:446
  291.4 45.1 %experts.1 = (bf16[1024,1536]{1,0:T(8,128)(2,1)}, bf16[1024,1536]{1,0:T(8,128)(2,1)}, f32[1024,128]{1,0:T(8,128)}, f32[1024,128]{1,0:T(8,128)}, bf16[1024,1280]{1,0:T(8,128)(2,1)}, /*index=5*/bf16[1024,2560]{1,0:T(8,128)(2,1)}) custom-call(s32[10]{0:T(128)} %pad_add_fusion.1.ids_ref, bf16[1024,1536]{1,0:T(8,128)(2,1)} %constant_dynamic-update-slice_fusion.x_ref, ...), custom_call_target="tpu_custom_call" | custom-call | tf_op jit(solution)/shard_map/experts/pallas_call | solution.py:333
  341.7 13.5 %convolution_convert_fusion = bf16[1536,2560]{1,0:T(8,128)(2,1)} fusion(bf16[1024,1536]{1,0:T(8,128)(2,1)} %constant_dynamic-update-slice_fusion.x_ref, bf16[1024,2560]{1,0:T(8,128)(2,1)} %get-tuple-element.34), kind=kOutput, calls=%fused_computation | convolution fusion | flops 8056995840 | bytes 16252928 | tf_op jit(solution)/shard_map/dot_general | solution.py:27
  355.2 17.0 %reshape.958 = bf16[1536,2,1280]{2,1,0:T(2,128)(2,1)} reshape(bf16[1536,2560]{1,0:T(8,128)(2,1)} %convolution_convert_fusion) | data formatting | bytes 15728640 | tf_op jit(solution)/shard_map/reshape | solution.py:553
  378.6 16.7 %fusion.111 = (bf16[1536,1,1280]{2,1,0:T(2,128)(2,1)}, bf16[1536,1,1280]{2,1,0:T(2,128)(2,1)S(1)}) fusion(bf16[1536,2,1280]{2,1,0:T(2,128)(2,1)} %reshape.958), kind=kLoop, calls=%fused_computation.303 | loop fusion | bytes 15728640 | tf_op jit(solution)/shard_map/slice | solution.py:554
  445.4 9.4 %collective-permute-done.52 = bf16[2,128,1536]{2,1,0:T(8,128)(2,1)} collective-permute-done((bf16[2,128,1536]{2,1,0:T(8,128)(2,1)S(1)}, bf16[2,128,1536]{2,1,0:T(8,128)(2,1)}, u32[]{:S(2)}, u32[]{:S(2)}) %collective-permute-start.52) | collective-permute-done | bytes 786464 | tf_op jit(solution)/shard_map/ppermute | solution.py:62
  462.4 11.6 %attention_backward.1 = (bf16[2,256,1536]{2,1,0:T(8,128)(2,1)}, bf16[2,256,640]{2,1,0:T(8,128)(2,1)}) custom-call(bf16[2,256,1536]{2,1,0:T(8,128)(2,1)} %pad_maximum_fusion.7.ga_ref, bf16[1536,640]{1,0:T(8,128)(2,1)} %bitcast.317, bf16[384,1536]{1,0:T(8,128)(2,1)} %bitcast.324, f32[2,256,128]{2,1,0:T(8,128)} %pad_maximum_fusion.13.cos_ref, ...), custom_call_target="tpu_custom_call" | custom-call | tf_op jit(solution)/shard_map/attention_backward/pallas_call | solution.py:234
  492.5 9.0 %collective-permute-done.57 = bf16[192,1024]{1,0:T(8,128)(2,1)S(1)} collective-permute-done((bf16[192,1024]{1,0:T(8,128)(2,1)}, bf16[192,1024]{1,0:T(8,128)(2,1)S(1)}, u32[]{:S(2)}, u32[]{:S(2)}) %collective-permute-start.57) | collective-permute-done | bytes 393248 | tf_op jit(solution)/shard_map/ppermute | solution.py:62
  529.8 5.9 all-to-all-start.4
  535.7 29.6 %collective-permute-done.55 = bf16[192,1024]{1,0:T(8,128)(2,1)} collective-permute-done((bf16[192,1024]{1,0:T(8,128)(2,1)}, bf16[192,1024]{1,0:T(8,128)(2,1)}, u32[]{:S(2)}, u32[]{:S(2)}) %collective-permute-start.55) | collective-permute-done | bytes 393248 | tf_op jit(solution)/shard_map/ppermute | solution.py:62
  594.4 15.3 %collective-permute-done.66 = bf16[5,64,1536]{2,1,0:T(8,128)(2,1)} collective-permute-done((bf16[5,64,1536]{2,1,0:T(8,128)(2,1)}, bf16[5,64,1536]{2,1,0:T(8,128)(2,1)}, u32[]{:S(2)}, u32[]{:S(2)}) %collective-permute-start.66) | collective-permute-done | bytes 983072 | tf_op jit(solution)/shard_map/ppermute | solution.py:62
  617.6 26.0 %collective-permute-done.62 = f32[48,1536]{1,0:T(8,128)S(1)} collective-permute-done((f32[48,1536]{1,0:T(8,128)}, f32[48,1536]{1,0:T(8,128)S(1)}, u32[]{:S(2)}, u32[]{:S(2)}) %collective-permute-start.62) | collective-permute-done | bytes 294944 | tf_op jit(solution)/shard_map/ppermute | solution.py:594
  652.7 8.1 %fusion.113 = (f32[1,5,192,4,128]{4,0,1,2,3:T(1,128)}, f32[1,5,192,4,128]{4,0,1,2,3:T(1,128)S(1)}) fusion(f32[2,5,192,4,128]{4,0,1,2,3:T(2,128)} %bitcast.318), kind=kLoop, calls=%fused_computation.305 | loop fusion | bytes 7864320 | tf_op jit(solution)/shard_map/slice | solution.py:613
  (397 shorter events, 313.1 us)
Async XLA Ops:
  0.7 48.8 %collective-permute-start.2 = (bf16[48,1536]{1,0:T(8,128)(2,1)}, bf16[48,1536]{1,0:T(8,128)(2,1)}, u32[]{:S(2)}, u32[]{:S(2)}) collective-permute-start(bf16[48,1536]{1,0:T(8,128)(2,1)} %param.22), channel_id=1, source_target_pairs={{0,0},{1,4},{2,8},{3,12},{4,16},{5,20},{6,24},{7,28},{8,1},{9,5},{... | collective-permute-start | bytes 442376 | tf_op jit(solution)/shard_map/ppermute | solution.py:409
  5.3 172.6 %collective-permute-start.28 = (bf16[5,64,1536]{2,1,0:T(8,128)(2,1)}, bf16[5,64,1536]{2,1,0:T(8,128)(2,1)}, u32[]{:S(2)}, u32[]{:S(2)}) collective-permute-start(bf16[5,64,1536]{2,1,0:T(8,128)(2,1)} %param.26), channel_id=1, source_target_pairs={{0,4},{4,0},{8,12},{12,8},{16,20},{20,16},{24,28},{28,24},{1,5},{5... | collective-permute-start | bytes 2949128 | tf_op jit(solution)/shard_map/ppermute | solution.py:62
  53.5 124.4 %all-to-all-start.3 = ((bf16[4,5,192,256]{3,2,1,0:T(8,128)(2,1)}), bf16[4,5,192,256]{3,2,1,0:T(8,128)(2,1)}, u32[]{:S(2)}, u32[]{:S(2)}) async-start(bf16[4,5,192,256]{3,2,1,0:T(8,128)(2,1)} %copy.170), calls=%async_computation.3 | async-start | bytes 3932160 | tf_op jit(solution)/shard_map/all_to_all | solution.py:440
  58.8 45.0 %collective-permute-start.3 = (bf16[192,1024]{1,0:T(8,128)(2,1)S(1)}, bf16[192,1024]{1,0:T(8,128)(2,1)}, u32[]{:S(2)}, u32[]{:S(2)}) collective-permute-start(bf16[192,1024]{1,0:T(8,128)(2,1)S(1)} %get-tuple-element.89), channel_id=1, source_target_pairs={{0,8},{4,12},{8,16},{12,20},{16,24},{20,28},{24,0},{28,4},{1,9},{5... | collective-permute-start | bytes 1179656 | tf_op jit(solution)/shard_map/ppermute | solution.py:62
  61.6 53.3 %collective-permute-start.19 = (bf16[128,1664]{1,0:T(8,128)(2,1)}, bf16[128,1664]{1,0:T(8,128)(2,1)}, u32[]{:S(2)}, u32[]{:S(2)}) collective-permute-start(bf16[128,1664]{1,0:T(8,128)(2,1)} %bitcast.29), channel_id=1, source_target_pairs={{0,8},{4,12},{8,16},{12,20},{16,24},{20,28},{24,0},{28,4},{1,9},{5... | collective-permute-start | bytes 1277960 | tf_op jit(solution)/shard_map/ppermute | solution.py:62
  64.0 69.1 %collective-permute-start.1 = (bf16[2,128,1536]{2,1,0:T(8,128)(2,1)}, bf16[2,128,1536]{2,1,0:T(8,128)(2,1)}, u32[]{:S(2)}, u32[]{:S(2)}) collective-permute-start(bf16[2,128,1536]{2,1,0:T(8,128)(2,1)} %pad_maximum_fusion.8), channel_id=1, source_target_pairs={{0,2},{1,3},{2,0},{3,1},{4,6},{5,7},{6,4},{7,5},{8,10},{9,11},{10,... | collective-permute-start | bytes 2359304 | tf_op jit(solution)/shard_map/ppermute | solution.py:62
  142.9 40.3 %collective-permute-start.22 = (bf16[128,1664]{1,0:T(8,128)(2,1)}, bf16[128,1664]{1,0:T(8,128)(2,1)}, u32[]{:S(2)}, u32[]{:S(2)}) collective-permute-start(bf16[128,1664]{1,0:T(8,128)(2,1)} %bitcast.29), channel_id=1, source_target_pairs={{0,2},{1,3},{2,0},{3,1},{4,6},{5,7},{6,4},{7,5},{8,10},{9,11},{10,... | collective-permute-start | bytes 1277960 | tf_op jit(solution)/shard_map/ppermute | solution.py:62
  143.6 83.8 %collective-permute-start.23 = (bf16[128,1664]{1,0:T(8,128)(2,1)}, bf16[128,1664]{1,0:T(8,128)(2,1)}, u32[]{:S(2)}, u32[]{:S(2)}) collective-permute-start(bf16[128,1664]{1,0:T(8,128)(2,1)} %collective-permute-done.19), channel_id=1, source_target_pairs={{0,2},{1,3},{2,0},{3,1},{4,6},{5,7},{6,4},{7,5},{8,10},{9,11},{10,... | collective-permute-start | bytes 1277960 | tf_op jit(solution)/shard_map/ppermute | solution.py:62
  177.9 45.4 %collective-permute-start.26 = (bf16[4,5,192,256]{3,2,1,0:T(8,128)(2,1)}, bf16[4,5,192,256]{3,2,1,0:T(8,128)(2,1)S(1)}, u32[]{:S(2)}, u32[]{:S(2)}) collective-permute-start(bf16[4,5,192,256]{3,2,1,0:T(8,128)(2,1)} %all-to-all-done.3), channel_id=1, source_target_pairs={{0,4},{4,0},{8,12},{12,8},{16,20},{20,16},{24,28},{28,24},{1,5},{5... | collective-permute-start | bytes 5898248 | tf_op jit(solution)/shard_map/ppermute | solution.py:62
  181.8 57.3 %collective-permute-start.24 = (bf16[128,1664]{1,0:T(8,128)(2,1)}, bf16[128,1664]{1,0:T(8,128)(2,1)S(1)}, u32[]{:S(2)}, u32[]{:S(2)}) collective-permute-start(bf16[128,1664]{1,0:T(8,128)(2,1)} %collective-permute-done.20), channel_id=1, source_target_pairs={{0,2},{1,3},{2,0},{3,1},{4,6},{5,7},{6,4},{7,5},{8,10},{9,11},{10,... | collective-permute-start | bytes 1277960 | tf_op jit(solution)/shard_map/ppermute | solution.py:62
  183.2 67.4 %collective-permute-start.29 = (bf16[5,128,1536]{2,1,0:T(8,128)(2,1)S(1)}, bf16[5,128,1536]{2,1,0:T(8,128)(2,1)S(1)}, u32[]{:S(2)}, u32[]{:S(2)}) collective-permute-start(bf16[5,128,1536]{2,1,0:T(8,128)(2,1)S(1)} %pad_maximum_fusion.3), channel_id=1, source_target_pairs={{0,1},{1,0},{2,3},{3,2},{4,5},{5,4},{6,7},{7,6},{8,9},{9,8},{10,11... | collective-permute-start | bytes 5898248 | tf_op jit(solution)/shard_map/ppermute | solution.py:62
  184.3 55.5 %collective-permute-start.25 = (bf16[128,1664]{1,0:T(8,128)(2,1)}, bf16[128,1664]{1,0:T(8,128)(2,1)S(1)}, u32[]{:S(2)}, u32[]{:S(2)}) collective-permute-start(bf16[128,1664]{1,0:T(8,128)(2,1)} %collective-permute-done.21), channel_id=1, source_target_pairs={{0,2},{1,3},{2,0},{3,1},{4,6},{5,7},{6,4},{7,5},{8,10},{9,11},{10,... | collective-permute-start | bytes 1277960 | tf_op jit(solution)/shard_map/ppermute | solution.py:62
  227.4 56.8 %collective-permute-start.27 = (bf16[5,1536,256]{2,1,0:T(8,128)(2,1)S(1)}, bf16[5,1536,256]{2,1,0:T(8,128)(2,1)}, u32[]{:S(2)}, u32[]{:S(2)}) collective-permute-start(bf16[5,1536,256]{2,1,0:T(8,128)(2,1)S(1)} %bitcast.319), channel_id=1, source_target_pairs={{0,1},{1,0},{2,3},{3,2},{4,5},{5,4},{6,7},{7,6},{8,9},{9,8},{10,11... | collective-permute-start | bytes 11796488 | tf_op jit(solution)/shard_map/ppermute | solution.py:62
  407.6 96.7 %collective-permute-start.63 = (bf16[1536,1280]{1,0:T(8,128)(2,1)}, bf16[1536,1280]{1,0:T(8,128)(2,1)}, u32[]{:S(2)}, u32[]{:S(2)}) collective-permute-start(bf16[1536,1280]{1,0:T(8,128)(2,1)} %bitcast.297), channel_id=1, source_target_pairs={{0,1},{1,0},{2,3},{3,2},{4,5},{5,4},{6,7},{7,6},{8,9},{9,8},{10,11... | collective-permute-start | bytes 11796488 | tf_op jit(solution)/shard_map/ppermute | solution.py:62
  435.9 84.1 %collective-permute-start.65 = (bf16[5,128,1536]{2,1,0:T(8,128)(2,1)}, bf16[5,128,1536]{2,1,0:T(8,128)(2,1)}, u32[]{:S(2)}, u32[]{:S(2)}) collective-permute-start(bf16[5,128,1536]{2,1,0:T(8,128)(2,1)} %bitcast.107), channel_id=1, source_target_pairs={{0,1},{1,0},{2,3},{3,2},{4,5},{5,4},{6,7},{7,6},{8,9},{9,8},{10,11... | collective-permute-start | bytes 5898248 | tf_op jit(solution)/shard_map/ppermute | solution.py:62
  437.9 40.3 %collective-permute-start.31 = (bf16[128,1536]{1,0:T(8,128)(2,1)}, bf16[128,1536]{1,0:T(8,128)(2,1)}, u32[]{:S(2)}, u32[]{:S(2)}) collective-permute-start(bf16[128,1536]{1,0:T(8,128)(2,1)} %get-tuple-element.65), channel_id=1, source_target_pairs={{0,2},{1,3},{2,0},{3,1},{4,6},{5,7},{6,4},{7,5},{8,10},{9,11},{10,... | collective-permute-start | bytes 1179656 | tf_op jit(solution)/shard_map/ppermute | solution.py:62
  442.4 144.9 %collective-permute-start.30 = (bf16[128,1536]{1,0:T(8,128)(2,1)}, bf16[128,1536]{1,0:T(8,128)(2,1)}, u32[]{:S(2)}, u32[]{:S(2)}) collective-permute-start(bf16[128,1536]{1,0:T(8,128)(2,1)} %get-tuple-element.62), channel_id=1, source_target_pairs={{0,2},{1,3},{2,0},{3,1},{4,6},{5,7},{6,4},{7,5},{8,10},{9,11},{10,... | collective-permute-start | bytes 1179656 | tf_op jit(solution)/shard_map/ppermute | solution.py:62
  485.7 44.1 %all-to-all-start.5 = ((f32[32,1,1008]{2,1,0:T(1,128)}), f32[32,1,1008]{2,1,0:T(1,128)S(1)}, u32[]{:S(2)}, u32[]{:S(2)}) async-start(f32[32,1,1008]{2,1,0:T(1,128)} %reshape.1002), calls=%async_computation.5 | async-start | bytes 262144 | tf_op jit(solution)/shard_map/all_to_all | solution.py:545
  511.2 60.6 %collective-permute-start.64 = (bf16[4,192,1280]{2,1,0:T(8,128)(2,1)}, bf16[4,192,1280]{2,1,0:T(8,128)(2,1)}, u32[]{:S(2)}, u32[]{:S(2)}) collective-permute-start(bf16[4,192,1280]{2,1,0:T(8,128)(2,1)} %dynamic-slice_bitcast_fusion), channel_id=1, source_target_pairs={{0,4},{4,0},{8,12},{12,8},{16,20},{20,16},{24,28},{28,24},{1,5},{5... | collective-permute-start | bytes 5898248 | tf_op jit(solution)/shard_map/ppermute | solution.py:62
  512.5 52.8 %collective-permute-start.55 = (bf16[192,1024]{1,0:T(8,128)(2,1)}, bf16[192,1024]{1,0:T(8,128)(2,1)}, u32[]{:S(2)}, u32[]{:S(2)}) collective-permute-start(bf16[192,1024]{1,0:T(8,128)(2,1)} %get-tuple-element.54), channel_id=1, source_target_pairs={{0,4},{4,0},{8,12},{12,8},{16,20},{20,16},{24,28},{28,24},{1,5},{5... | collective-permute-start | bytes 1179656 | tf_op jit(solution)/shard_map/ppermute | solution.py:62
  520.0 45.3 %collective-permute-start.61 = (bf16[192,1024]{1,0:T(8,128)(2,1)}, bf16[192,1024]{1,0:T(8,128)(2,1)}, u32[]{:S(2)}, u32[]{:S(2)}) collective-permute-start(bf16[192,1024]{1,0:T(8,128)(2,1)} %fusion.37), channel_id=1, source_target_pairs={{0,8},{4,12},{8,16},{12,20},{16,24},{20,28},{24,0},{28,4},{1,9},{5... | collective-permute-start | bytes 1179656 | tf_op jit(solution)/shard_map/ppermute | solution.py:62
  528.4 59.0 %collective-permute-start.36 = (bf16[128,1536]{1,0:T(8,128)(2,1)}, bf16[128,1536]{1,0:T(8,128)(2,1)}, u32[]{:S(2)}, u32[]{:S(2)}) collective-permute-start(bf16[128,1536]{1,0:T(8,128)(2,1)} %fusion.51), channel_id=1, source_target_pairs={{0,8},{4,12},{8,16},{12,20},{16,24},{20,28},{24,0},{28,4},{1,9},{5... | collective-permute-start | bytes 1179656 | tf_op jit(solution)/shard_map/ppermute | solution.py:62
  529.8 38.5 %all-to-all-start.4 = ((f32[32,1,48]{2,1,0:T(1,128)}), f32[32,1,48]{2,1,0:T(1,128)S(1)}, u32[]{:S(2)}, u32[]{:S(2)}) async-start(f32[32,1,48]{2,1,0:T(1,128)} %reshape.948), calls=%async_computation.4 | async-start | bytes 32768 | tf_op jit(solution)/shard_map/all_to_all | solution.py:548
  580.3 67.3 %all-to-all-start.7 = ((bf16[4,192,1280]{2,1,0:T(8,128)(2,1)}), bf16[4,192,1280]{2,1,0:T(8,128)(2,1)}, u32[]{:S(2)}, u32[]{:S(2)}) async-start(bf16[4,192,1280]{2,1,0:T(8,128)(2,1)} %fusion.2), calls=%async_computation.7 | async-start | bytes 3932160 | tf_op jit(solution)/shard_map/all_to_all | solution.py:559
  (99 other events, 1760.9 us)

commit v2 on v1

v2 whole, which is shorter than its diff:
```python
import functools

import jax
import jax.numpy as jnp
from jax import lax
from jax.experimental import pallas as pl
from jax.experimental.pallas import tpu as pltpu
from jax.sharding import PartitionSpec as P

HEADS = 24
KV_HEADS = 8
HEAD_DIM = 64

EPSILON = 1e-06
ROPE_BASE = 10000.0
RESIDUAL_SCALE = 0.22
SCORE_SCALE = 1.0 / 64.0
NEGATIVE = -1e30
LANES = 128

BF16 = jnp.bfloat16
F32 = jnp.float32
ALL = ("dp", "expert")


def dot(a, b, dims=((1,), (0,))):
    return lax.dot_general(a, b, (dims, ((), ())), preferred_element_type=F32)


class Rings:
    def __init__(self, dp_count, expert_count):
        y_count = 1
        while dp_count % (2 * y_count) == 0 and 8 * y_count * y_count <= dp_count:
            y_count *= 2
        self.y, self.z = y_count, dp_count // y_count
        self.core = 2 if expert_count % 2 == 0 else 1
        self.x = expert_count // self.core
        zs, ys, xs, cs = range(self.z), range(self.y), range(self.x), range(self.core)
        self.z_groups = [[z * self.y + y for z in zs] for y in ys]
        self.token_groups = [
            [(z * self.y + y) * expert_count + x * self.core + c for z in zs for x in xs]
            for y in ys
            for c in cs
        ]
        self.table = {
            "z": ("dp", self.z, [(z * self.y + y, (z + 1) % self.z * self.y + y) for z in zs for y in ys]),
            "y": ("dp", self.y, [(z * self.y + y, z * self.y + (y + 1) % self.y) for z in zs for y in ys]),
            "x": (
                "expert",
                self.x,
                [(x * self.core + c, (x + 1) % self.x * self.core + c) for x in xs for c in cs],
            ),
            "c": (
                "expert",
                self.core,
                [(x * self.core + c, x * self.core + (c + 1) % self.core) for x in xs for c in cs],
            ),
        }
        d, e = lax.axis_index("dp"), lax.axis_index("expert")
        self.at = {"z": d // self.y, "y": d % self.y, "x": e // self.core, "c": e % self.core}

    def count(self, ring):
        return self.table[ring][1]

    def step(self, value, ring):
        axis, _, pairs = self.table[ring]
        return lax.ppermute(value, axis, pairs)

    def origin(self, ring, slot):
        return lax.rem(self.at[ring] + (self.count(ring) - slot), self.count(ring))

    def gather(self, value, ring, meet=None):
        slots = [value]
        for s in range(1, self.count(ring)):
            arrived = self.step(slots[-1], ring)
            slots.append(arrived if meet is None else meet(s, arrived))
        return slots

    def reduce(self, parts, ring, wire=BF16, meet=None):
        running = None
        for slot in range(1, self.count(ring)):
            term = parts[slot]
            if running is not None:
                term = term.astype(F32) + running.astype(F32)
            running = self.step(term.astype(wire), ring)
            if meet is not None:
                running = meet(slot, running)
        own = parts[0].astype(F32)
        return own if running is None else own + running.astype(F32)

    def gather_two(self, value, first, second, meet=None):
        columns, slots = [], [value]
        for t in range(1, self.count(first)):
            arrived = self.step(slots[-1], first)
            column = self.gather(slots[-1], second)
            arrived, *rest = tie(arrived, *column[1:])
            columns.append([column[0]] + rest)
            slots.append(arrived if meet is None else meet(t, arrived))
        columns.append(self.gather(slots[-1], second))
        return [[column[s] for column in columns] for s in range(self.count(second))]

    def reduce_two(self, parts, first, second, wire=BF16, meet=None):
        count = self.count(first)
        arrived = {}
        for t in list(range(1, count)) + [0]:
            running = None
            for slot in range(1, self.count(second)):
                term = parts[slot][t]
                if running is not None:
                    term = term.astype(F32) + running.astype(F32)
                running = self.step(term.astype(wire), second)
            if running is not None and meet is not None:
                running = meet(second, t, running)
            arrived[t] = running

        def partial(t):
            own = parts[0][t].astype(F32)
            return own if arrived[t] is None else own + arrived[t].astype(F32)

        running = None
        for t in range(1, count):
            term = partial(t)
            if running is not None:
                term = term + running.astype(F32)
            running = self.step(term.astype(wire), first)
            ahead = (t + 2) % count
            if arrived[ahead] is not None and 0 < t < count - 1:
                running, arrived[ahead] = tie(running, arrived[ahead])
            if meet is not None:
                running = meet(first, t, running)
        own = partial(0)
        return own if running is None else own + running.astype(F32)


def tie(*values):
    return lax.optimization_barrier(values)


def in_order(slots, position_of, count):
    stacked = jnp.stack(slots)
    return [
        lax.dynamic_index_in_dim(stacked, lax.rem(position_of + (count - i), count), 0, False)
        for i in range(count)
    ]


def fetch(copies, semaphores):
    started = [pltpu.make_async_copy(a, b, semaphores.at[i]) for i, (a, b) in enumerate(copies)]
    for copy in started:
        copy.start()
    for copy in started:
        copy.wait()


def anywhere():
    return pl.BlockSpec(memory_space=pl.ANY)


def on_chip():
    return pl.BlockSpec(memory_space=pltpu.VMEM)


def rotate_pairs(values, cosine, sine, direction):
    lane = lax.broadcasted_iota(jnp.int32, (values.shape[0], LANES), 1)
    low = (lane & (HEAD_DIM - 1)) < HEAD_DIM // 2
    pieces = []
    for start in range(0, values.shape[1], LANES):
        piece = values[:, start : start + LANES]
        partner = jnp.where(
            low,
            pltpu.roll(piece, LANES - HEAD_DIM // 2, 1),
            pltpu.roll(piece, HEAD_DIM // 2, 1),
        )
        turned = partner * sine
        pieces.append(piece * cosine + turned if direction > 0 else piece * cosine - turned)
    return jnp.concatenate(pieces, 1)


def weight_copies(shape, spots_ref, packs, w_ref, wo_ref, small_ref=None):
    if shape["whole"]:
        copies = [(packs[0], w_ref), (packs[1], wo_ref)]
        return copies if small_ref is None else copies + [(packs[2], small_ref)]
    copies = []
    rows, part, columns = shape["pack_rows"], shape["weight_rows"], shape["qkv_columns"]
    wide = shape["merged_columns"]
    for slot, pack in enumerate(packs):
        spot = spots_ref[slot]
        at = pl.multiple_of(spot * rows, rows)
        copies.append((pack.at[:, pl.ds(0, columns)], w_ref.at[pl.ds(at, rows), :]))
        if small_ref is not None:
            copies.append((pack.at[:, pl.ds(columns, LANES)], small_ref.at[pl.ds(at, rows), :]))
        at = pl.multiple_of(spot * part, part)
        for i in range(rows // part):
            copies.append(
                (
                    pack.at[pl.ds(i * part, part), pl.ds(columns + LANES, wide)],
                    wo_ref.at[pl.ds(at, part), pl.ds(i * wide, wide)],
                )
            )
    return copies


def row_copies(slots, into_ref):
    micros, rows, _ = slots[0].shape
    return [
        (slot.at[m], into_ref.at[m, pl.ds(i * rows, rows), :])
        for i, slot in enumerate(slots)
        for m in range(micros)
    ]


def attention_forward_kernel(shape, spots_ref, *refs):
    packs, refs = refs[: shape["packs"]], refs[shape["packs"] :]
    slots, refs = refs[: shape["slots"]], refs[shape["slots"] :]
    cos_ref, sin_ref, bias_ref = refs[:3]
    out_refs, refs = refs[3 : 3 + shape["slots"]], refs[3 + shape["slots"] :]
    x_ref, n1_ref, small_ref, rows_ref, qkv_ref, merged_ref, lse_ref = refs[:7]
    w_ref, wo_ref, semaphores = refs[7:]
    heads, kv_heads = shape["heads"], shape["kv_heads"]
    share = heads // kv_heads
    rotated = (heads + kv_heads) * HEAD_DIM
    micro = pl.program_id(0)

    @pl.when(micro == 0)
    def _():
        copies = weight_copies(shape, spots_ref, packs, w_ref, wo_ref, small_ref)
        fetch(row_copies(slots, x_ref) + copies, semaphores)
        count = rows_ref.shape[0]
        row = lax.broadcasted_iota(jnp.int32, (count, LANES), 0)
        column = lax.broadcasted_iota(jnp.int32, (count, LANES), 1)
        same = jnp.where(row == column, 1.0, 0.0).astype(BF16)
        rows_ref[...] = dot(same, small_ref[...], ((1,), (1,)))

    x = x_ref[micro].astype(F32)
    inverse = lax.rsqrt(jnp.mean(x * x, -1, keepdims=True) + EPSILON)
    at = shape["gain_at"]
    n1_ref[micro] = (x * inverse * rows_ref[at : at + 1, :]).astype(BF16)
    pre = dot(n1_ref[micro], w_ref[...])
    turned = rotate_pairs(pre[:, :rotated], cos_ref[0], sin_ref[0], 1)
    qkv_ref[0, :, :rotated] = turned.astype(BF16)
    qkv_ref[0, :, rotated:] = pre[:, rotated:].astype(BF16)
    bias = bias_ref[0]
    lane = lax.broadcasted_iota(jnp.int32, (pre.shape[0], LANES), 1)
    sums = jnp.zeros((pre.shape[0], LANES), F32)
    for head in range(heads):
        group = head // share
        key_at = (heads + group) * HEAD_DIM
        value_at = rotated + group * HEAD_DIM
        query = qkv_ref[0, :, head * HEAD_DIM : (head + 1) * HEAD_DIM]
        key = qkv_ref[0, :, key_at : key_at + HEAD_DIM]
        value = qkv_ref[0, :, value_at : value_at + HEAD_DIM]
        scores = dot(query, key, ((1,), (1,))) * SCORE_SCALE + bias
        highest = jnp.max(scores, -1, keepdims=True)
        exponent = jnp.exp(scores - highest)
        total = jnp.sum(exponent, -1, keepdims=True)
        weights = (exponent / total).astype(BF16)
        merged_ref[0, :, head * HEAD_DIM : (head + 1) * HEAD_DIM] = dot(weights, value).astype(BF16)
        sums = jnp.where(lane == head, highest + jnp.log(total), sums)
    lse_ref[0] = sums
    rows = out_refs[0].shape[1]
    for i, out_ref in enumerate(out_refs):
        out_ref[0] = dot(merged_ref[0, i * rows : (i + 1) * rows, :], wo_ref[...]).astype(BF16)


def attention_backward_kernel(shape, spots_ref, *refs):
    packs, refs = refs[: shape["packs"]], refs[shape["packs"] :]
    slots, refs = refs[: shape["slots"]], refs[shape["slots"] :]
    cos_ref, sin_ref, bias_ref, qkv_ref, lse_ref, n1_ref, merged_ref = refs[:7]
    x_ref, n2_ref, logits_ref, mlp_ref = refs[7:11]
    refs = refs[11:]
    out_refs, refs = refs[: shape["slots"]], refs[shape["slots"] :]
    grads, refs = refs[: shape["packs"]], refs[shape["packs"] :]
    ga_ref, w_ref, wo_ref, dqkv_ref, turned_ref, gain_ref, dw_ref, dwo_ref, ds_ref, semaphores = refs
    heads, kv_heads = shape["heads"], shape["kv_heads"]
    share = heads // kv_heads
    rotated = (heads + kv_heads) * HEAD_DIM
    micro = pl.program_id(0)

    @pl.when(micro == 0)
    def _():
        copies = row_copies(slots, ga_ref) + weight_copies(shape, spots_ref, packs, w_ref, wo_ref)
        fetch(copies, semaphores)
        gain_ref[...] = jnp.zeros_like(gain_ref)
        gain_ref[1:2, :] = mlp_ref[...]

    grad_merged = dot(ga_ref[micro], wo_ref[...], ((1,), (1,))).astype(BF16)
    bias = bias_ref[0]
    for group in range(kv_heads):
        key_at = (heads + group) * HEAD_DIM
        value_at = rotated + group * HEAD_DIM
        key = qkv_ref[0, :, key_at : key_at + HEAD_DIM]
        value = qkv_ref[0, :, value_at : value_at + HEAD_DIM]
        grad_key, grad_value = None, None
        for head in range(group * share, (group + 1) * share):
            query = qkv_ref[0, :, head * HEAD_DIM : (head + 1) * HEAD_DIM]
            grad_rows = grad_merged[:, head * HEAD_DIM : (head + 1) * HEAD_DIM]
            scores = dot(query, key, ((1,), (1,))) * SCORE_SCALE + bias
            chance = jnp.exp(scores - lse_ref[0, :, head : head + 1])
            weights = chance.astype(BF16)
            grad_chance = dot(grad_rows, value, ((1,), (1,)))
            delta = jnp.sum(chance * grad_chance, -1, keepdims=True)
            grad_raw = (chance * (grad_chance - delta) * SCORE_SCALE).astype(BF16)
            turned_ref[:, head * HEAD_DIM : (head + 1) * HEAD_DIM] = dot(grad_raw, key)
            key_part = dot(grad_raw, query, ((0,), (0,)))
            value_part = dot(weights, grad_rows, ((0,), (0,)))
            grad_key = key_part if grad_key is None else grad_key + key_part
            grad_value = value_part if grad_value is None else grad_value + value_part
        turned_ref[:, key_at : key_at + HEAD_DIM] = grad_key
        dqkv_ref[micro, :, value_at : value_at + HEAD_DIM] = grad_value.astype(BF16)
    back = rotate_pairs(turned_ref[...], cos_ref[0], sin_ref[0], -1)
    dqkv_ref[micro, :, :rotated] = back.astype(BF16)
    rows = out_refs[0].shape[1]
    first = dot(dqkv_ref[micro], w_ref[...], ((1,), (1,)))
    for i, out_ref in enumerate(out_refs):
        out_ref[0] = first[i * rows : (i + 1) * rows, :].astype(BF16)
    x = x_ref[0].astype(F32)
    unit = x * lax.rsqrt(jnp.mean(x * x, -1, keepdims=True) + EPSILON)
    gain_ref[0:1, :] += jnp.sum(first * unit, 0, keepdims=True)

    @pl.when(micro == pl.num_programs(0) - 1)
    def _():
        def flat(ref):
            return ref[...].reshape(ref.shape[0] * ref.shape[1], ref.shape[2])

        dw = dot(flat(n1_ref), flat(dqkv_ref), ((0,), (0,))).astype(BF16)
        dwo = dot(flat(merged_ref), flat(ga_ref), ((0,), (0,))).astype(BF16)
        row = lax.broadcasted_iota(jnp.int32, (gain_ref.shape[0], LANES), 0)
        column = lax.broadcasted_iota(jnp.int32, (gain_ref.shape[0], LANES), 1)
        spread = jnp.where((row < 2) & (column == row + shape["gain_at"]), 1.0, 0.0)
        gains = lax.dot_general(
            gain_ref[...],
            spread,
            (((0,), (0,)), ((), ())),
            precision=lax.Precision.HIGHEST,
            preferred_element_type=F32,
        )
        ds = (gains + dot(n2_ref[...], logits_ref[...], ((0,), (0,)))).astype(BF16)
        if shape["whole"]:
            grads[0][...] = dw
            grads[1][...] = dwo
            grads[2][...] = ds
        else:
            dw_ref[...] = dw
            dwo_ref[...] = dwo
            ds_ref[...] = ds
            pack_rows, part, columns = shape["pack_rows"], shape["weight_rows"], shape["qkv_columns"]
            wide = shape["merged_columns"]
            for slot, grad_ref in enumerate(grads):
                spot = spots_ref[slot]
                at = pl.multiple_of(spot * pack_rows, pack_rows)
                grad_ref[:, :columns] = dw_ref[pl.ds(at, pack_rows), :]
                grad_ref[:, columns : columns + LANES] = ds_ref[pl.ds(at, pack_rows), :]
                at = pl.multiple_of(spot * part, part)
                for i in range(pack_rows // part):
                    grad_ref[i * part : (i + 1) * part, columns + LANES :] = dwo_ref[
                        pl.ds(at, part), i * wide : (i + 1) * wide
                    ]


def per_micro(shape):
    return pl.BlockSpec((1,) + tuple(shape[1:]), lambda m, s: (m,) + (0,) * (len(shape) - 1))


def fixed(shape):
    return pl.BlockSpec(tuple(shape), lambda m, s: (0,) * len(shape))


def attention_forward(shape, spots, packs, slots, cosine, sine, bias):
    micros, rows, width = slots[0].shape
    group = rows * len(slots)
    columns, merged = shape["qkv_columns"], shape["heads"] * HEAD_DIM
    outs = [jax.ShapeDtypeStruct((micros, rows, width), BF16) for _ in slots]
    specs = [per_micro(o.shape) for o in outs]
    more = [
        jax.ShapeDtypeStruct((micros, group, width), BF16),
        jax.ShapeDtypeStruct((micros, group, width), BF16),
        jax.ShapeDtypeStruct((width, LANES), BF16),
        jax.ShapeDtypeStruct((LANES // 2, width), F32),
        jax.ShapeDtypeStruct((micros, group, columns), BF16),
        jax.ShapeDtypeStruct((micros, group, merged), BF16),
        jax.ShapeDtypeStruct((micros, group, LANES), F32),
    ]
    specs += [fixed(o.shape) for o in more[:4]] + [per_micro(o.shape) for o in more[4:]]
    results = pl.pallas_call(
        functools.partial(attention_forward_kernel, shape),
        grid_spec=pltpu.PrefetchScalarGridSpec(
            num_scalar_prefetch=1,
            grid=(micros,),
            in_specs=[anywhere() for _ in packs + slots]
            + [per_micro(cosine.shape), per_micro(sine.shape), per_micro(bias.shape)],
            out_specs=specs,
            scratch_shapes=[
                pltpu.VMEM((width, columns), BF16),
                pltpu.VMEM((merged, width), BF16),
                pltpu.SemaphoreType.DMA((shape["copies"],)),
            ],
        ),
        out_shape=outs + more,
        name="attention_forward",
    )(spots, *packs, *slots, cosine, sine, bias)
    return (results[: len(slots)],) + tuple(results[len(slots) :])


def attention_backward(shape, spots, packs, slots, by_micro, at_once):
    micros, rows, width = slots[0].shape
    group = rows * len(slots)
    columns, merged_rows = shape["qkv_columns"], shape["heads"] * HEAD_DIM
    outs = [jax.ShapeDtypeStruct((micros, rows, width), BF16) for _ in slots]
    grads = [jax.ShapeDtypeStruct(pack.shape, BF16) for pack in packs]
    results = pl.pallas_call(
        functools.partial(attention_backward_kernel, shape),
        grid_spec=pltpu.PrefetchScalarGridSpec(
            num_scalar_prefetch=1,
            grid=(micros,),
            in_specs=[anywhere() for _ in packs + slots]
            + [per_micro(v.shape) for v in by_micro[:5]]
            + [fixed(v.shape) for v in at_once[:2]]
            + [per_micro(by_micro[5].shape)]
            + [fixed(v.shape) for v in at_once[2:]],
            out_specs=[per_micro(o.shape) for o in outs] + [fixed(g.shape) for g in grads],
            scratch_shapes=[
                pltpu.VMEM((micros, group, width), BF16),
                pltpu.VMEM((width, columns), BF16),
                pltpu.VMEM((merged_rows, width), BF16),
                pltpu.VMEM((micros, group, columns), BF16),
                pltpu.VMEM((group, (shape["heads"] + shape["kv_heads"]) * HEAD_DIM), F32),
                pltpu.VMEM((8, width), F32),
                pltpu.VMEM((width, columns), BF16),
                pltpu.VMEM((merged_rows, width), BF16),
                pltpu.VMEM((width, LANES), BF16),
                pltpu.SemaphoreType.DMA((shape["copies"],)),
            ],
        ),
        out_shape=outs + grads,
        name="attention_backward",
    )(spots, *packs, *slots, *by_micro[:5], *at_once[:2], by_micro[5], *at_once[2:])
    return list(results[: len(slots)]), list(results[len(slots) :])


def experts_kernel(shape, table_ref, *refs):
    slots, cores, ys, zs = shape["slots"], shape["cores"], shape["ys"], shape["zs"]
    own, hidden, half = shape["own"], shape["hidden"], LANES // 2
    x_slots, refs = refs[:slots], refs[slots:]
    beside, refs = refs[:slots], refs[slots:]
    gu_parts, refs = refs[: cores * ys], refs[cores * ys :]
    dn_parts, refs = refs[: cores * ys], refs[cores * ys :]
    wr_ref, mixed_ref, dx_ref, gate_ref, gg_ref, x_ref, gm_ref = refs[:7]
    act_refs, refs = refs[7 : 7 + cores], refs[7 + cores :]
    dgu_refs, refs = refs[:cores], refs[cores:]
    mask_ref, wgu_ref, wdn_ref, semaphores = refs
    rows, width = x_slots[0].shape
    part = width // (ys * zs)
    wide = 2 * hidden * own
    local = cores * own

    copies = []
    for i in range(slots):
        at = pl.ds(i * rows, rows)
        copies.append((x_slots[i], x_ref.at[at, :]))
        copies.append((beside[i].at[:, pl.ds(0, width)], gm_ref.at[at, :]))
        copies.append((beside[i].at[:, pl.ds(width, LANES)], mask_ref.at[at, :]))
    step = hidden // ys
    for c in range(cores):
        for s in range(ys):
            y = table_ref[local + s]
            for z in range(zs):
                at = pl.multiple_of((z * ys + y) * part, part)
                copies.append(
                    (
                        gu_parts[c * ys + s].at[z],
                        wgu_ref.at[pl.ds(at, part), pl.ds(c * wide, wide)],
                    )
                )
            for e in range(own):
                at = pl.multiple_of((c * own + e) * hidden + y * step, step)
                copies.append((dn_parts[c * ys + s].at[e], wdn_ref.at[pl.ds(at, step), :]))
    fetch(copies, semaphores)

    block = shape["block"]
    lane = lax.broadcasted_iota(jnp.int32, (block, LANES), 1)

    def body(b, carry):
        at = pl.ds(pl.multiple_of(b * block, block), block)
        x = x_ref[at, :]
        named = mask_ref[at, :].astype(F32) > 0.5
        logits = jnp.where(named, dot(x, wr_ref[...]), NEGATIVE)
        highest = jnp.max(logits, -1, keepdims=True)
        exponent = jnp.where(named, jnp.exp(logits - highest), 0.0)
        gates = exponent / jnp.sum(exponent, -1, keepdims=True)
        gate_ref[at, :] = gates
        picked = jnp.zeros((block, LANES), F32)
        pre_all = dot(x, wgu_ref[...])
        grad_act = dot(gm_ref[at, :], wdn_ref[...], ((1,), (1,)))
        for c in range(cores):
            for e in range(own):
                j = c * own + e
                mine = lane == table_ref[j]
                gate = jnp.sum(jnp.where(mine, gates, 0.0), -1, keepdims=True)
                gate_pre = pre_all[:, 2 * hidden * j : 2 * hidden * j + hidden]
                up_pre = pre_all[:, 2 * hidden * j + hidden : 2 * hidden * (j + 1)]
                grad_one = grad_act[:, j * hidden : (j + 1) * hidden]
                sig = jax.nn.sigmoid(gate_pre)
                silu = gate_pre * sig
                activated = (silu * up_pre).astype(BF16).astype(F32)
                found = jnp.sum(activated * grad_one, -1, keepdims=True)
                picked = jnp.where(mine, found, picked)
                act_refs[c][at, e * hidden : (e + 1) * hidden] = (activated * gate).astype(BF16)
                grad_one = grad_one * gate
                base = 2 * hidden * e
                dgu_refs[c][at, base : base + hidden] = (
                    grad_one * up_pre * sig * (1.0 + gate_pre * (1.0 - sig))
                ).astype(BF16)
                dgu_refs[c][at, base + hidden : base + 2 * hidden] = (grad_one * silu).astype(BF16)
        dgu = jnp.concatenate([ref[at, :] for ref in dgu_refs], 1)
        dx_ref[at, :] = dot(dgu, wgu_ref[...], ((1,), (1,))).astype(BF16)
        act = jnp.concatenate([ref[at, :] for ref in act_refs], 1)
        mixed_ref[at, :] = dot(act, wdn_ref[...]).astype(BF16)
        coarse = picked.astype(BF16).astype(F32)
        fine = pltpu.roll(picked - coarse, half, 1)
        packed = jnp.where(lane < half, coarse, fine).astype(BF16)
        for q in range(block // rows):
            place = table_ref[local + ys + b * (block // rows) + q]
            gg_ref[pl.ds(pl.multiple_of(place * rows, rows), rows), :] = packed[q * rows : (q + 1) * rows]
        return carry

    lax.fori_loop(0, slots * rows // block, body, 0)


def run_experts(shape, table, x_slots, beside, gu_parts, dn_parts, wr):
    rows, width = x_slots[0].shape
    total = rows * len(x_slots)
    cores, own, hidden = shape["cores"], shape["own"], shape["hidden"]
    outs = [
        jax.ShapeDtypeStruct((total, width), BF16),
        jax.ShapeDtypeStruct((total, width), BF16),
        jax.ShapeDtypeStruct((total, LANES), F32),
        jax.ShapeDtypeStruct((total, LANES), BF16),
        jax.ShapeDtypeStruct((total, width), BF16),
        jax.ShapeDtypeStruct((total, width), BF16),
    ]
    outs += [jax.ShapeDtypeStruct((total, own * hidden), BF16) for _ in range(cores)]
    outs += [jax.ShapeDtypeStruct((total, 2 * own * hidden), BF16) for _ in range(cores)]
    shape = dict(shape, slots=len(x_slots), block=2 * rows if len(x_slots) % 2 == 0 else rows)
    copies = 3 * len(x_slots) + cores * shape["ys"] * (shape["zs"] + own)
    operands = x_slots + beside + gu_parts + dn_parts
    return pl.pallas_call(
        functools.partial(experts_kernel, shape),
        in_specs=[pl.BlockSpec(memory_space=pltpu.SMEM)] + [anywhere() for _ in operands] + [on_chip()],
        out_specs=[on_chip() for _ in outs],
        out_shape=outs,
        scratch_shapes=[
            pltpu.VMEM((total, LANES), BF16),
            pltpu.VMEM((width, cores * own * 2 * hidden), BF16),
            pltpu.VMEM((cores * own * hidden, width), BF16),
            pltpu.SemaphoreType.DMA((copies,)),
        ],
        compiler_params=pltpu.CompilerParams(vmem_limit_bytes=60 << 20),
        name="experts",
    )(table, *operands, wr)


def pack_kernel(hidden, gate_ref, up_ref, out_ref):
    for z in range(out_ref.shape[0]):
        out_ref[z, :, :hidden] = gate_ref[0, :, z * hidden : (z + 1) * hidden]
        out_ref[z, :, hidden:] = up_ref[0, :, z * hidden : (z + 1) * hidden]


def pack_experts(w_gate, w_up, zs):
    own, part, hidden_all = w_gate.shape
    hidden = hidden_all // zs
    return pl.pallas_call(
        functools.partial(pack_kernel, hidden),
        grid=(own,),
        in_specs=[pl.BlockSpec((1, part, hidden_all), lambda e: (e, 0, 0))] * 2,
        out_specs=pl.BlockSpec((zs, part, 2 * hidden), lambda e: (0, 0, e)),
        out_shape=jax.ShapeDtypeStruct((zs, part, own * 2 * hidden), BF16),
        name="pack_experts",
    )(w_gate, w_up)


def unpack_kernel(hidden, in_ref, gate_ref, up_ref):
    for z in range(in_ref.shape[0]):
        gate_ref[0, :, z * hidden : (z + 1) * hidden] = in_ref[z, :, :hidden].astype(F32)
        up_ref[0, :, z * hidden : (z + 1) * hidden] = in_ref[z, :, hidden:].astype(F32)


def unpack_experts(packed, own):
    zs, part, wide = packed.shape
    hidden = wide // own // 2
    out = jax.ShapeDtypeStruct((own, part, zs * hidden), F32)
    return pl.pallas_call(
        functools.partial(unpack_kernel, hidden),
        grid=(own,),
        in_specs=[pl.BlockSpec((zs, part, 2 * hidden), lambda e: (0, 0, e))],
        out_specs=[pl.BlockSpec((1, part, zs * hidden), lambda e: (e, 0, 0))] * 2,
        out_shape=[out, out],
        name="unpack_experts",
    )(packed)


def per_device(
    tokens,
    cotangent,
    attn_gain,
    mlp_gain,
    w_query,
    w_key,
    w_value,
    w_out,
    w_router,
    w_gate,
    w_up,
    w_down,
    shuffle,
    routes,
    lengths,
):
    micros, rows, width = tokens.shape
    dp_count, members = lax.axis_size("dp"), lax.axis_size("expert")
    devices = dp_count * members
    rings = Rings(dp_count, members)
    zn, yn, xn, cn = rings.z, rings.y, rings.x, rings.core
    group_rows = rows * members
    experts_all = w_router.shape[1]
    own_experts, model_part, hidden_all = w_gate.shape
    hidden_part = hidden_all // zn
    heads, kv_heads = HEADS // members, KV_HEADS // members
    weight_rows = w_query.shape[0]
    home_rows = micros * rows
    half_lanes = LANES // 2

    def over_members(value):
        return [slot for column in rings.gather_two(value, "c", "x") for slot in column]

    def sum_members(parts):
        return rings.reduce_two([[parts[s * cn + t] for s in range(xn)] for t in range(cn)], "x", "c")

    def by_member(w):
        return w.reshape(weight_rows, members, w.shape[1] // members)

    small = jnp.concatenate([w_router, attn_gain[:, None], mlp_gain[:, None]], 1)
    small = jnp.pad(small, ((0, 0), (0, LANES - experts_all - 2)))
    small = jnp.broadcast_to(small[:, None, :], (weight_rows, members, LANES))
    mine = jnp.concatenate([by_member(w_query), by_member(w_key), by_member(w_value), small], 2)
    mine = lax.all_to_all(mine.transpose(1, 0, 2), "expert", 0, 0)
    gate_up = pack_experts(w_gate, w_up, zn)
    mine, gate_up = tie(mine, gate_up)
    small_at = mine.shape[2]
    qkv_columns = small_at - LANES
    pack_rows = members * weight_rows
    mine = mine.reshape(pack_rows, small_at)
    to_heads = [(s, (s % dp_count) * members + s // dp_count) for s in range(devices)]
    to_home = [(t, s) for s, t in to_heads]
    out_mine = lax.ppermute(w_out, ALL, to_heads)
    merged_columns = width // members
    pack = jnp.concatenate(
        [out_mine[:, i * merged_columns : (i + 1) * merged_columns] for i in range(members)], 0
    )
    pack = jnp.concatenate([mine, pack], 1)
    whole = weight_rows % 16 != 0
    attention_shape = {
        "heads": heads,
        "kv_heads": kv_heads,
        "whole": whole,
        "pack_rows": pack_rows,
        "weight_rows": weight_rows,
        "qkv_columns": qkv_columns,
        "merged_columns": merged_columns,
        "slots": members,
        "gain_at": experts_all,
        "packs": 3 if whole else dp_count,
        "copies": micros * members + (3 if whole else dp_count * (2 + members)),
    }
    inputs = tokens.astype(F32)
    inv_first = lax.rsqrt(jnp.mean(inputs * inputs, -1, keepdims=True) + EPSILON)
    unit_first = inputs * inv_first
    group_tokens = over_members(tokens)

    pack, routes = tie(pack, routes)
    dealt = lax.all_to_all(
        routes.reshape(micros, dp_count, rows // dp_count, routes.shape[2]), "dp", 1, 1
    ).reshape(micros, rows, routes.shape[2])
    lane_ids = jnp.arange(LANES, dtype=jnp.int32)
    hot = jnp.sum((dealt[:, :, :, None] == lane_ids).astype(F32), 2).astype(BF16)
    place = (shuffle[:, 0, :, None] == jnp.arange(rows, dtype=jnp.int32)).astype(BF16)
    named = jnp.einsum("mir,mix->mrx", place, hot, preferred_element_type=F32).astype(BF16)

    grad_result = cotangent.astype(F32)
    grad_moe = (RESIDUAL_SCALE * grad_result).astype(BF16)
    beside = jnp.concatenate([grad_moe, named], 2).reshape(home_rows, width + LANES)

    row_at = jnp.concatenate(
        [
            (rings.origin("x", s) * cn + rings.origin("c", t)) * rows
            + jnp.arange(rows, dtype=jnp.int32)
            for s in range(xn)
            for t in range(cn)
        ]
    )
    row_at, pack = tie(row_at, pack)
    half = HEAD_DIM // 2
    lane = jnp.arange(LANES, dtype=jnp.int32)
    inverse = ROPE_BASE ** (-((lane % half).astype(F32) * 2.0) / HEAD_DIM)
    sign = jnp.where(lane % HEAD_DIM < half, -1.0, 1.0)
    doc_lengths = lengths[:, 0]
    doc_ends = jnp.cumsum(doc_lengths, 1)
    doc_starts = doc_ends - doc_lengths
    segment = jnp.sum((row_at[None, :, None] >= doc_ends[:, None, :]).astype(jnp.int32), 2)
    docs = jnp.arange(doc_lengths.shape[1], dtype=jnp.int32)
    start = jnp.sum(jnp.where(segment[:, :, None] == docs, doc_starts[:, None, :], 0), 2)
    position = row_at[None, :] - start
    angles = position.astype(F32)[:, :, None] * inverse
    cosine, sine = jnp.cos(angles), jnp.sin(angles) * sign
    allowed = segment[:, :, None] == segment[:, None, :]
    bias = jnp.where(allowed & (row_at[None, :] <= row_at[:, None]), 0.0, NEGATIVE)

    waiting = {"beside": beside, "gate_up": gate_up, "down": w_down}
    tables = {"cosine": cosine, "sine": sine, "bias": bias}

    def weights_arrived(slot, value):
        if slot == 1:
            value, *tied = tie(value, *tables.values())
            tables.update(zip(list(tables), tied))
        if slot < zn - 1:
            return value
        names = list(waiting)
        tied = tie(value, *waiting.values())
        waiting.update(zip(names, tied[1:]))
        return tied[0]

    packs = rings.gather_two(pack, "z", "y", weights_arrived)
    spots = jnp.stack(
        [rings.origin("z", t) * yn + rings.origin("y", s) for s in range(yn) for t in range(zn)]
    )
    if whole:
        packs = [in_order(column, rings.at["z"], zn) for column in packs]
        packs = [in_order([packs[s][z] for s in range(yn)], rings.at["y"], yn) for z in range(zn)]
        packs = jnp.stack([packs[z][y] for z in range(zn) for y in range(yn)])
        w_merge = packs[:, :, small_at:].reshape(dp_count, members, weight_rows, merged_columns)
        w_merge = w_merge.transpose(0, 2, 1, 3).reshape(dp_count * weight_rows, width)
        w_small = packs[:, :, qkv_columns:small_at].reshape(width, LANES)
        packs = [packs[:, :, :qkv_columns].reshape(width, qkv_columns), w_merge, w_small]
    else:
        packs = [slot for column in packs for slot in column]

    beside = rings.gather_two(waiting["beside"], "z", "x")
    gate_up = lax.all_to_all(waiting["gate_up"], "dp", 0, 0, axis_index_groups=rings.z_groups)
    down = rings.gather(waiting["down"], "y")
    cosine, sine, bias = tables["cosine"], tables["sine"], tables["bias"]
    attn_parts, group_in, n1, router_columns, small_rows, qkv, merged, lse = attention_forward(
        attention_shape, spots, packs, group_tokens, cosine, sine, bias
    )
    gain_first = small_rows[experts_all]
    gain_second = small_rows[experts_all + 1]
    hidden = inputs + RESIDUAL_SCALE * sum_members(attn_parts)
    inv_second = lax.rsqrt(jnp.mean(hidden * hidden, -1, keepdims=True) + EPSILON)
    unit_second = hidden * inv_second
    normed_second = (unit_second * gain_second).astype(BF16).reshape(home_rows, width)
    def meeting(store, *names):
        def meet(value):
            value, *values = tie(value, *[store[name] for name in names])
            store.update(zip(names, values))
            return value

        return meet

    waiting = {"gate_up": gate_up, "down": down[-1]}

    def rows_arrived(slot, value):
        if slot == 1:
            value = meeting(waiting, "gate_up", "down")(value)
            waiting["parts"] = rings.gather(waiting["gate_up"], "y")[1:]
        if slot == zn - 1:
            value, *waiting["parts"] = tie(value, *waiting["parts"])
        return value

    group_x = rings.gather_two(normed_second, "z", "x", rows_arrived)

    gate_up = [rings.gather(part, "c") for part in [waiting["gate_up"]] + waiting["parts"]]
    down = [rings.gather(part, "c") for part in down[:-1] + [waiting["down"]]]
    gu_parts = [gate_up[s][c] for c in range(cn) for s in range(yn)]
    dn_parts = [down[s][c] for c in range(cn) for s in range(yn)]

    slots = [(s, t) for s in range(xn) for t in range(zn)]
    x_slots = [group_x[s][t] for s, t in slots]
    beside = [beside[s][t] for s, t in slots]
    chunk = min(len(slots), 8)
    chunks = len(slots) // chunk
    table = [
        (rings.at["x"] * cn + rings.origin("c", s)) * own_experts
        + jnp.arange(own_experts, dtype=jnp.int32)
        for s in range(cn)
    ]
    table.append(jnp.stack([rings.origin("y", s) for s in range(yn)]))
    goals = jnp.stack([rings.origin("z", t) * xn + rings.origin("x", s) for s, t in slots])
    table.append(goals if chunks == 1 else jnp.arange(chunk, dtype=jnp.int32))
    table = jnp.concatenate(table)
    experts_shape = {"cores": cn, "ys": yn, "zs": zn, "own": own_experts, "hidden": hidden_part}
    results = [
        run_experts(
            experts_shape,
            table,
            x_slots[i * chunk : (i + 1) * chunk],
            beside[i * chunk : (i + 1) * chunk],
            gu_parts,
            dn_parts,
            router_columns,
        )
        for i in range(chunks)
    ]
    if chunks == 1:
        results = list(results[0])
    else:
        results = [jnp.concatenate(pieces, 0) for pieces in zip(*results)]
    mixed, dx, gates, grad_gates, x_all, gm_all = results[:6]
    acts, dgus = results[6 : 6 + cn], results[6 + cn :]

    def to_owner(value, meet=None):
        parts = value.reshape(xn, zn, home_rows, width)
        parts = [[parts[s, t] for t in range(zn)] for s in range(xn)]
        return rings.reduce_two(parts, "z", "x", meet=meet)

    grad_gates = grad_gates.reshape(len(slots), home_rows, LANES)
    if chunks > 1:
        grad_gates = jnp.zeros_like(grad_gates).at[goals].set(grad_gates)
    grad_gates = lax.all_to_all(grad_gates, ALL, 0, 0, axis_index_groups=rings.token_groups)
    grad_gates = jnp.sum(grad_gates.astype(F32), 0)
    grad_gates = grad_gates[:, :half_lanes] + grad_gates[:, half_lanes:]
    def sum_cores(terms):
        running = None
        for slot in range(1, cn):
            term = terms(slot)
            running = rings.step((term if running is None else term + running).astype(BF16), "c")
            running = running.astype(F32)
        own = terms(0)
        return (own if running is None else own + running).astype(BF16)

    grad_gu = sum_cores(lambda s: dot(x_all, dgus[s], ((0,), (0,))))
    grad_dn = sum_cores(lambda s: dot(acts[s], gm_all, ((0,), (0,))))
    wide = own_experts * 2 * hidden_part
    grad_gu = grad_gu.reshape(zn, yn, model_part, wide)
    grad_gu = [lax.dynamic_index_in_dim(grad_gu, rings.origin("y", s), 1, False) for s in range(yn)]
    grad_dn = grad_dn.reshape(own_experts, yn, hidden_part // yn, width)
    grad_dn = [lax.dynamic_index_in_dim(grad_dn, rings.origin("y", s), 1, False) for s in range(yn)]
    waiting = {"mixed": mixed, "weights": grad_gu + grad_dn}

    def rows_sent(ring, slot, value):
        if ring == "x" and slot == 0:
            value = meeting(waiting, "mixed")(value)
        if ring == "z" and slot == min(2, zn - 1):
            value, *waiting["weights"] = tie(value, *waiting["weights"])
        return value

    grad_dealt = to_owner(dx, rows_sent)
    grad_gu, grad_dn = waiting["weights"][:yn], waiting["weights"][yn:]
    own_gates = gates[:home_rows, :half_lanes]
    grad_picked = own_gates * (grad_gates - jnp.sum(own_gates * grad_gates, -1, keepdims=True))
    grad_logits = grad_picked.astype(BF16)
    grad_dealt = (grad_dealt + dot(grad_logits, small_rows.astype(BF16))).astype(BF16)
    grad_normed_second = grad_dealt.astype(F32).reshape(micros, rows, width)
    scaled_second = grad_normed_second * gain_second
    grad_hidden = grad_result + inv_second * (
        scaled_second - unit_second * jnp.mean(scaled_second * unit_second, -1, keepdims=True)
    )
    mlp_gain_grad = jnp.sum(grad_normed_second * unit_second, (0, 1))[None]
    grad_attn = (RESIDUAL_SCALE * grad_hidden).astype(BF16)

    grad_attn = over_members(grad_attn)
    moe_rows = to_owner(waiting["mixed"]).astype(BF16).reshape(micros, rows, width)
    grad_attn[-1], moe_rows = tie(grad_attn[-1], moe_rows)
    output = (hidden + RESIDUAL_SCALE * moe_rows.astype(F32)).astype(BF16)

    first_parts, weight_grads = attention_backward(
        attention_shape,
        spots,
        packs,
        grad_attn,
        [cosine, sine, bias, qkv, lse, group_in],
        [n1, merged, normed_second, jnp.pad(grad_logits, ((0, 0), (0, half_lanes))), mlp_gain_grad],
    )
    grad_normed_first = sum_members(first_parts)
    scaled_first = grad_normed_first * gain_first
    grad_tokens = grad_hidden + inv_first * (
        scaled_first - unit_first * jnp.mean(scaled_first * unit_first, -1, keepdims=True)
    )

    waiting = {"weights": weight_grads}

    def experts_sent(slot, value):
        value, *waiting["weights"] = tie(value, *waiting["weights"])
        return value

    grad_gu = rings.reduce(grad_gu, "y", meet=experts_sent).astype(BF16)
    grad_dn = rings.reduce(grad_dn, "y", meet=experts_sent)
    grad_gu = lax.all_to_all(grad_gu, "dp", 0, 0, axis_index_groups=rings.z_groups)
    weight_grads = waiting["weights"]

    if whole:
        grad_qkv, grad_out, grad_small = weight_grads
        grad_out = grad_out.reshape(dp_count, weight_rows, members, merged_columns).transpose(0, 2, 1, 3)
        both = jnp.concatenate(
            [
                grad_qkv.reshape(dp_count, pack_rows, qkv_columns),
                grad_small.reshape(dp_count, pack_rows, LANES),
                grad_out.reshape(dp_count, pack_rows, merged_columns),
            ],
            2,
        )
        weight_grads = [
            lax.dynamic_index_in_dim(both, spots[i], 0, False) for i in range(dp_count)
        ]
    both = rings.reduce_two(
        [[weight_grads[s * zn + t] for t in range(zn)] for s in range(yn)], "z", "y"
    )
    both, grad_gu = tie(both, grad_gu)
    grad_gate, grad_up = unpack_experts(grad_gu, own_experts)
    grad_out = [
        both[i * weight_rows : (i + 1) * weight_rows, small_at:] for i in range(members)
    ]
    grad_out = lax.ppermute(jnp.concatenate(grad_out, 1), ALL, to_home)
    home = both[:, :small_at].reshape(members, weight_rows, small_at)
    home = lax.all_to_all(home, "expert", 0, 0)

    def columns(start, count):
        return jnp.concatenate([home[i, :, start : start + count] for i in range(members)], 1)

    query_columns, key_columns = heads * HEAD_DIM, kv_heads * HEAD_DIM
    grad_query = columns(0, query_columns)
    grad_key = columns(query_columns, key_columns)
    grad_value = columns(query_columns + key_columns, key_columns)

    small = jnp.sum(home[:, :, qkv_columns:], 0)
    grad_w_router = small[:, :experts_all]
    grad_attn_gain, grad_mlp_gain = small[:, experts_all], small[:, experts_all + 1]

    return (
        output,
        grad_tokens,
        grad_attn_gain,
        grad_mlp_gain,
        grad_query,
        grad_key,
        grad_value,
        grad_out,
        grad_w_router,
        grad_gate,
        grad_up,
        grad_dn,
    )


def solution(mesh):
    rows = P(None, ALL, None)
    placed = (rows, rows, P(ALL), P(ALL)) + (P(ALL, None),) * 5
    placed += (P("expert", "dp", None),) * 3 + (rows, rows, P(None, "dp", None))
    results = (rows, rows, P(ALL), P(ALL)) + (P(ALL, None),) * 5
    results += (P("expert", "dp", None),) * 3
    return jax.shard_map(per_device, mesh=mesh, in_specs=placed, out_specs=results, check_vma=False)
```

time: 679 us -> 537 us (0.79)
  local copies, waits for them, and re-layouts: 122 us -> 24.9 us
  starting transfers between devices: 134 us -> 91.3 us
  other arithmetic: 79.6 us -> 40.1 us
  waiting for transfers between devices: 242 us -> 263 us
  Pallas kernels: 66.1 us -> 83.1 us
    ppermute x65 -> x64, waiting for transfers between devices: 204 us -> 252 us  [step(): return lax.ppermute(value, axis, pairs)]
    slice x14 -> x5, local copies, waits for them, and re-layouts: 38.6 us -> 4.89 us  [the longest x1 1.92 us: per_device(): home = both[:, :small_at].reshape(members, weight_rows, small_at)]
    ppermute x65 -> x64, starting transfers between devices: 89.6 us -> 57.3 us  [step(): return lax.ppermute(value, axis, pairs)]
    reshape x10 -> x0, local copies, waits for them, and re-layouts: 25.8 us -> none  [the longest x1 17 us: per_device(): grad_gu = grad_gu.reshape(width, cn, own_experts * 2 * hidden_part)]
    unnamed x122 -> x103, local copies, waits for them, and re-layouts: 29.5 us -> 7.51 us
    ppermute x1, waiting for transfers between devices: 26 us -> 8.59 us  [per_device(): grad_out = lax.ppermute(jnp.concatenate(grad_out, 1), ALL, to_home)]
    pallas_call x3 -> x5, Pallas kernels: 66.1 us -> 83.1 us  [the longest x1 41 us: run_experts(): pl.pallas_call(functools.partial(experts_kernel, shape), in_specs=[pl.Blo...]
    concatenate x10 -> x7, other arithmetic: 18.4 us -> 3.61 us  [the longest x3 2.03 us: columns(): jnp.concatenate([home[i, :, start:start + count] for i in range(members)]...]
  transfers between devices with their start and end apart: 75 -> 72, of which waited for: 26 -> 38; matrix products, arithmetic and copies ran while one was open for 29% -> 14% of each run, Pallas kernels for 3% -> 8%
where the time goes in v2:
time: 537 us; the launch traced here: 529 us
  waiting for transfers between devices  263 us (49%)
  starting transfers between devices  91.3 us (17%)
  Pallas kernels  83.1 us (15%)
  other arithmetic  40.1 us (7%)
  local copies, waits for them, and re-layouts  24.9 us (5%)
  matrix products  23.9 us (4%)
    ppermute x64, waiting for transfers between devices, step(): return lax.ppermute(value, axis, pairs)  252 us
    ppermute x64, starting transfers between devices, step(): return lax.ppermute(value, axis, pairs)  57.3 us
    pallas_call x1, Pallas kernels, run_experts(): pl.pallas_call(functools.partial(experts_kernel, shape), in_specs=[pl.Blo...  41 us
    dot_general x5, matrix products, dot(): return lax.dot_general(a, b, (dims, ((), ())), preferred_element_type=F32)  23.8 us
    pallas_call x1, Pallas kernels, attention_backward(): pl.pallas_call(functools.partial(attention_backward_kernel, shape), grid_...  19.2 us
    pallas_call x1, Pallas kernels, attention_forward(): pl.pallas_call(functools.partial(attention_forward_kernel, shape), grid_s...  13.5 us
    convert_element_type x11, other arithmetic, reduce_two(): running = self.step(term.astype(wire), first)  12.4 us
  transfers between devices with their start and end apart: 72, of which 38 were waited for; matrix products, arithmetic and copies ran while one was open for 14% of the time, Pallas kernels for 8%

profile of v2, /device:TPU:4, one launch (start us, length us, event | category | flops | bytes accessed | tf_op | source)
XLA Modules:
  0.0 528.7 jit_solution(5403642296828121210)
XLA Ops:
  38.7 8.2 %collective-permute-done.4.refs_5_ = bf16[192,1152]{1,0:T(8,128)(2,1)S(1)} collective-permute-done((bf16[192,1152]{1,0:T(8,128)(2,1)S(1)}, bf16[192,1152]{1,0:T(8,128)(2,1)S(1)}, u32[]{:S(2)}, u32[]{:S(2)}) %collective-permute-start.4) | collective-permute-done | bytes 442400 | tf_op jit(solution)/shard_map/ppermute | solution.py:67
  52.1 9.7 %collective-permute-done.6.refs_6_ = bf16[192,1152]{1,0:T(8,128)(2,1)S(1)} collective-permute-done((bf16[192,1152]{1,0:T(8,128)(2,1)S(1)}, bf16[192,1152]{1,0:T(8,128)(2,1)S(1)}, u32[]{:S(2)}, u32[]{:S(2)}) %collective-permute-start.6) | collective-permute-done | bytes 442400 | tf_op jit(solution)/shard_map/ppermute | solution.py:67
  76.7 13.5 %attention_forward.1 = (bf16[2,64,1536]{2,1,0:T(8,128)(2,1)}, bf16[2,64,1536]{2,1,0:T(8,128)(2,1)}, bf16[2,64,1536]{2,1,0:T(8,128)(2,1)}, bf16[2,64,1536]{2,1,0:...) custom-call(s32[8]{0:T(128)} %stack.65.spots_ref, ...), custom_call_target="tpu_custom_call" | custom-call | tf_op jit(solution)/shard_map/attention_forward/pallas_call | solution.py:384
  95.4 9.2 %collective-permute-done.13 = bf16[2,64,1536]{2,1,0:T(8,128)(2,1)S(1)} collective-permute-done((bf16[2,64,1536]{2,1,0:T(8,128)(2,1)S(1)}, bf16[2,64,1536]{2,1,0:T(8,128)(2,1)S(1)}, u32[]{:S(2)}, u32[]{:S(2)}) %collective-permute-start.13) | collective-permute-done | bytes 393248 | tf_op jit(solution)/shard_map/ppermute | solution.py:67
  106.5 10.1 %collective-permute-done.15.refs_4_ = bf16[128,1536]{1,0:T(8,128)(2,1)S(1)} collective-permute-done((bf16[128,1536]{1,0:T(8,128)(2,1)S(1)}, bf16[128,1536]{1,0:T(8,128)(2,1)S(1)}, u32[]{:S(2)}, u32[]{:S(2)}) %collective-permute-start.15) | collective-permute-done | bytes 393248 | tf_op jit(solution)/shard_map/ppermute | solution.py:67
  125.8 8.3 %collective-permute-done.18.refs_5_ = bf16[128,1536]{1,0:T(8,128)(2,1)S(1)} collective-permute-done((bf16[128,1536]{1,0:T(8,128)(2,1)}, bf16[128,1536]{1,0:T(8,128)(2,1)S(1)}, u32[]{:S(2)}, u32[]{:S(2)}) %collective-permute-start.18) | collective-permute-done | bytes 393248 | tf_op jit(solution)/shard_map/ppermute | solution.py:67
  139.3 10.0 %collective-permute-done.20.refs_6_ = bf16[128,1536]{1,0:T(8,128)(2,1)S(1)} collective-permute-done((bf16[128,1536]{1,0:T(8,128)(2,1)S(1)}, bf16[128,1536]{1,0:T(8,128)(2,1)S(1)}, u32[]{:S(2)}, u32[]{:S(2)}) %collective-permute-start.20) | collective-permute-done | bytes 393248 | tf_op jit(solution)/shard_map/ppermute | solution.py:67
  151.5 15.0 %collective-permute-done.21.refs_17_ = bf16[4,192,1280]{2,1,0:T(8,128)(2,1)} collective-permute-done((bf16[4,192,1280]{2,1,0:T(8,128)(2,1)S(1)}, bf16[4,192,1280]{2,1,0:T(8,128)(2,1)}, u32[]{:S(2)}, u32[]{:S(2)}) %collective-permute-start.21) | collective-permute-done | bytes 1966112 | tf_op jit(solution)/shard_map/ppermute | solution.py:67
  168.5 10.3 %collective-permute-done.26.refs_13_ = bf16[128,1664]{1,0:T(8,128)(2,1)S(1)} collective-permute-done((bf16[128,1664]{1,0:T(8,128)(2,1)S(1)}, bf16[128,1664]{1,0:T(8,128)(2,1)S(1)}, u32[]{:S(2)}, u32[]{:S(2)}) %collective-permute-start.26) | collective-permute-done | bytes 426016 | tf_op jit(solution)/shard_map/ppermute | solution.py:67
  183.0 10.2 %collective-permute-done.28.refs_14_ = bf16[128,1664]{1,0:T(8,128)(2,1)S(1)} collective-permute-done((bf16[128,1664]{1,0:T(8,128)(2,1)S(1)}, bf16[128,1664]{1,0:T(8,128)(2,1)S(1)}, u32[]{:S(2)}, u32[]{:S(2)}) %collective-permute-start.28) | collective-permute-done | bytes 426016 | tf_op jit(solution)/shard_map/ppermute | solution.py:67
  193.4 12.1 %collective-permute-done.27.refs_11_ = bf16[128,1664]{1,0:T(8,128)(2,1)} collective-permute-done((bf16[128,1664]{1,0:T(8,128)(2,1)S(1)}, bf16[128,1664]{1,0:T(8,128)(2,1)}, u32[]{:S(2)}, u32[]{:S(2)}) %collective-permute-start.27) | collective-permute-done | bytes 426016 | tf_op jit(solution)/shard_map/ppermute | solution.py:67
  208.1 10.4 %collective-permute-done.29.refs_15_ = bf16[128,1664]{1,0:T(8,128)(2,1)} collective-permute-done((bf16[128,1664]{1,0:T(8,128)(2,1)}, bf16[128,1664]{1,0:T(8,128)(2,1)}, u32[]{:S(2)}, u32[]{:S(2)}) %collective-permute-start.29) | collective-permute-done | bytes 426016 | tf_op jit(solution)/shard_map/ppermute | solution.py:67
  223.7 41.0 %experts.1 = (bf16[1024,1536]{1,0:T(8,128)(2,1)}, bf16[1024,1536]{1,0:T(8,128)(2,1)}, f32[1024,128]{1,0:T(8,128)}, bf16[1024,128]{1,0:T(8,128)(2,1)}, bf16[1024,...) custom-call(s32[20]{0:T(128)} %concatenate.39.table_ref, ...), custom_call_target="tpu_custom_call" | custom-call | tf_op jit(solution)/shard_map/experts/pallas_call | solution.py:546
  270.5 7.8 %convolution_convert_fusion = bf16[1536,1280]{1,0:T(8,128)(2,1)} fusion(bf16[1024,1536]{1,0:T(8,128)(2,1)S(1)} %copy-done.45, bf16[1024,1280]{1,0:T(8,128)(2,1)} %get-tuple-element.183), kind=kOutput, calls=%fused_computation.1 | convolution fusion | flops 4028497920 | bytes 9699328 | tf_op jit(solution)/shard_map/dot_general | solution.py:27
  282.3 13.0 %collective-permute-done.35 = bf16[128,1536]{1,0:T(8,128)(2,1)S(1)} collective-permute-done((bf16[128,1536]{1,0:T(8,128)(2,1)S(1)}, bf16[128,1536]{1,0:T(8,128)(2,1)S(1)}, u32[]{:S(2)}, u32[]{:S(2)}) %collective-permute-start.35) | collective-permute-done | bytes 393248 | tf_op jit(solution)/shard_map/ppermute | solution.py:67
  299.3 8.5 %collective-permute-done.36 = bf16[128,1536]{1,0:T(8,128)(2,1)S(1)} collective-permute-done((bf16[128,1536]{1,0:T(8,128)(2,1)S(1)}, bf16[128,1536]{1,0:T(8,128)(2,1)S(1)}, u32[]{:S(2)}, u32[]{:S(2)}) %collective-permute-start.36) | collective-permute-done | bytes 393248 | tf_op jit(solution)/shard_map/ppermute | solution.py:67
  317.9 8.5 %collective-permute-done.38 = bf16[128,1536]{1,0:T(8,128)(2,1)S(1)} collective-permute-done((bf16[128,1536]{1,0:T(8,128)(2,1)S(1)}, bf16[128,1536]{1,0:T(8,128)(2,1)S(1)}, u32[]{:S(2)}, u32[]{:S(2)}) %collective-permute-start.38) | collective-permute-done | bytes 393248 | tf_op jit(solution)/shard_map/ppermute | solution.py:67
  386.5 19.2 %attention_backward.1 = (bf16[2,64,1536]{2,1,0:T(8,128)(2,1)}, bf16[2,64,1536]{2,1,0:T(8,128)(2,1)}, bf16[2,64,1536]{2,1,0:T(8,128)(2,1)}, bf16[2,64,1536]{2,1,0...) custom-call(s32[8]{0:T(128)} %stack.65.spots_ref, ...), custom_call_target="tpu_custom_call" | custom-call | tf_op jit(solution)/shard_map/attention_backward/pallas_call | solution.py:410
  406.3 12.0 %collective-permute-done.57 = bf16[4,192,1280]{2,1,0:T(8,128)(2,1)} collective-permute-done((bf16[4,192,1280]{2,1,0:T(8,128)(2,1)}, bf16[4,192,1280]{2,1,0:T(8,128)(2,1)}, u32[]{:S(2)}, u32[]{:S(2)}) %collective-permute-start.57) | collective-permute-done | bytes 1966112 | tf_op jit(solution)/shard_map/ppermute | solution.py:67
  422.9 7.7 %all-to-all-start.4 = ((bf16[4,192,1280]{2,1,0:T(8,128)(2,1)}), bf16[4,192,1280]{2,1,0:T(8,128)(2,1)S(1)}, u32[]{:S(2)}, u32[]{:S(2)}) async-start(bf16[4,192,1280]{2,1,0:T(8,128)(2,1)} %add_convert_fusion), calls=%async_computation.4 | async-start | bytes 3932160 | tf_op jit(solution)/shard_map/all_to_all | solution.py:895
  437.7 11.0 %collective-permute-done.61 = bf16[192,1152]{1,0:T(8,128)(2,1)S(1)} collective-permute-done((bf16[192,1152]{1,0:T(8,128)(2,1)}, bf16[192,1152]{1,0:T(8,128)(2,1)S(1)}, u32[]{:S(2)}, u32[]{:S(2)}) %collective-permute-start.61) | collective-permute-done | bytes 442400 | tf_op jit(solution)/shard_map/ppermute | solution.py:67
  449.3 15.7 %collective-permute-done.60 = bf16[192,1152]{1,0:T(8,128)(2,1)S(1)} collective-permute-done((bf16[192,1152]{1,0:T(8,128)(2,1)S(1)}, bf16[192,1152]{1,0:T(8,128)(2,1)S(1)}, u32[]{:S(2)}, u32[]{:S(2)}) %collective-permute-start.60) | collective-permute-done | bytes 442400 | tf_op jit(solution)/shard_map/ppermute | solution.py:67
  474.0 8.9 %collective-permute-done.62 = bf16[192,1152]{1,0:T(8,128)(2,1)S(1)} collective-permute-done((bf16[192,1152]{1,0:T(8,128)(2,1)S(1)}, bf16[192,1152]{1,0:T(8,128)(2,1)S(1)}, u32[]{:S(2)}, u32[]{:S(2)}) %collective-permute-start.62) | collective-permute-done | bytes 442400 | tf_op jit(solution)/shard_map/ppermute | solution.py:67
  512.7 8.6 %collective-permute-done.65 = f32[48,1536]{1,0:T(8,128)S(1)} collective-permute-done((f32[48,1536]{1,0:T(8,128)}, f32[48,1536]{1,0:T(8,128)S(1)}, u32[]{:S(2)}, u32[]{:S(2)}) %collective-permute-start.65) | collective-permute-done | bytes 294944 | tf_op jit(solution)/shard_map/ppermute | solution.py:920
  (307 shorter events, 237.7 us)
Async XLA Ops:
  0.7 64.8 %collective-permute-start.8 = (bf16[2,64,1536]{2,1,0:T(8,128)(2,1)}, bf16[2,64,1536]{2,1,0:T(8,128)(2,1)}, u32[]{:S(2)}, u32[]{:S(2)}) collective-permute-start(bf16[2,64,1536]{2,1,0:T(8,128)(2,1)} %refs_8_.1), channel_id=1, source_target_pairs={{0,1},{1,0},{2,3},{3,2},{4,5},{5,4},{6,7},{7,6},{8,9},{9,8},{10,11... | collective-permute-start | bytes 1179656 | tf_op jit(solution)/shard_map/ppermute | solution.py:67
  0.7 64.7 %collective-permute-start.9 = (bf16[2,64,1536]{2,1,0:T(8,128)(2,1)}, bf16[2,64,1536]{2,1,0:T(8,128)(2,1)S(1)}, u32[]{:S(2)}, u32[]{:S(2)}) collective-permute-start(bf16[2,64,1536]{2,1,0:T(8,128)(2,1)} %refs_8_.1), channel_id=1, source_target_pairs={{0,2},{1,3},{2,0},{3,1},{4,6},{5,7},{6,4},{7,5},{8,10},{9,11},{10,... | collective-permute-start | bytes 1179656 | tf_op jit(solution)/shard_map/ppermute | solution.py:67
  65.5 57.1 %all-to-all-start.2 = ((bf16[4,192,1280]{2,1,0:T(8,128)(2,1)}), bf16[4,192,1280]{2,1,0:T(8,128)(2,1)S(1)}, u32[]{:S(2)}, u32[]{:S(2)}) async-start(bf16[4,192,1280]{2,1,0:T(8,128)(2,1)} %pack_experts.1), calls=%async_computation.2 | async-start | bytes 3932160 | tf_op jit(solution)/shard_map/all_to_all | solution.py:747
  122.6 43.9 %collective-permute-start.21 = (bf16[4,192,1280]{2,1,0:T(8,128)(2,1)S(1)}, bf16[4,192,1280]{2,1,0:T(8,128)(2,1)}, u32[]{:S(2)}, u32[]{:S(2)}) collective-permute-start(bf16[4,192,1280]{2,1,0:T(8,128)(2,1)S(1)} %all-to-all-done.2.refs_16_), channel_id=1, source_target_pairs={{0,4},{4,0},{8,12},{12,8},{16,20},{20,16},{24,28},{28,24},{1,5},{5... | collective-permute-start | bytes 5898248 | tf_op jit(solution)/shard_map/ppermute | solution.py:67
  137.6 28.9 %collective-permute-start.24 = (bf16[128,1664]{1,0:T(8,128)(2,1)}, bf16[128,1664]{1,0:T(8,128)(2,1)}, u32[]{:S(2)}, u32[]{:S(2)}) collective-permute-start(bf16[128,1664]{1,0:T(8,128)(2,1)} %bitcast.181), channel_id=1, source_target_pairs={{0,2},{1,3},{2,0},{3,1},{4,6},{5,7},{6,4},{7,5},{8,10},{9,11},{10,... | collective-permute-start | bytes 1277960 | tf_op jit(solution)/shard_map/ppermute | solution.py:67
  139.3 27.2 %collective-permute-start.23 = (bf16[128,1664]{1,0:T(8,128)(2,1)}, bf16[128,1664]{1,0:T(8,128)(2,1)S(1)}, u32[]{:S(2)}, u32[]{:S(2)}) collective-permute-start(bf16[128,1664]{1,0:T(8,128)(2,1)} %bitcast.182), channel_id=1, source_target_pairs={{0,8},{4,12},{8,16},{12,20},{16,24},{20,28},{24,0},{28,4},{1,9},{5... | collective-permute-start | bytes 1277960 | tf_op jit(solution)/shard_map/ppermute | solution.py:67
  149.3 69.2 %collective-permute-start.30 = (bf16[4,192,1280]{2,1,0:T(8,128)(2,1)S(1)}, bf16[4,192,1280]{2,1,0:T(8,128)(2,1)}, u32[]{:S(2)}, u32[]{:S(2)}) collective-permute-start(bf16[4,192,1280]{2,1,0:T(8,128)(2,1)S(1)} %all-to-all-done.2.refs_16_), channel_id=1, source_target_pairs={{0,1},{1,0},{2,3},{3,2},{4,5},{5,4},{6,7},{7,6},{8,9},{9,8},{10,11... | collective-permute-start | bytes 5898248 | tf_op jit(solution)/shard_map/ppermute | solution.py:67
  166.5 57.2 %collective-permute-start.31 = (bf16[4,192,1280]{2,1,0:T(8,128)(2,1)}, bf16[4,192,1280]{2,1,0:T(8,128)(2,1)}, u32[]{:S(2)}, u32[]{:S(2)}) collective-permute-start(bf16[4,192,1280]{2,1,0:T(8,128)(2,1)} %collective-permute-done.21.refs_17_), channel_id=1, source_target_pairs={{0,1},{1,0},{2,3},{3,2},{4,5},{5,4},{6,7},{7,6},{8,9},{9,8},{10,11... | collective-permute-start | bytes 5898248 | tf_op jit(solution)/shard_map/ppermute | solution.py:67
  168.3 38.8 %collective-permute-start.32 = (bf16[5,64,1536]{2,1,0:T(8,128)(2,1)}, bf16[5,64,1536]{2,1,0:T(8,128)(2,1)}, u32[]{:S(2)}, u32[]{:S(2)}) collective-permute-start(bf16[5,64,1536]{2,1,0:T(8,128)(2,1)} %refs_20_), channel_id=1, source_target_pairs={{0,1},{1,0},{2,3},{3,2},{4,5},{5,4},{6,7},{7,6},{8,9},{9,8},{10,11... | collective-permute-start | bytes 2949128 | tf_op jit(solution)/shard_map/ppermute | solution.py:67
  183.0 35.5 %collective-permute-start.33 = (bf16[5,64,1536]{2,1,0:T(8,128)(2,1)}, bf16[5,64,1536]{2,1,0:T(8,128)(2,1)}, u32[]{:S(2)}, u32[]{:S(2)}) collective-permute-start(bf16[5,64,1536]{2,1,0:T(8,128)(2,1)} %collective-permute-done.16.refs_21_), channel_id=1, source_target_pairs={{0,1},{1,0},{2,3},{3,2},{4,5},{5,4},{6,7},{7,6},{8,9},{9,8},{10,11... | collective-permute-start | bytes 2949128 | tf_op jit(solution)/shard_map/ppermute | solution.py:67
  268.1 29.4 %collective-permute-start.37 = (bf16[128,1536]{1,0:T(8,128)(2,1)S(1)}, bf16[128,1536]{1,0:T(8,128)(2,1)S(1)}, u32[]{:S(2)}, u32[]{:S(2)}) collective-permute-start(bf16[128,1536]{1,0:T(8,128)(2,1)S(1)} %get-tuple-element.297), channel_id=1, source_target_pairs={{0,2},{1,3},{2,0},{3,1},{4,6},{5,7},{6,4},{7,5},{8,10},{9,11},{10,... | collective-permute-start | bytes 1179656 | tf_op jit(solution)/shard_map/ppermute | solution.py:67
  270.2 40.9 %collective-permute-start.34 = (bf16[128,1536]{1,0:T(8,128)(2,1)S(1)}, bf16[128,1536]{1,0:T(8,128)(2,1)S(1)}, u32[]{:S(2)}, u32[]{:S(2)}) collective-permute-start(bf16[128,1536]{1,0:T(8,128)(2,1)S(1)} %get-tuple-element.299), channel_id=1, source_target_pairs={{0,2},{1,3},{2,0},{3,1},{4,6},{5,7},{6,4},{7,5},{8,10},{9,11},{10,... | collective-permute-start | bytes 1179656 | tf_op jit(solution)/shard_map/ppermute | solution.py:67
  278.2 65.0 %collective-permute-start.40 = (bf16[1536,1280]{1,0:T(8,128)(2,1)}, bf16[1536,1280]{1,0:T(8,128)(2,1)}, u32[]{:S(2)}, u32[]{:S(2)}) collective-permute-start(bf16[1536,1280]{1,0:T(8,128)(2,1)} %convolution_convert_fusion), channel_id=1, source_target_pairs={{0,1},{1,0},{2,3},{3,2},{4,5},{5,4},{6,7},{7,6},{8,9},{9,8},{10,11... | collective-permute-start | bytes 11796488 | tf_op jit(solution)/shard_map/ppermute | solution.py:67
  281.8 55.4 %collective-permute-start.41 = (bf16[640,1536]{1,0:T(8,128)(2,1)}, bf16[640,1536]{1,0:T(8,128)(2,1)S(1)}, u32[]{:S(2)}, u32[]{:S(2)}) collective-permute-start(bf16[640,1536]{1,0:T(8,128)(2,1)} %convolution_convert_fusion.1), channel_id=1, source_target_pairs={{0,1},{1,0},{2,3},{3,2},{4,5},{5,4},{6,7},{7,6},{8,9},{9,8},{10,11... | collective-permute-start | bytes 5898248 | tf_op jit(solution)/shard_map/ppermute | solution.py:67
  297.6 33.0 %collective-permute-start.49 = (bf16[128,1536]{1,0:T(8,128)(2,1)}, bf16[128,1536]{1,0:T(8,128)(2,1)}, u32[]{:S(2)}, u32[]{:S(2)}) collective-permute-start(bf16[128,1536]{1,0:T(8,128)(2,1)} %get-tuple-element.293), channel_id=1, source_target_pairs={{0,2},{1,3},{2,0},{3,1},{4,6},{5,7},{6,4},{7,5},{8,10},{9,11},{10,... | collective-permute-start | bytes 1179656 | tf_op jit(solution)/shard_map/ppermute | solution.py:67
  327.1 27.4 %all-to-all-start.3 = ((bf16[8,128,128]{2,1,0:T(8,128)(2,1)}), bf16[8,128,128]{2,1,0:T(8,128)(2,1)S(1)}, u32[]{:S(2)}, u32[]{:S(2)}) async-start(bf16[8,128,128]{2,1,0:T(8,128)(2,1)} %bitcast.188), calls=%async_computation.3 | async-start | bytes 524288 | tf_op jit(solution)/shard_map/all_to_all | solution.py:826
  356.6 61.6 %collective-permute-start.56 = (bf16[5,64,1536]{2,1,0:T(8,128)(2,1)}, bf16[5,64,1536]{2,1,0:T(8,128)(2,1)}, u32[]{:S(2)}, u32[]{:S(2)}) collective-permute-start(bf16[5,64,1536]{2,1,0:T(8,128)(2,1)} %get-tuple-element.208), channel_id=1, source_target_pairs={{0,4},{4,0},{8,12},{12,8},{16,20},{20,16},{24,28},{28,24},{1,5},{5... | collective-permute-start | bytes 2949128 | tf_op jit(solution)/shard_map/ppermute | solution.py:67
  358.1 60.1 %collective-permute-start.57 = (bf16[4,192,1280]{2,1,0:T(8,128)(2,1)}, bf16[4,192,1280]{2,1,0:T(8,128)(2,1)}, u32[]{:S(2)}, u32[]{:S(2)}) collective-permute-start(bf16[4,192,1280]{2,1,0:T(8,128)(2,1)} %get-tuple-element.209), channel_id=1, source_target_pairs={{0,4},{4,0},{8,12},{12,8},{16,20},{20,16},{24,28},{28,24},{1,5},{5... | collective-permute-start | bytes 5898248 | tf_op jit(solution)/shard_map/ppermute | solution.py:67
  405.7 66.9 %collective-permute-start.53 = (bf16[2,64,1536]{2,1,0:T(8,128)(2,1)}, bf16[2,64,1536]{2,1,0:T(8,128)(2,1)}, u32[]{:S(2)}, u32[]{:S(2)}) collective-permute-start(bf16[2,64,1536]{2,1,0:T(8,128)(2,1)} %get-tuple-element.205), channel_id=1, source_target_pairs={{0,1},{1,0},{2,3},{3,2},{4,5},{5,4},{6,7},{7,6},{8,9},{9,8},{10,11... | collective-permute-start | bytes 1179656 | tf_op jit(solution)/shard_map/ppermute | solution.py:67
  405.8 30.3 %collective-permute-start.54 = (bf16[2,64,1536]{2,1,0:T(8,128)(2,1)}, bf16[2,64,1536]{2,1,0:T(8,128)(2,1)}, u32[]{:S(2)}, u32[]{:S(2)}) collective-permute-start(bf16[2,64,1536]{2,1,0:T(8,128)(2,1)} %get-tuple-element.207), channel_id=1, source_target_pairs={{0,1},{1,0},{2,3},{3,2},{4,5},{5,4},{6,7},{7,6},{8,9},{9,8},{10,11... | collective-permute-start | bytes 1179656 | tf_op jit(solution)/shard_map/ppermute | solution.py:67
  422.9 71.5 %all-to-all-start.4 = ((bf16[4,192,1280]{2,1,0:T(8,128)(2,1)}), bf16[4,192,1280]{2,1,0:T(8,128)(2,1)S(1)}, u32[]{:S(2)}, u32[]{:S(2)}) async-start(bf16[4,192,1280]{2,1,0:T(8,128)(2,1)} %add_convert_fusion), calls=%async_computation.4 | async-start | bytes 3932160 | tf_op jit(solution)/shard_map/all_to_all | solution.py:895
  430.7 34.3 %collective-permute-start.58 = (bf16[192,1152]{1,0:T(8,128)(2,1)}, bf16[192,1152]{1,0:T(8,128)(2,1)S(1)}, u32[]{:S(2)}, u32[]{:S(2)}) collective-permute-start(bf16[192,1152]{1,0:T(8,128)(2,1)} %get-tuple-element.228), channel_id=1, source_target_pairs={{0,4},{4,0},{8,12},{12,8},{16,20},{20,16},{24,28},{28,24},{1,5},{5... | collective-permute-start | bytes 1327112 | tf_op jit(solution)/shard_map/ppermute | solution.py:67
  434.0 31.0 %collective-permute-start.60 = (bf16[192,1152]{1,0:T(8,128)(2,1)S(1)}, bf16[192,1152]{1,0:T(8,128)(2,1)S(1)}, u32[]{:S(2)}, u32[]{:S(2)}) collective-permute-start(bf16[192,1152]{1,0:T(8,128)(2,1)S(1)} %add_convert_fusion.4), channel_id=1, source_target_pairs={{0,8},{4,12},{8,16},{12,20},{16,24},{20,28},{24,0},{28,4},{1,9},{5... | collective-permute-start | bytes 1327112 | tf_op jit(solution)/shard_map/ppermute | solution.py:67
  437.3 35.3 %collective-permute-start.55 = (bf16[2,64,1536]{2,1,0:T(8,128)(2,1)S(1)}, bf16[2,64,1536]{2,1,0:T(8,128)(2,1)S(1)}, u32[]{:S(2)}, u32[]{:S(2)}) collective-permute-start(bf16[2,64,1536]{2,1,0:T(8,128)(2,1)S(1)} %add_convert_fusion.5), channel_id=1, source_target_pairs={{0,2},{1,3},{2,0},{3,1},{4,6},{5,7},{6,4},{7,5},{8,10},{9,11},{10,... | collective-permute-start | bytes 1179656 | tf_op jit(solution)/shard_map/ppermute | solution.py:67
  (97 other events, 1676.6 us)

commit v3 on v2

--- a/solution.py
+++ b/solution.py
@@ -69,67 +69,147 @@
     def origin(self, ring, slot):
         return lax.rem(self.at[ring] + (self.count(ring) - slot), self.count(ring))
 
-    def gather(self, value, ring, meet=None):
+    def gather(self, value, ring):
         slots = [value]
-        for s in range(1, self.count(ring)):
-            arrived = self.step(slots[-1], ring)
-            slots.append(arrived if meet is None else meet(s, arrived))
+        for _ in range(1, self.count(ring)):
+            slots.append(self.step(slots[-1], ring))
         return slots
 
-    def reduce(self, parts, ring, wire=BF16, meet=None):
+    def send(self, terms, ring, wire=None):
         running = None
-        for slot in range(1, self.count(ring)):
-            term = parts[slot]
-            if running is not None:
+        for term in terms[1:]:
+            if running is None:
+                term = term.astype(BF16)
+            else:
                 term = term.astype(F32) + running.astype(F32)
-            running = self.step(term.astype(wire), ring)
-            if meet is not None:
-                running = meet(slot, running)
-        own = parts[0].astype(F32)
+                term = term.astype(BF16) if wire is None else wire(term)
+            running = self.step(term, ring)
+        return running
+
+
+    def gather_two(self, value, first, second, count=None):
+        columns, slot = [], value
+        count = self.count(first) if count is None else count
+        for t in range(count):
+            column = self.gather(slot, second)
+            ahead = [self.step(slot, first)] if t + 1 < count else []
+            tied = yield ahead + column[1:]
+            columns.append([column[0]] + tied[len(ahead) :])
+            slot = tied[0]
+        return [[column[s] for column in columns] for s in range(self.count(second))]
+
+    def reduce(self, parts, ring):
+        running = self.send(parts, ring)
+        own = parts[0]
+        if running is not None:
+            own, running = yield [own, running]
+        return own.astype(F32) if running is None else own.astype(F32) + running.astype(F32)
+
+    def reduce_two(self, parts, first, second, wire=None):
+        count = self.count(first)
+        parts = [list(row) for row in parts]
+        arrived, running = {}, None
+        order = list(range(1, count)) + [0]
+        for phase in range(count + (count > 1)):
+            made = []
+            if phase > 0:
+                t = order[phase - 1]
+                term = self.partial(parts, arrived, t)
+                if running is not None:
+                    term = term + running.astype(F32)
+                made.append(self.step(term.astype(BF16) if wire is None else wire(term), first))
+            if phase < count:
+                passing = self.send([row[order[phase]] for row in parts], second, wire)
+                if passing is not None:
+                    made.append(passing)
+            after = [row[order[phase + 1]] for row in parts] if phase + 1 < count else []
+            tied = yield made + after
+            if after:
+                for row, value in zip(parts, tied[len(made) :]):
+                    row[order[phase + 1]] = value
+            if phase < count and passing is not None:
+                arrived[order[phase]] = tied[len(made) - 1]
+            if phase > 0:
+                running = tied[0]
+            if phase == count - 1 and count > 1:
+                break
+        own = self.partial(parts, arrived, 0)
         return own if running is None else own + running.astype(F32)
 
-    def gather_two(self, value, first, second, meet=None):
-        columns, slots = [], [value]
-        for t in range(1, self.count(first)):
-            arrived = self.step(slots[-1], first)
-            column = self.gather(slots[-1], second)
-            arrived, *rest = tie(arrived, *column[1:])
-            columns.append([column[0]] + rest)
-            slots.append(arrived if meet is None else meet(t, arrived))
-        columns.append(self.gather(slots[-1], second))
-        return [[column[s] for column in columns] for s in range(self.count(second))]
-
-    def reduce_two(self, parts, first, second, wire=BF16, meet=None):
-        count = self.count(first)
-        arrived = {}
-        for t in list(range(1, count)) + [0]:
-            running = None
-            for slot in range(1, self.count(second)):
-                term = parts[slot][t]
-                if running is not None:
-                    term = term.astype(F32) + running.astype(F32)
-                running = self.step(term.astype(wire), second)
-            if running is not None and meet is not None:
-                running = meet(second, t, running)
-            arrived[t] = running
-
-        def partial(t):
-            own = parts[0][t].astype(F32)
-            return own if arrived[t] is None else own + arrived[t].astype(F32)
-
-        running = None
-        for t in range(1, count):
-            term = partial(t)
-            if running is not None:
-                term = term + running.astype(F32)
-            running = self.step(term.astype(wire), first)
-            ahead = (t + 2) % count
-            if arrived[ahead] is not None and 0 < t < count - 1:
-                running, arrived[ahead] = tie(running, arrived[ahead])
-            if meet is not None:
-                running = meet(first, t, running)
-        own = partial(0)
-        return own if running is None else own + running.astype(F32)
+    def partial(self, parts, arrived, t):
+        own = parts[0][t].astype(F32)
+        return own if t not in arrived else own + arrived[t].astype(F32)
+
+
+def two_part(term):
+    width = term.shape[1] - 2 * LANES
+    value = term[:, width : width + LANES] + term[:, width + LANES :]
+    coarse = value.astype(BF16)
+    fine = (value - coarse.astype(F32)).astype(BF16)
+    return jnp.concatenate([term[:, :width].astype(BF16), coarse, fine], 1)
+
+
+class Task:
+    def __init__(self, steps):
+        self.steps, self.made, self.result, self.done = steps, [], None, False
+        self.advance(None)
+
+    def advance(self, values):
+        try:
+            self.made = list(self.steps.send(values))
+        except StopIteration as stop:
+            self.result, self.done, self.made = stop.value, True, []
+
+
+class Phases:
+    def __init__(self):
+        self.tasks = []
+
+    def start(self, steps):
+        task = Task(steps)
+        self.tasks.append(task)
+        return task
+
+    def phase(self):
+        self.tasks = [task for task in self.tasks if not task.done]
+        made = [value for task in self.tasks for value in task.made]
+        tied = list(tie(*made)) if made else []
+        for task in self.tasks:
+            count = len(task.made)
+            values, tied = tied[:count], tied[count:]
+            task.advance(values)
+
+    def finish(self, *tasks):
+        while not all(task.done for task in tasks):
+            self.phase()
+        return [task.result for task in tasks]
+
+
+def resumed(steps, made):
+    while True:
+        made = yield made
+        try:
+            made = steps.send(made)
+        except StopIteration as stop:
+            return stop.value
+
+
+def paced(steps, ready):
+    made = next(steps)
+    while True:
+        tied = yield made
+        while not ready:
+            tied = yield tied
+        try:
+            made = steps.send(tied)
+        except StopIteration as stop:
+            return stop.value
+
+
+def make(function, *arguments):
+    flat, tree = jax.tree.flatten(function(*arguments))
+    flat = yield flat
+    return jax.tree.unflatten(tree, flat)
 
 
 def tie(*values):
@@ -439,120 +519,155 @@
 
 def experts_kernel(shape, table_ref, *refs):
     slots, cores, ys, zs = shape["slots"], shape["cores"], shape["ys"], shape["zs"]
-    own, hidden, half = shape["own"], shape["hidden"], LANES // 2
+    own, hidden = shape["own"], shape["hidden"]
     x_slots, refs = refs[:slots], refs[slots:]
     beside, refs = refs[:slots], refs[slots:]
     gu_parts, refs = refs[: cores * ys], refs[cores * ys :]
     dn_parts, refs = refs[: cores * ys], refs[cores * ys :]
-    wr_ref, mixed_ref, dx_ref, gate_ref, gg_ref, x_ref, gm_ref = refs[:7]
-    act_refs, refs = refs[7 : 7 + cores], refs[7 + cores :]
-    dgu_refs, refs = refs[:cores], refs[cores:]
-    mask_ref, wgu_ref, wdn_ref, semaphores = refs
-    rows, width = x_slots[0].shape
+    wr_ref, gate_ref, x_out, gm_out = refs[:4]
+    back_outs, refs = refs[4 : 4 + slots], refs[4 + slots :]
+    act_outs, refs = refs[:cores], refs[cores:]
+    dgu_outs, refs = refs[:cores], refs[cores:]
+    x_ref, gm_ref, mask_ref, wgu_ref, wdn_ref, act_ref, dgu_ref, back_ref, in_sems, out_sems = refs
+    rows, width = x_slots[0].shape[0], x_ref.shape[1]
     part = width // (ys * zs)
-    wide = 2 * hidden * own
+    wide, tall = 2 * hidden * own, hidden * own
     local = cores * own
 
-    copies = []
+    fetched = [[] for _ in range(cores + 2)]
     for i in range(slots):
         at = pl.ds(i * rows, rows)
-        copies.append((x_slots[i], x_ref.at[at, :]))
-        copies.append((beside[i].at[:, pl.ds(0, width)], gm_ref.at[at, :]))
-        copies.append((beside[i].at[:, pl.ds(width, LANES)], mask_ref.at[at, :]))
+        first = width if shape["joined"][i] else 0
+        fetched[0].append((x_slots[i].at[:, pl.ds(0, width)], x_ref.at[at, :]))
+        fetched[cores].append((beside[i].at[:, pl.ds(first + width, LANES)], mask_ref.at[at, :]))
+        fetched[cores + 1].append((beside[i].at[:, pl.ds(first, width)], gm_ref.at[at, :]))
     step = hidden // ys
     for c in range(cores):
         for s in range(ys):
             y = table_ref[local + s]
             for z in range(zs):
                 at = pl.multiple_of((z * ys + y) * part, part)
-                copies.append(
-                    (
-                        gu_parts[c * ys + s].at[z],
-                        wgu_ref.at[pl.ds(at, part), pl.ds(c * wide, wide)],
-                    )
-                )
+                goal = wgu_ref.at[pl.ds(at, part), pl.ds(c * wide, wide)]
+                fetched[c].append((gu_parts[c * ys + s].at[z], goal))
             for e in range(own):
                 at = pl.multiple_of((c * own + e) * hidden + y * step, step)
-                copies.append((dn_parts[c * ys + s].at[e], wdn_ref.at[pl.ds(at, step), :]))
-    fetch(copies, semaphores)
-
-    block = shape["block"]
-    lane = lax.broadcasted_iota(jnp.int32, (block, LANES), 1)
-
-    def body(b, carry):
-        at = pl.ds(pl.multiple_of(b * block, block), block)
-        x = x_ref[at, :]
-        named = mask_ref[at, :].astype(F32) > 0.5
-        logits = jnp.where(named, dot(x, wr_ref[...]), NEGATIVE)
-        highest = jnp.max(logits, -1, keepdims=True)
-        exponent = jnp.where(named, jnp.exp(logits - highest), 0.0)
-        gates = exponent / jnp.sum(exponent, -1, keepdims=True)
-        gate_ref[at, :] = gates
-        picked = jnp.zeros((block, LANES), F32)
-        pre_all = dot(x, wgu_ref[...])
-        grad_act = dot(gm_ref[at, :], wdn_ref[...], ((1,), (1,)))
-        for c in range(cores):
-            for e in range(own):
-                j = c * own + e
-                mine = lane == table_ref[j]
-                gate = jnp.sum(jnp.where(mine, gates, 0.0), -1, keepdims=True)
-                gate_pre = pre_all[:, 2 * hidden * j : 2 * hidden * j + hidden]
-                up_pre = pre_all[:, 2 * hidden * j + hidden : 2 * hidden * (j + 1)]
-                grad_one = grad_act[:, j * hidden : (j + 1) * hidden]
-                sig = jax.nn.sigmoid(gate_pre)
-                silu = gate_pre * sig
-                activated = (silu * up_pre).astype(BF16).astype(F32)
-                found = jnp.sum(activated * grad_one, -1, keepdims=True)
-                picked = jnp.where(mine, found, picked)
-                act_refs[c][at, e * hidden : (e + 1) * hidden] = (activated * gate).astype(BF16)
-                grad_one = grad_one * gate
-                base = 2 * hidden * e
-                dgu_refs[c][at, base : base + hidden] = (
-                    grad_one * up_pre * sig * (1.0 + gate_pre * (1.0 - sig))
-                ).astype(BF16)
-                dgu_refs[c][at, base + hidden : base + 2 * hidden] = (grad_one * silu).astype(BF16)
-        dgu = jnp.concatenate([ref[at, :] for ref in dgu_refs], 1)
-        dx_ref[at, :] = dot(dgu, wgu_ref[...], ((1,), (1,))).astype(BF16)
-        act = jnp.concatenate([ref[at, :] for ref in act_refs], 1)
-        mixed_ref[at, :] = dot(act, wdn_ref[...]).astype(BF16)
-        coarse = picked.astype(BF16).astype(F32)
-        fine = pltpu.roll(picked - coarse, half, 1)
-        packed = jnp.where(lane < half, coarse, fine).astype(BF16)
-        for q in range(block // rows):
-            place = table_ref[local + ys + b * (block // rows) + q]
-            gg_ref[pl.ds(pl.multiple_of(place * rows, rows), rows), :] = packed[q * rows : (q + 1) * rows]
-        return carry
-
-    lax.fori_loop(0, slots * rows // block, body, 0)
+                goal = wdn_ref.at[pl.ds(at, step), :]
+                fetched[cores + 1].append((dn_parts[c * ys + s].at[e], goal))
+    used = 0
+    for group in fetched:
+        for i, (source, goal) in enumerate(group):
+            group[i] = pltpu.make_async_copy(source, goal, in_sems.at[used])
+            group[i].start()
+            used += 1
+
+    def arrive(group):
+        for copy in fetched[group]:
+            copy.wait()
+
+    leaving = []
+
+    def leave(source, goal):
+        leaving.append(pltpu.make_async_copy(source, goal, out_sems.at[len(leaving)]))
+        leaving[-1].start()
+
+    pre = []
+    for c in range(cores):
+        arrive(c)
+        if c == 0:
+            leave(x_ref, x_out)
+        pre.append(dot(x_ref[...], wgu_ref[:, c * wide : (c + 1) * wide]))
+    arrive(cores)
+    total = slots * rows
+    lane = lax.broadcasted_iota(jnp.int32, (total, LANES), 1)
+    named = mask_ref[...].astype(F32) > 0.5
+    logits = jnp.where(named, dot(x_ref[...], wr_ref[...]), NEGATIVE)
+    highest = jnp.max(logits, -1, keepdims=True)
+    exponent = jnp.where(named, jnp.exp(logits - highest), 0.0)
+    gates = exponent / jnp.sum(exponent, -1, keepdims=True)
+    gate_ref[...] = gates
+    arrive(cores + 1)
+    leave(gm_ref, gm_out)
+    grad_act = dot(gm_ref[...], wdn_ref[...], ((1,), (1,)))
+    picked = jnp.zeros((total, LANES), F32)
+    for c in range(cores):
+        for e in range(own):
+            j = c * own + e
+            mine = lane == table_ref[j]
+            gate = jnp.sum(jnp.where(mine, gates, 0.0), -1, keepdims=True)
+            base = 2 * hidden * e
+            gate_pre = pre[c][:, base : base + hidden]
+            up_pre = pre[c][:, base + hidden : base + 2 * hidden]
+            grad_one = grad_act[:, j * hidden : (j + 1) * hidden]
+            sig = jax.nn.sigmoid(gate_pre)
+            silu = gate_pre * sig
+            activated = (silu * up_pre).astype(BF16).astype(F32)
+            found = jnp.sum(activated * grad_one, -1, keepdims=True)
+            picked = jnp.where(mine, found, picked)
+            act_ref[c, :, e * hidden : (e + 1) * hidden] = (activated * gate).astype(BF16)
+            grad_one = grad_one * gate
+            base = 2 * hidden * j
+            dgu_ref[:, base : base + hidden] = (
+                grad_one * up_pre * sig * (1.0 + gate_pre * (1.0 - sig))
+            ).astype(BF16)
+            dgu_ref[:, base + hidden : base + 2 * hidden] = (grad_one * silu).astype(BF16)
+        leave(dgu_ref.at[:, pl.ds(c * wide, wide)], dgu_outs[c])
+        leave(act_ref.at[c], act_outs[c])
+
+    coarse = picked.astype(BF16)
+    back_ref[:, 2 * width : 2 * width + LANES] = coarse
+    back_ref[:, 2 * width + LANES :] = (picked - coarse.astype(F32)).astype(BF16)
+    back_ref[:, :width] = dot(dgu_ref[...], wgu_ref[...], ((1,), (1,))).astype(BF16)
+
+    def leave_back(low, count):
+        for i in range(slots):
+            source = back_ref.at[pl.ds(i * rows, rows), pl.ds(low, count)]
+            leave(source, back_outs[i].at[:, pl.ds(low, count)])
+
+    leave_back(0, width)
+    leave_back(2 * width, 2 * LANES)
+    if tall % LANES == 0:
+        acts = jnp.concatenate([act_ref[c] for c in range(cores)], 1)
+        mixed = dot(acts, wdn_ref[...])
+    else:
+        mixed = sum(dot(act_ref[c], wdn_ref[c * tall : (c + 1) * tall, :]) for c in range(cores))
+    back_ref[:, width : 2 * width] = mixed.astype(BF16)
+    leave_back(width, width)
+    for copy in leaving:
+        copy.wait()
 
 
 def run_experts(shape, table, x_slots, beside, gu_parts, dn_parts, wr):
-    rows, width = x_slots[0].shape
+    rows, width = x_slots[0].shape[0], wr.shape[0]
     total = rows * len(x_slots)
     cores, own, hidden = shape["cores"], shape["own"], shape["hidden"]
     outs = [
-        jax.ShapeDtypeStruct((total, width), BF16),
-        jax.ShapeDtypeStruct((total, width), BF16),
         jax.ShapeDtypeStruct((total, LANES), F32),
-        jax.ShapeDtypeStruct((total, LANES), BF16),
         jax.ShapeDtypeStruct((total, width), BF16),
         jax.ShapeDtypeStruct((total, width), BF16),
     ]
+    outs += [jax.ShapeDtypeStruct((rows, 2 * width + 2 * LANES), BF16) for _ in x_slots]
     outs += [jax.ShapeDtypeStruct((total, own * hidden), BF16) for _ in range(cores)]
     outs += [jax.ShapeDtypeStruct((total, 2 * own * hidden), BF16) for _ in range(cores)]
-    shape = dict(shape, slots=len(x_slots), block=2 * rows if len(x_slots) % 2 == 0 else rows)
+    joined = [slot.shape[1] > width for slot in x_slots]
+    shape = dict(shape, slots=len(x_slots), joined=joined)
     copies = 3 * len(x_slots) + cores * shape["ys"] * (shape["zs"] + own)
     operands = x_slots + beside + gu_parts + dn_parts
     return pl.pallas_call(
         functools.partial(experts_kernel, shape),
         in_specs=[pl.BlockSpec(memory_space=pltpu.SMEM)] + [anywhere() for _ in operands] + [on_chip()],
-        out_specs=[on_chip() for _ in outs],
+        out_specs=[on_chip()] + [anywhere() for _ in outs[1:]],
         out_shape=outs,
         scratch_shapes=[
+            pltpu.VMEM((total, width), BF16),
+            pltpu.VMEM((total, width), BF16),
             pltpu.VMEM((total, LANES), BF16),
             pltpu.VMEM((width, cores * own * 2 * hidden), BF16),
             pltpu.VMEM((cores * own * hidden, width), BF16),
+            pltpu.VMEM((cores, total, own * hidden), BF16),
+            pltpu.VMEM((total, cores * own * 2 * hidden), BF16),
+            pltpu.VMEM((total, 2 * width + 2 * LANES), BF16),
             pltpu.SemaphoreType.DMA((copies,)),
+            pltpu.SemaphoreType.DMA((2 + 2 * cores + 3 * len(x_slots),)),
         ],
         compiler_params=pltpu.CompilerParams(vmem_limit_bytes=60 << 20),
         name="experts",
@@ -627,13 +742,18 @@
     heads, kv_heads = HEADS // members, KV_HEADS // members
     weight_rows = w_query.shape[0]
     home_rows = micros * rows
-    half_lanes = LANES // 2
+
+    phases = Phases()
 
     def over_members(value):
-        return [slot for column in rings.gather_two(value, "c", "x") for slot in column]
+        return phases.start(rings.gather_two(value, "c", "x"))
 
     def sum_members(parts):
-        return rings.reduce_two([[parts[s * cn + t] for s in range(xn)] for t in range(cn)], "x", "c")
+        parts = [[parts[s * cn + t] for s in range(xn)] for t in range(cn)]
+        return phases.start(rings.reduce_two(parts, "x", "c"))
+
+    def line(columns):
+        return [slot for column in columns for slot in column]
 
     def by_member(w):
         return w.reshape(weight_rows, members, w.shape[1] // members)
@@ -643,8 +763,6 @@
     small = jnp.broadcast_to(small[:, None, :], (weight_rows, members, LANES))
     mine = jnp.concatenate([by_member(w_query), by_member(w_key), by_member(w_value), small], 2)
     mine = lax.all_to_all(mine.transpose(1, 0, 2), "expert", 0, 0)
-    gate_up = pack_experts(w_gate, w_up, zn)
-    mine, gate_up = tie(mine, gate_up)
     small_at = mine.shape[2]
     qkv_columns = small_at - LANES
     pack_rows = members * weight_rows
@@ -652,6 +770,12 @@
     to_heads = [(s, (s % dp_count) * members + s // dp_count) for s in range(devices)]
     to_home = [(t, s) for s, t in to_heads]
     out_mine = lax.ppermute(w_out, ALL, to_heads)
+    weights_started = []
+    group_tokens = phases.start(paced(rings.gather_two(tokens, "c", "x"), weights_started))
+    gate_up = pack_experts(w_gate, w_up, zn)
+    begun = phases.start(make(lambda: (mine, gate_up, out_mine, routes)))
+    phases.phase()
+    (mine, gate_up, out_mine, routes) = begun.result
     merged_columns = width // members
     pack = jnp.concatenate(
         [out_mine[:, i * merged_columns : (i + 1) * merged_columns] for i in range(members)], 0
@@ -671,15 +795,26 @@
         "packs": 3 if whole else dp_count,
         "copies": micros * members + (3 if whole else dp_count * (2 + members)),
     }
+    def beside_started(value):
+        column = rings.gather(value, "x")
+        ahead = [rings.step(value, "z")] if zn > 1 else []
+        tied = yield ahead + column[1:]
+        return [column[0]] + tied[len(ahead) :], tied[0]
+
     inputs = tokens.astype(F32)
     inv_first = lax.rsqrt(jnp.mean(inputs * inputs, -1, keepdims=True) + EPSILON)
     unit_first = inputs * inv_first
-    group_tokens = over_members(tokens)
-
-    pack, routes = tie(pack, routes)
+
+    pack, routes, w_down = tie(pack, routes, w_down)
+    packs = phases.start(rings.gather_two(pack, "z", "y"))
+    weights_started.append(True)
+    phases.phase()
     dealt = lax.all_to_all(
         routes.reshape(micros, dp_count, rows // dp_count, routes.shape[2]), "dp", 1, 1
     ).reshape(micros, rows, routes.shape[2])
+    held = phases.start(make(lambda: dealt))
+    phases.phase()
+    dealt = held.result
     lane_ids = jnp.arange(LANES, dtype=jnp.int32)
     hot = jnp.sum((dealt[:, :, :, None] == lane_ids).astype(F32), 2).astype(BF16)
     place = (shuffle[:, 0, :, None] == jnp.arange(rows, dtype=jnp.int32)).astype(BF16)
@@ -697,7 +832,7 @@
             for t in range(cn)
         ]
     )
-    row_at, pack = tie(row_at, pack)
+    row_at, dealt = tie(row_at, dealt)
     half = HEAD_DIM // 2
     lane = jnp.arange(LANES, dtype=jnp.int32)
     inverse = ROPE_BASE ** (-((lane % half).astype(F32) * 2.0) / HEAD_DIM)
@@ -714,21 +849,14 @@
     allowed = segment[:, :, None] == segment[:, None, :]
     bias = jnp.where(allowed & (row_at[None, :] <= row_at[:, None]), 0.0, NEGATIVE)
 
-    waiting = {"beside": beside, "gate_up": gate_up, "down": w_down}
-    tables = {"cosine": cosine, "sine": sine, "bias": bias}
-
-    def weights_arrived(slot, value):
-        if slot == 1:
-            value, *tied = tie(value, *tables.values())
-            tables.update(zip(list(tables), tied))
-        if slot < zn - 1:
-            return value
-        names = list(waiting)
-        tied = tie(value, *waiting.values())
-        waiting.update(zip(names, tied[1:]))
-        return tied[0]
-
-    packs = rings.gather_two(pack, "z", "y", weights_arrived)
+    tables = phases.start(make(lambda: (cosine, sine, bias, beside, gate_up, w_down)))
+    phases.phase()
+    cosine, sine, bias, beside, gate_up, w_down = tables.result
+    beside = phases.start(beside_started(beside))
+    gate_up = lax.all_to_all(gate_up, "dp", 0, 0, axis_index_groups=rings.z_groups)
+    held = phases.start(make(lambda: w_down))
+    packs, group_tokens = phases.finish(packs, group_tokens)
+    w_down = held.result
     spots = jnp.stack(
         [rings.origin("z", t) * yn + rings.origin("y", s) for s in range(yn) for t in range(zn)]
     )
@@ -741,43 +869,58 @@
         w_small = packs[:, :, qkv_columns:small_at].reshape(width, LANES)
         packs = [packs[:, :, :qkv_columns].reshape(width, qkv_columns), w_merge, w_small]
     else:
-        packs = [slot for column in packs for slot in column]
-
-    beside = rings.gather_two(waiting["beside"], "z", "x")
-    gate_up = lax.all_to_all(waiting["gate_up"], "dp", 0, 0, axis_index_groups=rings.z_groups)
-    down = rings.gather(waiting["down"], "y")
-    cosine, sine, bias = tables["cosine"], tables["sine"], tables["bias"]
-    attn_parts, group_in, n1, router_columns, small_rows, qkv, merged, lse = attention_forward(
-        attention_shape, spots, packs, group_tokens, cosine, sine, bias
+        packs = line(packs)
+
+    down = rings.gather(w_down, "y")
+    attention = phases.start(
+        make(
+            attention_forward,
+            attention_shape,
+            spots,
+            packs,
+            line(group_tokens),
+            cosine,
+            sine,
+            bias,
+        )
     )
+    down_task = phases.start(make(lambda: down))
+    phases.finish(attention)
+    down = phases.start(make(lambda: [rings.gather(part, "c") for part in down_task.result]))
+    attn_parts, group_in, n1, router_columns, small_rows, qkv, merged, lse = attention.result
     gain_first = small_rows[experts_all]
     gain_second = small_rows[experts_all + 1]
-    hidden = inputs + RESIDUAL_SCALE * sum_members(attn_parts)
+    attended = sum_members(attn_parts)
+    for _ in range(xn - 1):
+        phases.phase()
+    gate_up = phases.start(make(lambda: gate_up))
+    attended, down, gate_up = phases.finish(attended, down, gate_up)
+    hidden = inputs + RESIDUAL_SCALE * attended
     inv_second = lax.rsqrt(jnp.mean(hidden * hidden, -1, keepdims=True) + EPSILON)
     unit_second = hidden * inv_second
     normed_second = (unit_second * gain_second).astype(BF16).reshape(home_rows, width)
-    def meeting(store, *names):
-        def meet(value):
-            value, *values = tie(value, *[store[name] for name in names])
-            store.update(zip(names, values))
-            return value
-
-        return meet
-
-    waiting = {"gate_up": gate_up, "down": down[-1]}
-
-    def rows_arrived(slot, value):
-        if slot == 1:
-            value = meeting(waiting, "gate_up", "down")(value)
-            waiting["parts"] = rings.gather(waiting["gate_up"], "y")[1:]
-        if slot == zn - 1:
-            value, *waiting["parts"] = tie(value, *waiting["parts"])
-        return value
-
-    group_x = rings.gather_two(normed_second, "z", "x", rows_arrived)
-
-    gate_up = [rings.gather(part, "c") for part in [waiting["gate_up"]] + waiting["parts"]]
-    down = [rings.gather(part, "c") for part in down[:-1] + [waiting["down"]]]
+
+    if zn > 1:
+        first = phases.start(make(lambda: [rings.step(normed_second, "z")] + rings.gather(normed_second, "x")))
+        phases.finish(first)
+        passed, *column = first.result
+        together = jnp.concatenate([passed, beside.result[1]], 1)
+        group = phases.start(rings.gather_two(together, "z", "x", zn - 1))
+    else:
+        first = phases.start(make(lambda: rings.gather(normed_second, "x")))
+        phases.finish(first)
+        column, group = first.result, None
+    gate_up = rings.gather(gate_up, "y")
+    if group is not None:
+        phases.phase()
+        phases.phase()
+    mine_too = phases.start(make(lambda: rings.gather(gate_up[0], "c")))
+    gate_up = phases.start(make(lambda: gate_up[1:]))
+    phases.finish(mine_too, gate_up, *([] if group is None else [group]))
+    gate_up = [mine_too.result] + [rings.gather(part, "c") for part in gate_up.result]
+    later = [[] for _ in range(xn)] if group is None else group.result
+    group_x = [[column[i]] + later[i] for i in range(xn)]
+    beside = [[beside.result[0][i]] + later[i] for i in range(xn)]
     gu_parts = [gate_up[s][c] for c in range(cn) for s in range(yn)]
     dn_parts = [down[s][c] for c in range(cn) for s in range(yn)]
 
@@ -792,8 +935,6 @@
         for s in range(cn)
     ]
     table.append(jnp.stack([rings.origin("y", s) for s in range(yn)]))
-    goals = jnp.stack([rings.origin("z", t) * xn + rings.origin("x", s) for s, t in slots])
-    table.append(goals if chunks == 1 else jnp.arange(chunk, dtype=jnp.int32))
     table = jnp.concatenate(table)
     experts_shape = {"cores": cn, "ys": yn, "zs": zn, "own": own_experts, "hidden": hidden_part}
     results = [
@@ -808,55 +949,68 @@
         )
         for i in range(chunks)
     ]
-    if chunks == 1:
-        results = list(results[0])
+    back = [part for pieces in results for part in pieces[3 : 3 + chunk]]
+    results = [pieces[:3] + pieces[3 + chunk :] for pieces in results]
+    results = [pieces[0] if chunks == 1 else jnp.concatenate(pieces, 0) for pieces in zip(*results)]
+    gates, x_all, gm_all = results[:3]
+    acts, dgus = results[3 : 3 + cn], results[3 + cn :]
+    back = [back[i * zn : (i + 1) * zn] for i in range(xn)]
+
+    def by_y(value, axis):
+        return [lax.dynamic_index_in_dim(value, rings.origin("y", s), axis, False) for s in range(yn)]
+
+    def product(core, kind, x, gm, coming):
+        if kind == 0:
+            term = dot(x, dgus[core], ((0,), (0,)))
+        else:
+            term = dot(acts[core], gm, ((0,), (0,)))
+        return (term if coming is None else term + coming.astype(F32)).astype(BF16)
+
+    def own_gu(x, coming):
+        return by_y(product(0, 0, x, None, coming).reshape(zn, yn, model_part, -1), 1)
+
+    def own_dn(gm, coming):
+        value = product(0, 1, None, gm, coming)
+        return by_y(value.reshape(own_experts, yn, hidden_part // yn, width), 1)
+
+    rows_back = phases.start(rings.reduce_two(back, "z", "x", two_part))
+    if cn > 1:
+        work = phases.start(make(lambda: (product(1, 0, x_all, None, None), x_all, gm_all)))
+        phases.phase()
+        other, x, gm = work.result
+        coming = rings.step(other, "c")
     else:
-        results = [jnp.concatenate(pieces, 0) for pieces in zip(*results)]
-    mixed, dx, gates, grad_gates, x_all, gm_all = results[:6]
-    acts, dgus = results[6 : 6 + cn], results[6 + cn :]
-
-    def to_owner(value, meet=None):
-        parts = value.reshape(xn, zn, home_rows, width)
-        parts = [[parts[s, t] for t in range(zn)] for s in range(xn)]
-        return rings.reduce_two(parts, "z", "x", meet=meet)
-
-    grad_gates = grad_gates.reshape(len(slots), home_rows, LANES)
-    if chunks > 1:
-        grad_gates = jnp.zeros_like(grad_gates).at[goals].set(grad_gates)
-    grad_gates = lax.all_to_all(grad_gates, ALL, 0, 0, axis_index_groups=rings.token_groups)
-    grad_gates = jnp.sum(grad_gates.astype(F32), 0)
-    grad_gates = grad_gates[:, :half_lanes] + grad_gates[:, half_lanes:]
-    def sum_cores(terms):
-        running = None
-        for slot in range(1, cn):
-            term = terms(slot)
-            running = rings.step((term if running is None else term + running).astype(BF16), "c")
-            running = running.astype(F32)
-        own = terms(0)
-        return (own if running is None else own + running).astype(BF16)
-
-    grad_gu = sum_cores(lambda s: dot(x_all, dgus[s], ((0,), (0,))))
-    grad_dn = sum_cores(lambda s: dot(acts[s], gm_all, ((0,), (0,))))
-    wide = own_experts * 2 * hidden_part
-    grad_gu = grad_gu.reshape(zn, yn, model_part, wide)
-    grad_gu = [lax.dynamic_index_in_dim(grad_gu, rings.origin("y", s), 1, False) for s in range(yn)]
-    grad_dn = grad_dn.reshape(own_experts, yn, hidden_part // yn, width)
-    grad_dn = [lax.dynamic_index_in_dim(grad_dn, rings.origin("y", s), 1, False) for s in range(yn)]
-    waiting = {"mixed": mixed, "weights": grad_gu + grad_dn}
-
-    def rows_sent(ring, slot, value):
-        if ring == "x" and slot == 0:
-            value = meeting(waiting, "mixed")(value)
-        if ring == "z" and slot == min(2, zn - 1):
-            value, *waiting["weights"] = tie(value, *waiting["weights"])
-        return value
-
-    grad_dealt = to_owner(dx, rows_sent)
-    grad_gu, grad_dn = waiting["weights"][:yn], waiting["weights"][yn:]
-    own_gates = gates[:home_rows, :half_lanes]
+        x, gm, coming = x_all, gm_all, None
+    work = phases.start(make(lambda: (own_gu(x, coming), gm)))
+    phases.phase()
+    made, gm = work.result
+    groups = [(0, 2), (2, 4), (4, own_experts)] if own_experts > 4 else [(0, own_experts)]
+    wide = 2 * hidden_part
+    made = [[part[:, :, low * wide : high * wide] for part in made] for low, high in groups]
+    grad_gu = []
+
+    def next_group():
+        if len(grad_gu) < len(groups):
+            grad_gu.append(phases.start(rings.reduce(made[len(grad_gu)], "y")))
+
+    next_group()
+    if cn > 1:
+        work = phases.start(make(lambda: (product(1, 1, None, gm, None), gm)))
+        phases.phase()
+        other, gm = work.result
+        coming = rings.step(other, "c")
+    next_group()
+    work = phases.start(make(lambda: own_dn(gm, coming)))
+    phases.finish(rows_back, work)
+    grad_dn = work.result
+    grad_dealt, moe_rows = rows_back.result[:, :width], rows_back.result[:, width : 2 * width]
+    grad_gates = rows_back.result[:, 2 * width :]
+    grad_gates = grad_gates[:, :LANES] + grad_gates[:, LANES:]
+    own_gates = gates[:home_rows]
     grad_picked = own_gates * (grad_gates - jnp.sum(own_gates * grad_gates, -1, keepdims=True))
     grad_logits = grad_picked.astype(BF16)
-    grad_dealt = (grad_dealt + dot(grad_logits, small_rows.astype(BF16))).astype(BF16)
+    router_rows = small_rows.astype(BF16)
+    grad_dealt = (grad_dealt + dot(grad_logits[:, : LANES // 2], router_rows)).astype(BF16)
     grad_normed_second = grad_dealt.astype(F32).reshape(micros, rows, width)
     scaled_second = grad_normed_second * gain_second
     grad_hidden = grad_result + inv_second * (
@@ -866,34 +1020,29 @@
     grad_attn = (RESIDUAL_SCALE * grad_hidden).astype(BF16)
 
     grad_attn = over_members(grad_attn)
-    moe_rows = to_owner(waiting["mixed"]).astype(BF16).reshape(micros, rows, width)
-    grad_attn[-1], moe_rows = tie(grad_attn[-1], moe_rows)
-    output = (hidden + RESIDUAL_SCALE * moe_rows.astype(F32)).astype(BF16)
-
-    first_parts, weight_grads = attention_backward(
-        attention_shape,
-        spots,
-        packs,
-        grad_attn,
-        [cosine, sine, bias, qkv, lse, group_in],
-        [n1, merged, normed_second, jnp.pad(grad_logits, ((0, 0), (0, half_lanes))), mlp_gain_grad],
+    grad_dn = rings.reduce(grad_dn, "y")
+    made_dn = next(grad_dn)
+    while len(grad_gu) < len(groups):
+        next_group()
+    phases.phase()
+    grad_gu = jnp.concatenate([part.astype(BF16) for part in phases.finish(*grad_gu)], 2)
+    grad_gu = lax.all_to_all(grad_gu, "dp", 0, 0, axis_index_groups=rings.z_groups)
+    phases.finish(grad_attn)
+    grad_dn = phases.start(resumed(grad_dn, made_dn))
+
+    attention = phases.start(
+        make(
+            attention_backward,
+            attention_shape,
+            spots,
+            packs,
+            line(grad_attn.result),
+            [cosine, sine, bias, qkv, lse, group_in],
+            [n1, merged, normed_second, grad_logits, mlp_gain_grad],
+        )
     )
-    grad_normed_first = sum_members(first_parts)
-    scaled_first = grad_normed_first * gain_first
-    grad_tokens = grad_hidden + inv_first * (
-        scaled_first - unit_first * jnp.mean(scaled_first * unit_first, -1, keepdims=True)
-    )
-
-    waiting = {"weights": weight_grads}
-
-    def experts_sent(slot, value):
-        value, *waiting["weights"] = tie(value, *waiting["weights"])
-        return value
-
-    grad_gu = rings.reduce(grad_gu, "y", meet=experts_sent).astype(BF16)
-    grad_dn = rings.reduce(grad_dn, "y", meet=experts_sent)
-    grad_gu = lax.all_to_all(grad_gu, "dp", 0, 0, axis_index_groups=rings.z_groups)
-    weight_grads = waiting["weights"]
+    phases.finish(attention)
+    first_parts, weight_grads = attention.result
 
     if whole:
         grad_qkv, grad_out, grad_small = weight_grads
@@ -909,11 +1058,22 @@
         weight_grads = [
             lax.dynamic_index_in_dim(both, spots[i], 0, False) for i in range(dp_count)
         ]
-    both = rings.reduce_two(
-        [[weight_grads[s * zn + t] for t in range(zn)] for s in range(yn)], "z", "y"
+    both = phases.start(
+        rings.reduce_two([[weight_grads[s * zn + t] for t in range(zn)] for s in range(yn)], "z", "y")
     )
-    both, grad_gu = tie(both, grad_gu)
+    grad_gu = phases.start(make(lambda: grad_gu))
+    phases.phase()
+    grad_normed_first = sum_members(first_parts)
+    both, grad_gu, grad_dn, grad_normed_first = phases.finish(
+        both, grad_gu, grad_dn, grad_normed_first
+    )
     grad_gate, grad_up = unpack_experts(grad_gu, own_experts)
+    moe_rows = moe_rows.astype(BF16).reshape(micros, rows, width)
+    output = (hidden + RESIDUAL_SCALE * moe_rows.astype(F32)).astype(BF16)
+    scaled_first = grad_normed_first * gain_first
+    grad_tokens = grad_hidden + inv_first * (
+        scaled_first - unit_first * jnp.mean(scaled_first * unit_first, -1, keepdims=True)
+    )
     grad_out = [
         both[i * weight_rows : (i + 1) * weight_rows, small_at:] for i in range(members)
     ]

time: 537 us -> 491 us (0.914)
  the two profiles are of different devices: /device:TPU:4 before, /device:TPU:3 now
where the time goes in v3:
time: 491 us; the launch traced here: 483 us
  waiting for transfers between devices  229 us (47%)
  starting transfers between devices  94.9 us (19%)
  Pallas kernels  81.1 us (17%)
  other arithmetic  32.4 us (7%)
  local copies, waits for them, and re-layouts  23 us (5%)
  matrix products  20.4 us (4%)
    ppermute x54, waiting for transfers between devices, step(): return lax.ppermute(value, axis, pairs)  202 us
    ppermute x54, starting transfers between devices, step(): return lax.ppermute(value, axis, pairs)  64.6 us
    pallas_call x1, Pallas kernels, run_experts(): pl.pallas_call(functools.partial(experts_kernel, shape), in_specs=[pl.Blo...  38.7 us
    dot_general x5, matrix products, dot(): return lax.dot_general(a, b, (dims, ((), ())), preferred_element_type=F32)  20.3 us
    pallas_call x1, Pallas kernels, attention_backward(): pl.pallas_call(functools.partial(attention_backward_kernel, shape), grid_...  19.3 us
    pallas_call x1, Pallas kernels, attention_forward(): pl.pallas_call(functools.partial(attention_forward_kernel, shape), grid_s...  13.7 us
    unnamed x126, local copies, waits for them, and re-layouts  12.7 us
    ppermute x1, waiting for transfers between devices, per_device(): grad_out = lax.ppermute(jnp.concatenate(grad_out, 1), ALL, to_home)  10.2 us
  transfers between devices with their start and end apart: 61, of which 38 were waited for; matrix products, arithmetic and copies ran while one was open for 10% of the time, Pallas kernels for 9%

profile of v3, /device:TPU:3, one launch (start us, length us, event | category | flops | bytes accessed | tf_op | source)
XLA Modules:
  0.0 483.3 jit_solution(9792194396040790311)
XLA Ops:
  24.2 6.1 %collective-permute-done.4.refs_4_ = bf16[192,1152]{1,0:T(8,128)(2,1)S(1)} collective-permute-done((bf16[192,1152]{1,0:T(8,128)(2,1)S(1)}, bf16[192,1152]{1,0:T(8,128)(2,1)S(1)}, u32[]{:S(2)}, u32[]{:S(2)}) %collective-permute-start.4) | collective-permute-done | bytes 442400 | tf_op jit(solution)/shard_map/ppermute | solution.py:67
  55.6 5.6 %collective-permute-done.9.refs_6_ = bf16[192,1152]{1,0:T(8,128)(2,1)S(1)} collective-permute-done((bf16[192,1152]{1,0:T(8,128)(2,1)S(1)}, bf16[192,1152]{1,0:T(8,128)(2,1)S(1)}, u32[]{:S(2)}, u32[]{:S(2)}) %collective-permute-start.9) | collective-permute-done | bytes 442400 | tf_op jit(solution)/shard_map/ppermute | solution.py:67
  81.8 13.7 %attention_forward.1 = (bf16[2,64,1536]{2,1,0:T(8,128)(2,1)}, bf16[2,64,1536]{2,1,0:T(8,128)(2,1)}, bf16[2,64,1536]{2,1,0:T(8,128)(2,1)}, bf16[2,64,1536]{2,1,0:...) custom-call(s32[8]{0:T(128)} %stack.41.spots_ref, ...), custom_call_target="tpu_custom_call" | custom-call | tf_op jit(solution)/shard_map/attention_forward/pallas_call | solution.py:464
  97.3 6.9 %collective-permute-start.14 = (bf16[5,64,1536]{2,1,0:T(8,128)(2,1)}, bf16[5,64,1536]{2,1,0:T(8,128)(2,1)}, u32[]{:S(2)}, u32[]{:S(2)}) collective-permute-start(bf16[5,64,1536]{2,1,0:T(8,128)(2,1)} %refs_20_), channel_id=1, source_target_pairs={{0,1},{1,0},{2,3},{3,2},{4,5},{5,4},{6,7},{7,6},{8,9},{9,8},{10,11... | collective-permute-start | bytes 2949128 | tf_op jit(solution)/shard_map/ppermute | solution.py:67
  111.7 8.5 %collective-permute-done.17 = bf16[2,64,1536]{2,1,0:T(8,128)(2,1)S(1)} collective-permute-done((bf16[2,64,1536]{2,1,0:T(8,128)(2,1)S(1)}, bf16[2,64,1536]{2,1,0:T(8,128)(2,1)S(1)}, u32[]{:S(2)}, u32[]{:S(2)}) %collective-permute-start.17) | collective-permute-done | bytes 393248 | tf_op jit(solution)/shard_map/ppermute | solution.py:67
  126.8 10.1 %collective-permute-done.20.refs_4_ = bf16[128,1536]{1,0:T(8,128)(2,1)S(1)} collective-permute-done((bf16[128,1536]{1,0:T(8,128)(2,1)S(1)}, bf16[128,1536]{1,0:T(8,128)(2,1)S(1)}, u32[]{:S(2)}, u32[]{:S(2)}) %collective-permute-start.20) | collective-permute-done | bytes 393248 | tf_op jit(solution)/shard_map/ppermute | solution.py:67
  144.7 13.2 %collective-permute-done.22.refs_5_.refs_13_ = bf16[128,3200]{1,0:T(8,128)(2,1)S(1)} collective-permute-done((bf16[128,3200]{1,0:T(8,128)(2,1)S(1)}, bf16[128,3200]{1,0:T(8,128)(2,1)S(1)}, u32[]{:S(2)}, u32[]{:S(2)}) %collective-permute-start.22) | collective-permute-done | bytes 819232 | tf_op jit(solution)/shard_map/ppermute | solution.py:67
  161.2 16.4 %collective-permute-done.24.refs_6_.refs_14_ = bf16[128,3200]{1,0:T(8,128)(2,1)S(1)} collective-permute-done((bf16[128,3200]{1,0:T(8,128)(2,1)S(1)}, bf16[128,3200]{1,0:T(8,128)(2,1)S(1)}, u32[]{:S(2)}, u32[]{:S(2)}) %collective-permute-start.24) | collective-permute-done | bytes 819232 | tf_op jit(solution)/shard_map/ppermute | solution.py:67
  183.5 11.7 %collective-permute-done.25.refs_7_.refs_15_ = bf16[128,3200]{1,0:T(8,128)(2,1)S(1)} collective-permute-done((bf16[128,3200]{1,0:T(8,128)(2,1)S(1)}, bf16[128,3200]{1,0:T(8,128)(2,1)S(1)}, u32[]{:S(2)}, u32[]{:S(2)}) %collective-permute-start.25) | collective-permute-done | bytes 819232 | tf_op jit(solution)/shard_map/ppermute | solution.py:67
  206.3 38.7 %experts.1 = (f32[1024,128]{1,0:T(8,128)}, bf16[1024,1536]{1,0:T(8,128)(2,1)}, bf16[1024,1536]{1,0:T(8,128)(2,1)}, bf16[128,3328]{1,0:T(8,128)(2,1)}, bf16[128,3...) custom-call(s32[12]{0:T(128)} %pad_add_fusion.1.table_ref, ...), custom_call_target="tpu_custom_call" | custom-call | tf_op jit(solution)/shard_map/experts/pallas_call | solution.py:655
  246.4 9.3 %convolution_convert_fusion = bf16[1536,1280]{1,0:T(8,128)(2,1)} fusion(bf16[1024,1536]{1,0:T(8,128)(2,1)} %get-tuple-element.262, bf16[1024,1280]{1,0:T(8,128)(2,1)} %get-tuple-element.254), kind=kOutput, calls=%fused_computation.1 | convolution fusion | flops 4028497920 | bytes 9699328 | tf_op jit(solution)/shard_map/dot_general | solution.py:27
  255.7 9.7 %collective-permute-done.29 = bf16[128,3328]{1,0:T(8,128)(2,1)S(1)} collective-permute-done((bf16[128,3328]{1,0:T(8,128)(2,1)}, bf16[128,3328]{1,0:T(8,128)(2,1)S(1)}, u32[]{:S(2)}, u32[]{:S(2)}) %collective-permute-start.29) | collective-permute-done | bytes 852000 | tf_op jit(solution)/shard_map/ppermute | solution.py:67
  273.4 6.2 %fusion = bf16[1536,1280]{1,0:T(8,128)(2,1)S(1)} fusion(bf16[1536,1280]{1,0:T(8,128)(2,1)} %collective-permute-done.32, bf16[1024,1536]{1,0:T(8,128)(2,1)S(1)} %copy-done.52, bf16[1024,1280]{1,0:T(8,128)(2,1)S(1)} %copy-done.53), kind=kOutput, calls=%fused_computation.2 | convolution fusion | flops 4032430080 | bytes 13631488 | tf_op jit(solution)/shard_map/dot_general | solution.py:27
  279.8 9.6 %collective-permute-done.30 = bf16[128,3328]{1,0:T(8,128)(2,1)S(1)} collective-permute-done((bf16[128,3328]{1,0:T(8,128)(2,1)S(1)}, bf16[128,3328]{1,0:T(8,128)(2,1)S(1)}, u32[]{:S(2)}, u32[]{:S(2)}) %collective-permute-start.30) | collective-permute-done | bytes 852000 | tf_op jit(solution)/shard_map/ppermute | solution.py:67
  296.8 13.6 %collective-permute-done.35 = bf16[4,192,512]{2,1,0:T(8,128)(2,1)S(1)} collective-permute-done((bf16[4,192,512]{2,1,0:T(8,128)(2,1)S(1)}, bf16[4,192,512]{2,1,0:T(8,128)(2,1)S(1)}, u32[]{:S(2)}, u32[]{:S(2)}) %collective-permute-start.35) | collective-permute-done | bytes 786464 | tf_op jit(solution)/shard_map/ppermute | solution.py:67
  321.4 19.7 %collective-permute-done.38 = bf16[4,192,512]{2,1,0:T(8,128)(2,1)S(1)} collective-permute-done((bf16[4,192,512]{2,1,0:T(8,128)(2,1)S(1)}, bf16[4,192,512]{2,1,0:T(8,128)(2,1)S(1)}, u32[]{:S(2)}, u32[]{:S(2)}) %collective-permute-start.38) | collective-permute-done | bytes 786464 | tf_op jit(solution)/shard_map/ppermute | solution.py:67
  347.2 7.2 %collective-permute-done.42.refs_10_ = bf16[2,64,1536]{2,1,0:T(8,128)(2,1)S(1)} collective-permute-done((bf16[2,64,1536]{2,1,0:T(8,128)(2,1)S(1)}, bf16[2,64,1536]{2,1,0:T(8,128)(2,1)S(1)}, u32[]{:S(2)}, u32[]{:S(2)}) %collective-permute-start.42) | collective-permute-done | bytes 393248 | tf_op jit(solution)/shard_map/ppermute | solution.py:67
  364.2 7.2 %collective-permute-done.44.refs_11_ = bf16[2,64,1536]{2,1,0:T(8,128)(2,1)} collective-permute-done((bf16[2,64,1536]{2,1,0:T(8,128)(2,1)}, bf16[2,64,1536]{2,1,0:T(8,128)(2,1)}, u32[]{:S(2)}, u32[]{:S(2)}) %collective-permute-start.44) | collective-permute-done | bytes 393248 | tf_op jit(solution)/shard_map/ppermute | solution.py:67
  371.3 19.3 %attention_backward.1 = (bf16[2,64,1536]{2,1,0:T(8,128)(2,1)}, bf16[2,64,1536]{2,1,0:T(8,128)(2,1)}, bf16[2,64,1536]{2,1,0:T(8,128)(2,1)}, bf16[2,64,1536]{2,1,0...) custom-call(s32[8]{0:T(128)} %stack.41.spots_ref, ...), custom_call_target="tpu_custom_call" | custom-call | tf_op jit(solution)/shard_map/attention_backward/pallas_call | solution.py:490
  390.9 8.9 %collective-permute-done.45 = bf16[192,1152]{1,0:T(8,128)(2,1)} collective-permute-done((bf16[192,1152]{1,0:T(8,128)(2,1)}, bf16[192,1152]{1,0:T(8,128)(2,1)}, u32[]{:S(2)}, u32[]{:S(2)}) %collective-permute-start.45) | collective-permute-done | bytes 442400 | tf_op jit(solution)/shard_map/ppermute | solution.py:67
  399.8 6.0 %all-to-all-done.3.in_ref = bf16[4,192,1280]{2,1,0:T(8,128)(2,1)S(1)} async-done(((bf16[4,192,1280]{2,1,0:T(8,128)(2,1)}), bf16[4,192,1280]{2,1,0:T(8,128)(2,1)S(1)}, u32[]{:S(2)}, u32[]{:S(2)}) %all-to-all-start.3) | async-done | bytes 1966112 | tf_op jit(solution)/shard_map/all_to_all | solution.py:1029
  412.9 7.3 %collective-permute-done.46 = bf16[192,1152]{1,0:T(8,128)(2,1)S(1)} collective-permute-done((bf16[192,1152]{1,0:T(8,128)(2,1)S(1)}, bf16[192,1152]{1,0:T(8,128)(2,1)S(1)}, u32[]{:S(2)}, u32[]{:S(2)}) %collective-permute-start.46) | collective-permute-done | bytes 442400 | tf_op jit(solution)/shard_map/ppermute | solution.py:67
  429.7 9.3 %collective-permute-done.49 = bf16[192,1152]{1,0:T(8,128)(2,1)S(1)} collective-permute-done((bf16[192,1152]{1,0:T(8,128)(2,1)S(1)}, bf16[192,1152]{1,0:T(8,128)(2,1)S(1)}, u32[]{:S(2)}, u32[]{:S(2)}) %collective-permute-start.49) | collective-permute-done | bytes 442400 | tf_op jit(solution)/shard_map/ppermute | solution.py:67
  467.4 10.2 %collective-permute-done.55 = f32[48,1536]{1,0:T(8,128)} collective-permute-done((f32[48,1536]{1,0:T(8,128)S(1)}, f32[48,1536]{1,0:T(8,128)}, u32[]{:S(2)}, u32[]{:S(2)}) %collective-permute-start.55) | collective-permute-done | bytes 294944 | tf_op jit(solution)/shard_map/ppermute | solution.py:1080
  (321 shorter events, 207.0 us)
Async XLA Ops:
  0.7 20.1 %collective-permute-start = (bf16[2,64,1536]{2,1,0:T(8,128)(2,1)}, bf16[2,64,1536]{2,1,0:T(8,128)(2,1)S(1)}, u32[]{:S(2)}, u32[]{:S(2)}) collective-permute-start(bf16[2,64,1536]{2,1,0:T(8,128)(2,1)} %refs_8_.1), channel_id=1, source_target_pairs={{0,1},{1,0},{2,3},{3,2},{4,5},{5,4},{6,7},{7,6},{8,9},{9,8},{10,11... | collective-permute-start | bytes 1179656 | tf_op jit(solution)/shard_map/ppermute | solution.py:67
  1.4 19.4 %collective-permute-start.1 = (bf16[2,64,1536]{2,1,0:T(8,128)(2,1)}, bf16[2,64,1536]{2,1,0:T(8,128)(2,1)S(1)}, u32[]{:S(2)}, u32[]{:S(2)}) collective-permute-start(bf16[2,64,1536]{2,1,0:T(8,128)(2,1)} %refs_8_.1), channel_id=1, source_target_pairs={{0,2},{1,3},{2,0},{3,1},{4,6},{5,7},{6,4},{7,5},{8,10},{9,11},{10,... | collective-permute-start | bytes 1179656 | tf_op jit(solution)/shard_map/ppermute | solution.py:67
  33.2 17.6 %collective-permute-start.7 = (bf16[192,1152]{1,0:T(8,128)(2,1)S(1)}, bf16[192,1152]{1,0:T(8,128)(2,1)S(1)}, u32[]{:S(2)}, u32[]{:S(2)}) collective-permute-start(bf16[192,1152]{1,0:T(8,128)(2,1)S(1)} %collective-permute-done.3.refs_1_), channel_id=1, source_target_pairs={{0,4},{4,0},{8,12},{12,8},{16,20},{20,16},{24,28},{28,24},{1,5},{5... | collective-permute-start | bytes 1327112 | tf_op jit(solution)/shard_map/ppermute | solution.py:67
  33.2 17.6 %collective-permute-start.6 = (bf16[192,1152]{1,0:T(8,128)(2,1)S(1)}, bf16[192,1152]{1,0:T(8,128)(2,1)S(1)}, u32[]{:S(2)}, u32[]{:S(2)}) collective-permute-start(bf16[192,1152]{1,0:T(8,128)(2,1)S(1)} %collective-permute-done.3.refs_1_), channel_id=1, source_target_pairs={{0,8},{4,12},{8,16},{12,20},{16,24},{20,28},{24,0},{28,4},{1,9},{5... | collective-permute-start | bytes 1327112 | tf_op jit(solution)/shard_map/ppermute | solution.py:67
  68.3 55.8 %all-to-all-start.2 = ((bf16[4,192,1280]{2,1,0:T(8,128)(2,1)}), bf16[4,192,1280]{2,1,0:T(8,128)(2,1)S(1)}, u32[]{:S(2)}, u32[]{:S(2)}) async-start(bf16[4,192,1280]{2,1,0:T(8,128)(2,1)} %pack_experts.1), calls=%async_computation.2 | async-start | bytes 3932160 | tf_op jit(solution)/shard_map/all_to_all | solution.py:856
  79.4 17.8 %collective-permute-start.13 = (bf16[5,64,1536]{2,1,0:T(8,128)(2,1)}, bf16[5,64,1536]{2,1,0:T(8,128)(2,1)}, u32[]{:S(2)}, u32[]{:S(2)}) collective-permute-start(bf16[5,64,1536]{2,1,0:T(8,128)(2,1)} %refs_20_), channel_id=1, source_target_pairs={{0,4},{4,0},{8,12},{12,8},{16,20},{20,16},{24,28},{28,24},{1,5},{5... | collective-permute-start | bytes 2949128 | tf_op jit(solution)/shard_map/ppermute | solution.py:67
  139.6 18.2 %collective-permute-start.22 = (bf16[128,3200]{1,0:T(8,128)(2,1)S(1)}, bf16[128,3200]{1,0:T(8,128)(2,1)S(1)}, u32[]{:S(2)}, u32[]{:S(2)}) collective-permute-start(bf16[128,3200]{1,0:T(8,128)(2,1)S(1)} %constant_dynamic-update-slice_fusion.refs_1_.refs_9_), channel_id=1, source_target_pairs={{0,2},{1,3},{2,0},{3,1},{4,6},{5,7},{6,4},{7,5},{8,10},{9,11},{10,... | collective-permute-start | bytes 2457608 | tf_op jit(solution)/shard_map/ppermute | solution.py:67
  141.0 19.6 %collective-permute-start.21 = (bf16[128,3200]{1,0:T(8,128)(2,1)S(1)}, bf16[128,3200]{1,0:T(8,128)(2,1)S(1)}, u32[]{:S(2)}, u32[]{:S(2)}) collective-permute-start(bf16[128,3200]{1,0:T(8,128)(2,1)S(1)} %constant_dynamic-update-slice_fusion.refs_1_.refs_9_), channel_id=1, source_target_pairs={{0,8},{4,12},{8,16},{12,20},{16,24},{20,28},{24,0},{28,4},{1,9},{5... | collective-permute-start | bytes 2457608 | tf_op jit(solution)/shard_map/ppermute | solution.py:67
  141.0 42.5 %collective-permute-start.27 = (bf16[4,192,1280]{2,1,0:T(8,128)(2,1)S(1)}, bf16[4,192,1280]{2,1,0:T(8,128)(2,1)}, u32[]{:S(2)}, u32[]{:S(2)}) collective-permute-start(bf16[4,192,1280]{2,1,0:T(8,128)(2,1)S(1)} %all-to-all-done.2.refs_16_), channel_id=1, source_target_pairs={{0,4},{4,0},{8,12},{12,8},{16,20},{20,16},{24,28},{28,24},{1,5},{5... | collective-permute-start | bytes 5898248 | tf_op jit(solution)/shard_map/ppermute | solution.py:67
  142.4 41.1 %collective-permute-start.26 = (bf16[4,192,1280]{2,1,0:T(8,128)(2,1)S(1)}, bf16[4,192,1280]{2,1,0:T(8,128)(2,1)S(1)}, u32[]{:S(2)}, u32[]{:S(2)}) collective-permute-start(bf16[4,192,1280]{2,1,0:T(8,128)(2,1)S(1)} %all-to-all-done.2.refs_16_), channel_id=1, source_target_pairs={{0,1},{1,0},{2,3},{3,2},{4,5},{5,4},{6,7},{7,6},{8,9},{9,8},{10,11... | collective-permute-start | bytes 5898248 | tf_op jit(solution)/shard_map/ppermute | solution.py:67
  160.7 18.9 %collective-permute-start.23 = (bf16[128,3200]{1,0:T(8,128)(2,1)S(1)}, bf16[128,3200]{1,0:T(8,128)(2,1)S(1)}, u32[]{:S(2)}, u32[]{:S(2)}) collective-permute-start(bf16[128,3200]{1,0:T(8,128)(2,1)S(1)} %collective-permute-done.21.refs_2_.refs_10_), channel_id=1, source_target_pairs={{0,8},{4,12},{8,16},{12,20},{16,24},{20,28},{24,0},{28,4},{1,9},{5... | collective-permute-start | bytes 2457608 | tf_op jit(solution)/shard_map/ppermute | solution.py:67
  245.0 20.4 %collective-permute-start.29 = (bf16[128,3328]{1,0:T(8,128)(2,1)}, bf16[128,3328]{1,0:T(8,128)(2,1)S(1)}, u32[]{:S(2)}, u32[]{:S(2)}) collective-permute-start(bf16[128,3328]{1,0:T(8,128)(2,1)} %get-tuple-element.250), channel_id=1, source_target_pairs={{0,2},{1,3},{2,0},{3,1},{4,6},{5,7},{6,4},{7,5},{8,10},{9,11},{10,... | collective-permute-start | bytes 2555912 | tf_op jit(solution)/shard_map/ppermute | solution.py:67
  267.0 22.4 %collective-permute-start.30 = (bf16[128,3328]{1,0:T(8,128)(2,1)S(1)}, bf16[128,3328]{1,0:T(8,128)(2,1)S(1)}, u32[]{:S(2)}, u32[]{:S(2)}) collective-permute-start(bf16[128,3328]{1,0:T(8,128)(2,1)S(1)} %pad_maximum_fusion.1), channel_id=1, source_target_pairs={{0,8},{4,12},{8,16},{12,20},{16,24},{20,28},{24,0},{28,4},{1,9},{5... | collective-permute-start | bytes 2555912 | tf_op jit(solution)/shard_map/ppermute | solution.py:67
  267.8 21.6 %collective-permute-start.31 = (bf16[128,3328]{1,0:T(8,128)(2,1)S(1)}, bf16[128,3328]{1,0:T(8,128)(2,1)S(1)}, u32[]{:S(2)}, u32[]{:S(2)}) collective-permute-start(bf16[128,3328]{1,0:T(8,128)(2,1)S(1)} %copy-done.57), channel_id=1, source_target_pairs={{0,2},{1,3},{2,0},{3,1},{4,6},{5,7},{6,4},{7,5},{8,10},{9,11},{10,... | collective-permute-start | bytes 2555912 | tf_op jit(solution)/shard_map/ppermute | solution.py:67
  289.9 21.5 %collective-permute-start.33 = (bf16[128,3328]{1,0:T(8,128)(2,1)S(1)}, bf16[128,3328]{1,0:T(8,128)(2,1)S(1)}, u32[]{:S(2)}, u32[]{:S(2)}) collective-permute-start(bf16[128,3328]{1,0:T(8,128)(2,1)S(1)} %pad_maximum_fusion.2), channel_id=1, source_target_pairs={{0,8},{4,12},{8,16},{12,20},{16,24},{20,28},{24,0},{28,4},{1,9},{5... | collective-permute-start | bytes 2555912 | tf_op jit(solution)/shard_map/ppermute | solution.py:67
  290.8 20.6 %collective-permute-start.34 = (bf16[128,3328]{1,0:T(8,128)(2,1)S(1)}, bf16[128,3328]{1,0:T(8,128)(2,1)S(1)}, u32[]{:S(2)}, u32[]{:S(2)}) collective-permute-start(bf16[128,3328]{1,0:T(8,128)(2,1)S(1)} %copy-done.56), channel_id=1, source_target_pairs={{0,2},{1,3},{2,0},{3,1},{4,6},{5,7},{6,4},{7,5},{8,10},{9,11},{10,... | collective-permute-start | bytes 2555912 | tf_op jit(solution)/shard_map/ppermute | solution.py:67
  292.4 18.0 %collective-permute-start.35 = (bf16[4,192,512]{2,1,0:T(8,128)(2,1)S(1)}, bf16[4,192,512]{2,1,0:T(8,128)(2,1)S(1)}, u32[]{:S(2)}, u32[]{:S(2)}) collective-permute-start(bf16[4,192,512]{2,1,0:T(8,128)(2,1)S(1)} %get-tuple-element.403), channel_id=1, source_target_pairs={{0,4},{4,0},{8,12},{12,8},{16,20},{20,16},{24,28},{28,24},{1,5},{5... | collective-permute-start | bytes 2359304 | tf_op jit(solution)/shard_map/ppermute | solution.py:67
  313.2 34.0 %collective-permute-start.43 = (bf16[4,192,256]{2,1,0:T(8,128)(2,1)S(1)}, bf16[4,192,256]{2,1,0:T(8,128)(2,1)S(1)}, u32[]{:S(2)}, u32[]{:S(2)}) collective-permute-start(bf16[4,192,256]{2,1,0:T(8,128)(2,1)S(1)} %slice.176), channel_id=1, source_target_pairs={{0,4},{4,0},{8,12},{12,8},{16,20},{20,16},{24,28},{28,24},{1,5},{5... | collective-permute-start | bytes 1179656 | tf_op jit(solution)/shard_map/ppermute | solution.py:67
  314.9 26.2 %collective-permute-start.38 = (bf16[4,192,512]{2,1,0:T(8,128)(2,1)S(1)}, bf16[4,192,512]{2,1,0:T(8,128)(2,1)S(1)}, u32[]{:S(2)}, u32[]{:S(2)}) collective-permute-start(bf16[4,192,512]{2,1,0:T(8,128)(2,1)S(1)} %get-tuple-element.402), channel_id=1, source_target_pairs={{0,4},{4,0},{8,12},{12,8},{16,20},{20,16},{24,28},{28,24},{1,5},{5... | collective-permute-start | bytes 2359304 | tf_op jit(solution)/shard_map/ppermute | solution.py:67
  315.5 25.6 %collective-permute-start.36 = (bf16[128,3328]{1,0:T(8,128)(2,1)S(1)}, bf16[128,3328]{1,0:T(8,128)(2,1)S(1)}, u32[]{:S(2)}, u32[]{:S(2)}) collective-permute-start(bf16[128,3328]{1,0:T(8,128)(2,1)S(1)} %pad_maximum_fusion.3), channel_id=1, source_target_pairs={{0,8},{4,12},{8,16},{12,20},{16,24},{20,28},{24,0},{28,4},{1,9},{5... | collective-permute-start | bytes 2555912 | tf_op jit(solution)/shard_map/ppermute | solution.py:67
  316.4 24.7 %collective-permute-start.37 = (bf16[128,3328]{1,0:T(8,128)(2,1)S(1)}, bf16[128,3328]{1,0:T(8,128)(2,1)S(1)}, u32[]{:S(2)}, u32[]{:S(2)}) collective-permute-start(bf16[128,3328]{1,0:T(8,128)(2,1)S(1)} %copy-done.55), channel_id=1, source_target_pairs={{0,2},{1,3},{2,0},{3,1},{4,6},{5,7},{6,4},{7,5},{8,10},{9,11},{10,... | collective-permute-start | bytes 2555912 | tf_op jit(solution)/shard_map/ppermute | solution.py:67
  357.4 48.4 %all-to-all-start.3 = ((bf16[4,192,1280]{2,1,0:T(8,128)(2,1)}), bf16[4,192,1280]{2,1,0:T(8,128)(2,1)S(1)}, u32[]{:S(2)}, u32[]{:S(2)}) async-start(bf16[4,192,1280]{2,1,0:T(8,128)(2,1)} %pad_maximum_fusion), calls=%async_computation.3 | async-start | bytes 3932160 | tf_op jit(solution)/shard_map/all_to_all | solution.py:1029
  361.0 29.7 %collective-permute-start.40 = (bf16[5,64,1536]{2,1,0:T(8,128)(2,1)}, bf16[5,64,1536]{2,1,0:T(8,128)(2,1)}, u32[]{:S(2)}, u32[]{:S(2)}) collective-permute-start(bf16[5,64,1536]{2,1,0:T(8,128)(2,1)} %get-tuple-element.287), channel_id=1, source_target_pairs={{0,4},{4,0},{8,12},{12,8},{16,20},{20,16},{24,28},{28,24},{1,5},{5... | collective-permute-start | bytes 2949128 | tf_op jit(solution)/shard_map/ppermute | solution.py:67
  455.0 22.7 %all-to-all-start.4 = ((f32[4,48,768]{2,1,0:T(8,128)}), f32[4,48,768]{2,1,0:T(8,128)S(1)}, u32[]{:S(2)}, u32[]{:S(2)}) async-start(f32[4,48,768]{2,1,0:T(8,128)} %bitcast.106), calls=%async_computation.4 | async-start | bytes 1179648 | tf_op jit(solution)/shard_map/all_to_all | solution.py:1082
  (97 other events, 1481.5 us)

commit v4 on v3

--- a/solution.py
+++ b/solution.py
@@ -329,11 +329,11 @@
         query = qkv_ref[0, :, head * HEAD_DIM : (head + 1) * HEAD_DIM]
         key = qkv_ref[0, :, key_at : key_at + HEAD_DIM]
         value = qkv_ref[0, :, value_at : value_at + HEAD_DIM]
-        scores = dot(query, key, ((1,), (1,))) * SCORE_SCALE + bias
+        scores = dot(query * SCORE_SCALE, key, ((1,), (1,))) + bias
         highest = jnp.max(scores, -1, keepdims=True)
         exponent = jnp.exp(scores - highest)
         total = jnp.sum(exponent, -1, keepdims=True)
-        weights = (exponent / total).astype(BF16)
+        weights = (exponent * (1.0 / total)).astype(BF16)
         merged_ref[0, :, head * HEAD_DIM : (head + 1) * HEAD_DIM] = dot(weights, value).astype(BF16)
         sums = jnp.where(lane == head, highest + jnp.log(total), sums)
     lse_ref[0] = sums
@@ -368,24 +368,24 @@
     for group in range(kv_heads):
         key_at = (heads + group) * HEAD_DIM
         value_at = rotated + group * HEAD_DIM
-        key = qkv_ref[0, :, key_at : key_at + HEAD_DIM]
+        key = qkv_ref[0, :, key_at : key_at + HEAD_DIM] * SCORE_SCALE
         value = qkv_ref[0, :, value_at : value_at + HEAD_DIM]
         grad_key, grad_value = None, None
         for head in range(group * share, (group + 1) * share):
             query = qkv_ref[0, :, head * HEAD_DIM : (head + 1) * HEAD_DIM]
             grad_rows = grad_merged[:, head * HEAD_DIM : (head + 1) * HEAD_DIM]
-            scores = dot(query, key, ((1,), (1,))) * SCORE_SCALE + bias
+            scores = dot(query, key, ((1,), (1,))) + bias
             chance = jnp.exp(scores - lse_ref[0, :, head : head + 1])
             weights = chance.astype(BF16)
             grad_chance = dot(grad_rows, value, ((1,), (1,)))
             delta = jnp.sum(chance * grad_chance, -1, keepdims=True)
-            grad_raw = (chance * (grad_chance - delta) * SCORE_SCALE).astype(BF16)
+            grad_raw = (chance * (grad_chance - delta)).astype(BF16)
             turned_ref[:, head * HEAD_DIM : (head + 1) * HEAD_DIM] = dot(grad_raw, key)
             key_part = dot(grad_raw, query, ((0,), (0,)))
             value_part = dot(weights, grad_rows, ((0,), (0,)))
             grad_key = key_part if grad_key is None else grad_key + key_part
             grad_value = value_part if grad_value is None else grad_value + value_part
-        turned_ref[:, key_at : key_at + HEAD_DIM] = grad_key
+        turned_ref[:, key_at : key_at + HEAD_DIM] = grad_key * SCORE_SCALE
         dqkv_ref[micro, :, value_at : value_at + HEAD_DIM] = grad_value.astype(BF16)
     back = rotate_pairs(turned_ref[...], cos_ref[0], sin_ref[0], -1)
     dqkv_ref[micro, :, :rotated] = back.astype(BF16)
@@ -526,9 +526,11 @@
     dn_parts, refs = refs[: cores * ys], refs[cores * ys :]
     wr_ref, gate_ref, x_out, gm_out = refs[:4]
     back_outs, refs = refs[4 : 4 + slots], refs[4 + slots :]
+    mixed_outs, refs = refs[:slots], refs[slots:]
     act_outs, refs = refs[:cores], refs[cores:]
     dgu_outs, refs = refs[:cores], refs[cores:]
-    x_ref, gm_ref, mask_ref, wgu_ref, wdn_ref, act_ref, dgu_ref, back_ref, in_sems, out_sems = refs
+    x_ref, gm_ref, mask_ref, wgu_ref, wdn_ref, act_ref, dgu_ref, back_ref, mixed_ref = refs[:9]
+    in_sems, out_sems = refs[9:]
     rows, width = x_slots[0].shape[0], x_ref.shape[1]
     part = width // (ys * zs)
     wide, tall = 2 * hidden * own, hidden * own
@@ -614,24 +616,22 @@
         leave(act_ref.at[c], act_outs[c])
 
     coarse = picked.astype(BF16)
-    back_ref[:, 2 * width : 2 * width + LANES] = coarse
-    back_ref[:, 2 * width + LANES :] = (picked - coarse.astype(F32)).astype(BF16)
+    back_ref[:, width : width + LANES] = coarse
+    back_ref[:, width + LANES :] = (picked - coarse.astype(F32)).astype(BF16)
     back_ref[:, :width] = dot(dgu_ref[...], wgu_ref[...], ((1,), (1,))).astype(BF16)
 
-    def leave_back(low, count):
+    def leave_slots(source, goals):
         for i in range(slots):
-            source = back_ref.at[pl.ds(i * rows, rows), pl.ds(low, count)]
-            leave(source, back_outs[i].at[:, pl.ds(low, count)])
-
-    leave_back(0, width)
-    leave_back(2 * width, 2 * LANES)
+            leave(source.at[pl.ds(i * rows, rows), :], goals[i])
+
+    leave_slots(back_ref, back_outs)
     if tall % LANES == 0:
         acts = jnp.concatenate([act_ref[c] for c in range(cores)], 1)
         mixed = dot(acts, wdn_ref[...])
     else:
         mixed = sum(dot(act_ref[c], wdn_ref[c * tall : (c + 1) * tall, :]) for c in range(cores))
-    back_ref[:, width : 2 * width] = mixed.astype(BF16)
-    leave_back(width, width)
+    mixed_ref[...] = mixed.astype(BF16)
+    leave_slots(mixed_ref, mixed_outs)
     for copy in leaving:
         copy.wait()
 
@@ -645,7 +645,8 @@
         jax.ShapeDtypeStruct((total, width), BF16),
         jax.ShapeDtypeStruct((total, width), BF16),
     ]
-    outs += [jax.ShapeDtypeStruct((rows, 2 * width + 2 * LANES), BF16) for _ in x_slots]
+    outs += [jax.ShapeDtypeStruct((rows, width + 2 * LANES), BF16) for _ in x_slots]
+    outs += [jax.ShapeDtypeStruct((rows, width), BF16) for _ in x_slots]
     outs += [jax.ShapeDtypeStruct((total, own * hidden), BF16) for _ in range(cores)]
     outs += [jax.ShapeDtypeStruct((total, 2 * own * hidden), BF16) for _ in range(cores)]
     joined = [slot.shape[1] > width for slot in x_slots]
@@ -665,9 +666,10 @@
             pltpu.VMEM((cores * own * hidden, width), BF16),
             pltpu.VMEM((cores, total, own * hidden), BF16),
             pltpu.VMEM((total, cores * own * 2 * hidden), BF16),
-            pltpu.VMEM((total, 2 * width + 2 * LANES), BF16),
+            pltpu.VMEM((total, width + 2 * LANES), BF16),
+            pltpu.VMEM((total, width), BF16),
             pltpu.SemaphoreType.DMA((copies,)),
-            pltpu.SemaphoreType.DMA((2 + 2 * cores + 3 * len(x_slots),)),
+            pltpu.SemaphoreType.DMA((2 + 2 * cores + 2 * len(x_slots),)),
         ],
         compiler_params=pltpu.CompilerParams(vmem_limit_bytes=60 << 20),
         name="experts",
@@ -950,11 +952,13 @@
         for i in range(chunks)
     ]
     back = [part for pieces in results for part in pieces[3 : 3 + chunk]]
-    results = [pieces[:3] + pieces[3 + chunk :] for pieces in results]
+    mixed = [part for pieces in results for part in pieces[3 + chunk : 3 + 2 * chunk]]
+    results = [pieces[:3] + pieces[3 + 2 * chunk :] for pieces in results]
     results = [pieces[0] if chunks == 1 else jnp.concatenate(pieces, 0) for pieces in zip(*results)]
     gates, x_all, gm_all = results[:3]
     acts, dgus = results[3 : 3 + cn], results[3 + cn :]
     back = [back[i * zn : (i + 1) * zn] for i in range(xn)]
+    mixed = [mixed[i * zn : (i + 1) * zn] for i in range(xn)]
 
     def by_y(value, axis):
         return [lax.dynamic_index_in_dim(value, rings.origin("y", s), axis, False) for s in range(yn)]
@@ -973,38 +977,46 @@
         value = product(0, 1, None, gm, coming)
         return by_y(value.reshape(own_experts, yn, hidden_part // yn, width), 1)
 
+    def held(*values):
+        return phases.start(make(lambda: values))
+
     rows_back = phases.start(rings.reduce_two(back, "z", "x", two_part))
+    x, gm, coming = x_all, gm_all, [None, None]
     if cn > 1:
-        work = phases.start(make(lambda: (product(1, 0, x_all, None, None), x_all, gm_all)))
+        work = held(product(1, 0, x, None, None), x, gm)
         phases.phase()
         other, x, gm = work.result
-        coming = rings.step(other, "c")
-    else:
-        x, gm, coming = x_all, gm_all, None
-    work = phases.start(make(lambda: (own_gu(x, coming), gm)))
+        coming[0] = rings.step(other, "c")
+    first = min(1, zn - 1)
+    other = [product(1, 1, None, gm, None)] if cn > 1 else []
+    work = held(own_gu(x, coming[0]), other, gm, [row[first] for row in mixed])
     phases.phase()
-    made, gm = work.result
-    groups = [(0, 2), (2, 4), (4, own_experts)] if own_experts > 4 else [(0, own_experts)]
+    made, other, gm, mixed_first = work.result
+    if cn > 1:
+        coming[1] = rings.step(other[0], "c")
+    groups = [(0, 2), (2, 4), (4, 5)] if own_experts == 5 else [(0, own_experts)]
     wide = 2 * hidden_part
-    made = [[part[:, :, low * wide : high * wide] for part in made] for low, high in groups]
+    waiting = [[part[:, :, low * wide : high * wide] for part in made] for low, high in groups]
     grad_gu = []
 
-    def next_group():
-        if len(grad_gu) < len(groups):
-            grad_gu.append(phases.start(rings.reduce(made[len(grad_gu)], "y")))
-
-    next_group()
-    if cn > 1:
-        work = phases.start(make(lambda: (product(1, 1, None, gm, None), gm)))
+    def next_group(*keep):
+        nonlocal waiting
+        if waiting:
+            grad_gu.append(phases.start(rings.reduce(waiting[0], "y")))
+            waiting = waiting[1:]
+        work = held(waiting, *keep)
         phases.phase()
-        other, gm = work.result
-        coming = rings.step(other, "c")
-    next_group()
-    work = phases.start(make(lambda: own_dn(gm, coming)))
-    phases.finish(rows_back, work)
-    grad_dn = work.result
-    grad_dealt, moe_rows = rows_back.result[:, :width], rows_back.result[:, width : 2 * width]
-    grad_gates = rows_back.result[:, 2 * width :]
+        waiting, *keep = work.result
+        return keep
+
+    for row, value in zip(mixed, mixed_first):
+        row[first] = value
+    moe_rows = phases.start(rings.reduce_two(mixed, "z", "x"))
+    (gm, *coming) = next_group(gm, *([coming[1]] if cn > 1 else []))
+    (grad_dn,) = next_group(own_dn(gm, coming[0] if coming else None))
+    phases.finish(rows_back)
+    grad_dealt = rows_back.result[:, :width]
+    grad_gates = rows_back.result[:, width:]
     grad_gates = grad_gates[:, :LANES] + grad_gates[:, LANES:]
     own_gates = gates[:home_rows]
     grad_picked = own_gates * (grad_gates - jnp.sum(own_gates * grad_gates, -1, keepdims=True))
@@ -1020,15 +1032,14 @@
     grad_attn = (RESIDUAL_SCALE * grad_hidden).astype(BF16)
 
     grad_attn = over_members(grad_attn)
-    grad_dn = rings.reduce(grad_dn, "y")
-    made_dn = next(grad_dn)
-    while len(grad_gu) < len(groups):
+    while waiting:
         next_group()
-    phases.phase()
     grad_gu = jnp.concatenate([part.astype(BF16) for part in phases.finish(*grad_gu)], 2)
+    work = held(grad_gu, grad_dn)
+    phases.finish(grad_attn, moe_rows, work)
+    grad_gu, grad_dn = work.result
     grad_gu = lax.all_to_all(grad_gu, "dp", 0, 0, axis_index_groups=rings.z_groups)
-    phases.finish(grad_attn)
-    grad_dn = phases.start(resumed(grad_dn, made_dn))
+    grad_dn = phases.start(rings.reduce(grad_dn, "y"))
 
     attention = phases.start(
         make(
@@ -1061,13 +1072,13 @@
     both = phases.start(
         rings.reduce_two([[weight_grads[s * zn + t] for t in range(zn)] for s in range(yn)], "z", "y")
     )
-    grad_gu = phases.start(make(lambda: grad_gu))
     phases.phase()
+    grad_gu = held(grad_gu)
     grad_normed_first = sum_members(first_parts)
-    both, grad_gu, grad_dn, grad_normed_first = phases.finish(
-        both, grad_gu, grad_dn, grad_normed_first
+    both, grad_gu, grad_dn, grad_normed_first, moe_rows = phases.finish(
+        both, grad_gu, grad_dn, grad_normed_first, moe_rows
     )
-    grad_gate, grad_up = unpack_experts(grad_gu, own_experts)
+    grad_gate, grad_up = unpack_experts(grad_gu[0], own_experts)
     moe_rows = moe_rows.astype(BF16).reshape(micros, rows, width)
     output = (hidden + RESIDUAL_SCALE * moe_rows.astype(F32)).astype(BF16)
     scaled_first = grad_normed_first * gain_first
@@ -1077,9 +1088,9 @@
     grad_out = [
         both[i * weight_rows : (i + 1) * weight_rows, small_at:] for i in range(members)
     ]
-    grad_out = lax.ppermute(jnp.concatenate(grad_out, 1), ALL, to_home)
+    grad_out = lax.ppermute(jnp.concatenate(grad_out, 1).astype(BF16), ALL, to_home).astype(F32)
     home = both[:, :small_at].reshape(members, weight_rows, small_at)
-    home = lax.all_to_all(home, "expert", 0, 0)
+    home = lax.all_to_all(home.astype(BF16), "expert", 0, 0).astype(F32)
 
     def columns(start, count):
         return jnp.concatenate([home[i, :, start : start + count] for i in range(members)], 1)

time: 491 us -> 479 us (0.976)
  waiting for transfers between devices: 229 us -> 204 us
  starting transfers between devices: 94.9 us -> 106 us
    ppermute x54 -> x61, waiting for transfers between devices: 202 us -> 176 us  [step(): return lax.ppermute(value, axis, pairs)]
    ppermute x54 -> x61, starting transfers between devices: 64.6 us -> 74.9 us  [step(): return lax.ppermute(value, axis, pairs)]
    all_to_all x1, waiting for transfers between devices: 6.02 us -> 12 us  [per_device(): lax.all_to_all(grad_gu, 'dp', 0, 0, axis_index_groups=rings.z_groups)]
    ppermute x1, waiting for transfers between devices: 10.2 us -> 5.17 us  [per_device(): lax.ppermute(jnp.concatenate(grad_out, 1).astype(BF16), ALL, to_home)]
    unnamed x126 -> x141, local copies, waits for them, and re-layouts: 12.7 us -> 11.9 us
  transfers between devices with their start and end apart: 61 -> 68, of which waited for: 38 -> 40; matrix products, arithmetic and copies ran while one was open for 10% -> 11% of each run, Pallas kernels for 9% -> 9%
where the time goes in v4:
time: 479 us; the launch traced here: 471 us
  waiting for transfers between devices  204 us (43%)
  starting transfers between devices  106 us (22%)
  Pallas kernels  80.8 us (17%)
  other arithmetic  34.6 us (7%)
  local copies, waits for them, and re-layouts  21.8 us (5%)
  matrix products  21.7 us (5%)
    ppermute x61, waiting for transfers between devices, step(): return lax.ppermute(value, axis, pairs)  176 us
    ppermute x61, starting transfers between devices, step(): return lax.ppermute(value, axis, pairs)  74.9 us
    pallas_call x1, Pallas kernels, run_experts(): pl.pallas_call(functools.partial(experts_kernel, shape), in_specs=[pl.Blo...  38.5 us
    dot_general x5, matrix products, dot(): return lax.dot_general(a, b, (dims, ((), ())), preferred_element_type=F32)  21.5 us
    pallas_call x1, Pallas kernels, attention_backward(): pl.pallas_call(functools.partial(attention_backward_kernel, shape), grid_...  19.2 us
    pallas_call x1, Pallas kernels, attention_forward(): pl.pallas_call(functools.partial(attention_forward_kernel, shape), grid_s...  13.7 us
    all_to_all x1, waiting for transfers between devices, per_device(): lax.all_to_all(grad_gu, 'dp', 0, 0, axis_index_groups=rings.z_groups)  12 us
    unnamed x141, local copies, waits for them, and re-layouts  11.9 us
  transfers between devices with their start and end apart: 68, of which 40 were waited for; matrix products, arithmetic and copies ran while one was open for 11% of the time, Pallas kernels for 9%

profile of v4, /device:TPU:3, one launch (start us, length us, event | category | flops | bytes accessed | tf_op | source)
XLA Modules:
  0.0 471.1 jit_solution(1617128038958658332)
XLA Ops:
  24.2 6.1 %collective-permute-done.4.refs_4_ = bf16[192,1152]{1,0:T(8,128)(2,1)S(1)} collective-permute-done((bf16[192,1152]{1,0:T(8,128)(2,1)S(1)}, bf16[192,1152]{1,0:T(8,128)(2,1)S(1)}, u32[]{:S(2)}, u32[]{:S(2)}) %collective-permute-start.4) | collective-permute-done | bytes 442400 | tf_op jit(solution)/shard_map/ppermute | solution.py:67
  55.7 5.5 %collective-permute-done.9.refs_6_ = bf16[192,1152]{1,0:T(8,128)(2,1)S(1)} collective-permute-done((bf16[192,1152]{1,0:T(8,128)(2,1)S(1)}, bf16[192,1152]{1,0:T(8,128)(2,1)S(1)}, u32[]{:S(2)}, u32[]{:S(2)}) %collective-permute-start.9) | collective-permute-done | bytes 442400 | tf_op jit(solution)/shard_map/ppermute | solution.py:67
  81.8 13.7 %attention_forward.1 = (bf16[2,64,1536]{2,1,0:T(8,128)(2,1)}, bf16[2,64,1536]{2,1,0:T(8,128)(2,1)}, bf16[2,64,1536]{2,1,0:T(8,128)(2,1)}, bf16[2,64,1536]{2,1,0:...) custom-call(s32[8]{0:T(128)} %stack.41.spots_ref, ...), custom_call_target="tpu_custom_call" | custom-call | tf_op jit(solution)/shard_map/attention_forward/pallas_call | solution.py:464
  97.3 6.9 %collective-permute-start.14 = (bf16[5,64,1536]{2,1,0:T(8,128)(2,1)}, bf16[5,64,1536]{2,1,0:T(8,128)(2,1)}, u32[]{:S(2)}, u32[]{:S(2)}) collective-permute-start(bf16[5,64,1536]{2,1,0:T(8,128)(2,1)} %refs_20_), channel_id=1, source_target_pairs={{0,1},{1,0},{2,3},{3,2},{4,5},{5,4},{6,7},{7,6},{8,9},{9,8},{10,11... | collective-permute-start | bytes 2949128 | tf_op jit(solution)/shard_map/ppermute | solution.py:67
  111.7 8.5 %collective-permute-done.17 = bf16[2,64,1536]{2,1,0:T(8,128)(2,1)S(1)} collective-permute-done((bf16[2,64,1536]{2,1,0:T(8,128)(2,1)S(1)}, bf16[2,64,1536]{2,1,0:T(8,128)(2,1)S(1)}, u32[]{:S(2)}, u32[]{:S(2)}) %collective-permute-start.17) | collective-permute-done | bytes 393248 | tf_op jit(solution)/shard_map/ppermute | solution.py:67
  126.8 10.1 %collective-permute-done.20.refs_4_ = bf16[128,1536]{1,0:T(8,128)(2,1)S(1)} collective-permute-done((bf16[128,1536]{1,0:T(8,128)(2,1)S(1)}, bf16[128,1536]{1,0:T(8,128)(2,1)S(1)}, u32[]{:S(2)}, u32[]{:S(2)}) %collective-permute-start.20) | collective-permute-done | bytes 393248 | tf_op jit(solution)/shard_map/ppermute | solution.py:67
  144.7 13.2 %collective-permute-done.22.refs_5_.refs_13_ = bf16[128,3200]{1,0:T(8,128)(2,1)S(1)} collective-permute-done((bf16[128,3200]{1,0:T(8,128)(2,1)S(1)}, bf16[128,3200]{1,0:T(8,128)(2,1)S(1)}, u32[]{:S(2)}, u32[]{:S(2)}) %collective-permute-start.22) | collective-permute-done | bytes 819232 | tf_op jit(solution)/shard_map/ppermute | solution.py:67
  161.2 16.5 %collective-permute-done.24.refs_6_.refs_14_ = bf16[128,3200]{1,0:T(8,128)(2,1)S(1)} collective-permute-done((bf16[128,3200]{1,0:T(8,128)(2,1)S(1)}, bf16[128,3200]{1,0:T(8,128)(2,1)S(1)}, u32[]{:S(2)}, u32[]{:S(2)}) %collective-permute-start.24) | collective-permute-done | bytes 819232 | tf_op jit(solution)/shard_map/ppermute | solution.py:67
  183.5 11.7 %collective-permute-done.25.refs_7_.refs_15_ = bf16[128,3200]{1,0:T(8,128)(2,1)S(1)} collective-permute-done((bf16[128,3200]{1,0:T(8,128)(2,1)S(1)}, bf16[128,3200]{1,0:T(8,128)(2,1)S(1)}, u32[]{:S(2)}, u32[]{:S(2)}) %collective-permute-start.25) | collective-permute-done | bytes 819232 | tf_op jit(solution)/shard_map/ppermute | solution.py:67
  206.2 38.5 %experts.1 = (f32[1024,128]{1,0:T(8,128)}, bf16[1024,1536]{1,0:T(8,128)(2,1)}, bf16[1024,1536]{1,0:T(8,128)(2,1)}, bf16[128,1792]{1,0:T(8,128)(2,1)}, bf16[128,1...) custom-call(s32[12]{0:T(128)} %pad_add_fusion.1.table_ref, ...), custom_call_target="tpu_custom_call" | custom-call | tf_op jit(solution)/shard_map/experts/pallas_call | solution.py:656
  246.2 9.2 %convolution_convert_fusion = bf16[1536,1280]{1,0:T(8,128)(2,1)} fusion(bf16[1024,1536]{1,0:T(8,128)(2,1)} %get-tuple-element.296, bf16[1024,1280]{1,0:T(8,128)(2,1)} %get-tuple-element.288), kind=kOutput, calls=%fused_computation.1 | convolution fusion | flops 4028497920 | bytes 9699328 | tf_op jit(solution)/shard_map/dot_general | solution.py:27
  264.7 6.1 %fusion = bf16[1536,1280]{1,0:T(8,128)(2,1)S(1)} fusion(bf16[1536,1280]{1,0:T(8,128)(2,1)} %collective-permute-done.32, bf16[1024,1536]{1,0:T(8,128)(2,1)S(1)} %copy-done.59, bf16[1024,1280]{1,0:T(8,128)(2,1)S(1)} %copy-done.60), kind=kOutput, calls=%fused_computation.2 | convolution fusion | flops 4032430080 | bytes 13631488 | tf_op jit(solution)/shard_map/dot_general | solution.py:27
  276.8 18.6 %collective-permute-done.35 = bf16[128,1536]{1,0:T(8,128)(2,1)S(1)} collective-permute-done((bf16[128,1536]{1,0:T(8,128)(2,1)S(1)}, bf16[128,1536]{1,0:T(8,128)(2,1)S(1)}, u32[]{:S(2)}, u32[]{:S(2)}) %collective-permute-start.35) | collective-permute-done | bytes 393248 | tf_op jit(solution)/shard_map/ppermute | solution.py:67
  307.2 9.8 %collective-permute-done.38 = bf16[128,1792]{1,0:T(8,128)(2,1)S(1)} collective-permute-done((bf16[128,1792]{1,0:T(8,128)(2,1)S(1)}, bf16[128,1792]{1,0:T(8,128)(2,1)S(1)}, u32[]{:S(2)}, u32[]{:S(2)}) %collective-permute-start.38) | collective-permute-done | bytes 458784 | tf_op jit(solution)/shard_map/ppermute | solution.py:67
  326.9 9.9 %collective-permute-done.43 = bf16[128,1536]{1,0:T(8,128)(2,1)S(1)} collective-permute-done((bf16[128,1536]{1,0:T(8,128)(2,1)S(1)}, bf16[128,1536]{1,0:T(8,128)(2,1)S(1)}, u32[]{:S(2)}, u32[]{:S(2)}) %collective-permute-start.43) | collective-permute-done | bytes 393248 | tf_op jit(solution)/shard_map/ppermute | solution.py:67
  340.9 5.9 %collective-permute-done.48 = bf16[128,1536]{1,0:T(8,128)(2,1)S(1)} collective-permute-done((bf16[128,1536]{1,0:T(8,128)(2,1)S(1)}, bf16[128,1536]{1,0:T(8,128)(2,1)S(1)}, u32[]{:S(2)}, u32[]{:S(2)}) %collective-permute-start.48) | collective-permute-done | bytes 393248 | tf_op jit(solution)/shard_map/ppermute | solution.py:67
  348.3 5.7 %collective-permute-done.50.refs_11_ = bf16[2,64,1536]{2,1,0:T(8,128)(2,1)} collective-permute-done((bf16[2,64,1536]{2,1,0:T(8,128)(2,1)S(1)}, bf16[2,64,1536]{2,1,0:T(8,128)(2,1)}, u32[]{:S(2)}, u32[]{:S(2)}) %collective-permute-start.50) | collective-permute-done | bytes 393248 | tf_op jit(solution)/shard_map/ppermute | solution.py:67
  360.3 19.2 %attention_backward.1 = (bf16[2,64,1536]{2,1,0:T(8,128)(2,1)}, bf16[2,64,1536]{2,1,0:T(8,128)(2,1)}, bf16[2,64,1536]{2,1,0:T(8,128)(2,1)}, bf16[2,64,1536]{2,1,0...) custom-call(s32[8]{0:T(128)} %stack.41.spots_ref, ...), custom_call_target="tpu_custom_call" | custom-call | tf_op jit(solution)/shard_map/attention_backward/pallas_call | solution.py:490
  379.6 7.4 %collective-permute-done.52 = bf16[192,1152]{1,0:T(8,128)(2,1)S(1)} collective-permute-done((bf16[192,1152]{1,0:T(8,128)(2,1)}, bf16[192,1152]{1,0:T(8,128)(2,1)S(1)}, u32[]{:S(2)}, u32[]{:S(2)}) %collective-permute-start.52) | collective-permute-done | bytes 442400 | tf_op jit(solution)/shard_map/ppermute | solution.py:67
  391.1 5.9 %collective-permute-start.55 = (bf16[2,64,1536]{2,1,0:T(8,128)(2,1)}, bf16[2,64,1536]{2,1,0:T(8,128)(2,1)S(1)}, u32[]{:S(2)}, u32[]{:S(2)}) collective-permute-start(bf16[2,64,1536]{2,1,0:T(8,128)(2,1)} %get-tuple-element.389), channel_id=1, source_target_pairs={{0,1},{1,0},{2,3},{3,2},{4,5},{5,4},{6,7},{7,6},{8,9},{9,8},{10,11... | collective-permute-start | bytes 1179656 | tf_op jit(solution)/shard_map/ppermute | solution.py:67
  400.1 12.0 %all-to-all-done.3.in_ref = bf16[4,192,1280]{2,1,0:T(8,128)(2,1)S(1)} async-done(((bf16[4,192,1280]{2,1,0:T(8,128)(2,1)}), bf16[4,192,1280]{2,1,0:T(8,128)(2,1)S(1)}, u32[]{:S(2)}, u32[]{:S(2)}) %all-to-all-start.3) | async-done | bytes 1966112 | tf_op jit(solution)/shard_map/all_to_all | solution.py:1041
  424.7 7.1 %collective-permute-done.56 = bf16[192,1152]{1,0:T(8,128)(2,1)S(1)} collective-permute-done((bf16[192,1152]{1,0:T(8,128)(2,1)S(1)}, bf16[192,1152]{1,0:T(8,128)(2,1)S(1)}, u32[]{:S(2)}, u32[]{:S(2)}) %collective-permute-start.56) | collective-permute-done | bytes 442400 | tf_op jit(solution)/shard_map/ppermute | solution.py:67
  448.6 5.6 %all-to-all-start.4 = ((bf16[4,48,768]{2,1,0:T(8,128)(2,1)}), bf16[4,48,768]{2,1,0:T(8,128)(2,1)S(1)}, u32[]{:S(2)}, u32[]{:S(2)}) async-start(bf16[4,48,768]{2,1,0:T(8,128)(2,1)} %bitcast.107), calls=%async_computation.4 | async-start | bytes 589824 | tf_op jit(solution)/shard_map/all_to_all | solution.py:1093
  461.2 5.2 %collective-permute-done.62 = bf16[48,1536]{1,0:T(8,128)(2,1)S(1)} collective-permute-done((bf16[48,1536]{1,0:T(8,128)(2,1)S(1)}, bf16[48,1536]{1,0:T(8,128)(2,1)S(1)}, u32[]{:S(2)}, u32[]{:S(2)}) %collective-permute-start.62) | collective-permute-done | bytes 147488 | tf_op jit(solution)/shard_map/ppermute | solution.py:1091
  (355 shorter events, 210.8 us)
Async XLA Ops:
  0.7 20.1 %collective-permute-start = (bf16[2,64,1536]{2,1,0:T(8,128)(2,1)}, bf16[2,64,1536]{2,1,0:T(8,128)(2,1)S(1)}, u32[]{:S(2)}, u32[]{:S(2)}) collective-permute-start(bf16[2,64,1536]{2,1,0:T(8,128)(2,1)} %refs_8_.1), channel_id=1, source_target_pairs={{0,1},{1,0},{2,3},{3,2},{4,5},{5,4},{6,7},{7,6},{8,9},{9,8},{10,11... | collective-permute-start | bytes 1179656 | tf_op jit(solution)/shard_map/ppermute | solution.py:67
  1.4 19.4 %collective-permute-start.1 = (bf16[2,64,1536]{2,1,0:T(8,128)(2,1)}, bf16[2,64,1536]{2,1,0:T(8,128)(2,1)S(1)}, u32[]{:S(2)}, u32[]{:S(2)}) collective-permute-start(bf16[2,64,1536]{2,1,0:T(8,128)(2,1)} %refs_8_.1), channel_id=1, source_target_pairs={{0,2},{1,3},{2,0},{3,1},{4,6},{5,7},{6,4},{7,5},{8,10},{9,11},{10,... | collective-permute-start | bytes 1179656 | tf_op jit(solution)/shard_map/ppermute | solution.py:67
  33.2 17.6 %collective-permute-start.7 = (bf16[192,1152]{1,0:T(8,128)(2,1)S(1)}, bf16[192,1152]{1,0:T(8,128)(2,1)S(1)}, u32[]{:S(2)}, u32[]{:S(2)}) collective-permute-start(bf16[192,1152]{1,0:T(8,128)(2,1)S(1)} %collective-permute-done.3.refs_1_), channel_id=1, source_target_pairs={{0,4},{4,0},{8,12},{12,8},{16,20},{20,16},{24,28},{28,24},{1,5},{5... | collective-permute-start | bytes 1327112 | tf_op jit(solution)/shard_map/ppermute | solution.py:67
  33.2 17.6 %collective-permute-start.6 = (bf16[192,1152]{1,0:T(8,128)(2,1)S(1)}, bf16[192,1152]{1,0:T(8,128)(2,1)S(1)}, u32[]{:S(2)}, u32[]{:S(2)}) collective-permute-start(bf16[192,1152]{1,0:T(8,128)(2,1)S(1)} %collective-permute-done.3.refs_1_), channel_id=1, source_target_pairs={{0,8},{4,12},{8,16},{12,20},{16,24},{20,28},{24,0},{28,4},{1,9},{5... | collective-permute-start | bytes 1327112 | tf_op jit(solution)/shard_map/ppermute | solution.py:67
  68.3 55.8 %all-to-all-start.2 = ((bf16[4,192,1280]{2,1,0:T(8,128)(2,1)}), bf16[4,192,1280]{2,1,0:T(8,128)(2,1)S(1)}, u32[]{:S(2)}, u32[]{:S(2)}) async-start(bf16[4,192,1280]{2,1,0:T(8,128)(2,1)} %pack_experts.1), calls=%async_computation.2 | async-start | bytes 3932160 | tf_op jit(solution)/shard_map/all_to_all | solution.py:858
  79.4 17.8 %collective-permute-start.13 = (bf16[5,64,1536]{2,1,0:T(8,128)(2,1)}, bf16[5,64,1536]{2,1,0:T(8,128)(2,1)}, u32[]{:S(2)}, u32[]{:S(2)}) collective-permute-start(bf16[5,64,1536]{2,1,0:T(8,128)(2,1)} %refs_20_), channel_id=1, source_target_pairs={{0,4},{4,0},{8,12},{12,8},{16,20},{20,16},{24,28},{28,24},{1,5},{5... | collective-permute-start | bytes 2949128 | tf_op jit(solution)/shard_map/ppermute | solution.py:67
  139.6 18.2 %collective-permute-start.22 = (bf16[128,3200]{1,0:T(8,128)(2,1)S(1)}, bf16[128,3200]{1,0:T(8,128)(2,1)S(1)}, u32[]{:S(2)}, u32[]{:S(2)}) collective-permute-start(bf16[128,3200]{1,0:T(8,128)(2,1)S(1)} %constant_dynamic-update-slice_fusion.refs_1_.refs_9_), channel_id=1, source_target_pairs={{0,2},{1,3},{2,0},{3,1},{4,6},{5,7},{6,4},{7,5},{8,10},{9,11},{10,... | collective-permute-start | bytes 2457608 | tf_op jit(solution)/shard_map/ppermute | solution.py:67
  141.0 19.6 %collective-permute-start.21 = (bf16[128,3200]{1,0:T(8,128)(2,1)S(1)}, bf16[128,3200]{1,0:T(8,128)(2,1)S(1)}, u32[]{:S(2)}, u32[]{:S(2)}) collective-permute-start(bf16[128,3200]{1,0:T(8,128)(2,1)S(1)} %constant_dynamic-update-slice_fusion.refs_1_.refs_9_), channel_id=1, source_target_pairs={{0,8},{4,12},{8,16},{12,20},{16,24},{20,28},{24,0},{28,4},{1,9},{5... | collective-permute-start | bytes 2457608 | tf_op jit(solution)/shard_map/ppermute | solution.py:67
  141.0 42.5 %collective-permute-start.27 = (bf16[4,192,1280]{2,1,0:T(8,128)(2,1)S(1)}, bf16[4,192,1280]{2,1,0:T(8,128)(2,1)}, u32[]{:S(2)}, u32[]{:S(2)}) collective-permute-start(bf16[4,192,1280]{2,1,0:T(8,128)(2,1)S(1)} %all-to-all-done.2.refs_16_), channel_id=1, source_target_pairs={{0,4},{4,0},{8,12},{12,8},{16,20},{20,16},{24,28},{28,24},{1,5},{5... | collective-permute-start | bytes 5898248 | tf_op jit(solution)/shard_map/ppermute | solution.py:67
  142.4 41.1 %collective-permute-start.26 = (bf16[4,192,1280]{2,1,0:T(8,128)(2,1)S(1)}, bf16[4,192,1280]{2,1,0:T(8,128)(2,1)S(1)}, u32[]{:S(2)}, u32[]{:S(2)}) collective-permute-start(bf16[4,192,1280]{2,1,0:T(8,128)(2,1)S(1)} %all-to-all-done.2.refs_16_), channel_id=1, source_target_pairs={{0,1},{1,0},{2,3},{3,2},{4,5},{5,4},{6,7},{7,6},{8,9},{9,8},{10,11... | collective-permute-start | bytes 5898248 | tf_op jit(solution)/shard_map/ppermute | solution.py:67
  160.6 17.0 %collective-permute-start.24 = (bf16[128,3200]{1,0:T(8,128)(2,1)S(1)}, bf16[128,3200]{1,0:T(8,128)(2,1)S(1)}, u32[]{:S(2)}, u32[]{:S(2)}) collective-permute-start(bf16[128,3200]{1,0:T(8,128)(2,1)S(1)} %collective-permute-done.21.refs_2_.refs_10_), channel_id=1, source_target_pairs={{0,2},{1,3},{2,0},{3,1},{4,6},{5,7},{6,4},{7,5},{8,10},{9,11},{10,... | collective-permute-start | bytes 2457608 | tf_op jit(solution)/shard_map/ppermute | solution.py:67
  160.7 18.8 %collective-permute-start.23 = (bf16[128,3200]{1,0:T(8,128)(2,1)S(1)}, bf16[128,3200]{1,0:T(8,128)(2,1)S(1)}, u32[]{:S(2)}, u32[]{:S(2)}) collective-permute-start(bf16[128,3200]{1,0:T(8,128)(2,1)S(1)} %collective-permute-done.21.refs_2_.refs_10_), channel_id=1, source_target_pairs={{0,8},{4,12},{8,16},{12,20},{16,24},{20,28},{24,0},{28,4},{1,9},{5... | collective-permute-start | bytes 2457608 | tf_op jit(solution)/shard_map/ppermute | solution.py:67
  272.1 23.3 %collective-permute-start.37 = (bf16[640,1536]{1,0:T(8,128)(2,1)S(1)}, bf16[640,1536]{1,0:T(8,128)(2,1)S(1)}, u32[]{:S(2)}, u32[]{:S(2)}) collective-permute-start(bf16[640,1536]{1,0:T(8,128)(2,1)S(1)} %convolution_convert_fusion.1), channel_id=1, source_target_pairs={{0,1},{1,0},{2,3},{3,2},{4,5},{5,4},{6,7},{7,6},{8,9},{9,8},{10,11... | collective-permute-start | bytes 5898248 | tf_op jit(solution)/shard_map/ppermute | solution.py:67
  273.0 22.4 %collective-permute-start.36 = (bf16[4,192,512]{2,1,0:T(8,128)(2,1)S(1)}, bf16[4,192,512]{2,1,0:T(8,128)(2,1)S(1)}, u32[]{:S(2)}, u32[]{:S(2)}) collective-permute-start(bf16[4,192,512]{2,1,0:T(8,128)(2,1)S(1)} %get-tuple-element.471), channel_id=1, source_target_pairs={{0,4},{4,0},{8,12},{12,8},{16,20},{20,16},{24,28},{28,24},{1,5},{5... | collective-permute-start | bytes 2359304 | tf_op jit(solution)/shard_map/ppermute | solution.py:67
  275.0 20.4 %collective-permute-start.33 = (bf16[128,1792]{1,0:T(8,128)(2,1)S(1)}, bf16[128,1792]{1,0:T(8,128)(2,1)S(1)}, u32[]{:S(2)}, u32[]{:S(2)}) collective-permute-start(bf16[128,1792]{1,0:T(8,128)(2,1)S(1)} %pad_maximum_fusion.2), channel_id=1, source_target_pairs={{0,8},{4,12},{8,16},{12,20},{16,24},{20,28},{24,0},{28,4},{1,9},{5... | collective-permute-start | bytes 1376264 | tf_op jit(solution)/shard_map/ppermute | solution.py:67
  275.1 20.3 %collective-permute-start.34 = (bf16[128,1792]{1,0:T(8,128)(2,1)S(1)}, bf16[128,1792]{1,0:T(8,128)(2,1)S(1)}, u32[]{:S(2)}, u32[]{:S(2)}) collective-permute-start(bf16[128,1792]{1,0:T(8,128)(2,1)S(1)} %copy-done.62), channel_id=1, source_target_pairs={{0,2},{1,3},{2,0},{3,1},{4,6},{5,7},{6,4},{7,5},{8,10},{9,11},{10,... | collective-permute-start | bytes 1376264 | tf_op jit(solution)/shard_map/ppermute | solution.py:67
  276.3 19.1 %collective-permute-start.35 = (bf16[128,1536]{1,0:T(8,128)(2,1)S(1)}, bf16[128,1536]{1,0:T(8,128)(2,1)S(1)}, u32[]{:S(2)}, u32[]{:S(2)}) collective-permute-start(bf16[128,1536]{1,0:T(8,128)(2,1)S(1)} %copy-done.67), channel_id=1, source_target_pairs={{0,2},{1,3},{2,0},{3,1},{4,6},{5,7},{6,4},{7,5},{8,10},{9,11},{10,... | collective-permute-start | bytes 1179656 | tf_op jit(solution)/shard_map/ppermute | solution.py:67
  297.6 19.3 %collective-permute-start.38 = (bf16[128,1792]{1,0:T(8,128)(2,1)S(1)}, bf16[128,1792]{1,0:T(8,128)(2,1)S(1)}, u32[]{:S(2)}, u32[]{:S(2)}) collective-permute-start(bf16[128,1792]{1,0:T(8,128)(2,1)S(1)} %pad_maximum_fusion.3), channel_id=1, source_target_pairs={{0,8},{4,12},{8,16},{12,20},{16,24},{20,28},{24,0},{28,4},{1,9},{5... | collective-permute-start | bytes 1376264 | tf_op jit(solution)/shard_map/ppermute | solution.py:67
  299.0 18.0 %collective-permute-start.39 = (bf16[128,1792]{1,0:T(8,128)(2,1)S(1)}, bf16[128,1792]{1,0:T(8,128)(2,1)S(1)}, u32[]{:S(2)}, u32[]{:S(2)}) collective-permute-start(bf16[128,1792]{1,0:T(8,128)(2,1)S(1)} %copy-done.61), channel_id=1, source_target_pairs={{0,2},{1,3},{2,0},{3,1},{4,6},{5,7},{6,4},{7,5},{8,10},{9,11},{10,... | collective-permute-start | bytes 1376264 | tf_op jit(solution)/shard_map/ppermute | solution.py:67
  299.2 17.7 %collective-permute-start.42 = (bf16[4,192,512]{2,1,0:T(8,128)(2,1)S(1)}, bf16[4,192,512]{2,1,0:T(8,128)(2,1)S(1)}, u32[]{:S(2)}, u32[]{:S(2)}) collective-permute-start(bf16[4,192,512]{2,1,0:T(8,128)(2,1)S(1)} %get-tuple-element.326), channel_id=1, source_target_pairs={{0,4},{4,0},{8,12},{12,8},{16,20},{20,16},{24,28},{28,24},{1,5},{5... | collective-permute-start | bytes 2359304 | tf_op jit(solution)/shard_map/ppermute | solution.py:67
  320.0 17.0 %collective-permute-start.46 = (bf16[2,64,1536]{2,1,0:T(8,128)(2,1)S(1)}, bf16[2,64,1536]{2,1,0:T(8,128)(2,1)S(1)}, u32[]{:S(2)}, u32[]{:S(2)}) collective-permute-start(bf16[2,64,1536]{2,1,0:T(8,128)(2,1)S(1)} %multiply_convert_fusion.refs_8_), channel_id=1, source_target_pairs={{0,2},{1,3},{2,0},{3,1},{4,6},{5,7},{6,4},{7,5},{8,10},{9,11},{10,... | collective-permute-start | bytes 1179656 | tf_op jit(solution)/shard_map/ppermute | solution.py:67
  354.0 58.1 %all-to-all-start.3 = ((bf16[4,192,1280]{2,1,0:T(8,128)(2,1)}), bf16[4,192,1280]{2,1,0:T(8,128)(2,1)S(1)}, u32[]{:S(2)}, u32[]{:S(2)}) async-start(bf16[4,192,1280]{2,1,0:T(8,128)(2,1)} %pad_maximum_fusion), calls=%async_computation.3 | async-start | bytes 3932160 | tf_op jit(solution)/shard_map/all_to_all | solution.py:1041
  357.7 21.8 %collective-permute-start.51 = (bf16[5,64,1536]{2,1,0:T(8,128)(2,1)}, bf16[5,64,1536]{2,1,0:T(8,128)(2,1)}, u32[]{:S(2)}, u32[]{:S(2)}) collective-permute-start(bf16[5,64,1536]{2,1,0:T(8,128)(2,1)} %get-tuple-element.360), channel_id=1, source_target_pairs={{0,4},{4,0},{8,12},{12,8},{16,20},{20,16},{24,28},{28,24},{1,5},{5... | collective-permute-start | bytes 2949128 | tf_op jit(solution)/shard_map/ppermute | solution.py:67
  448.6 18.5 %all-to-all-start.4 = ((bf16[4,48,768]{2,1,0:T(8,128)(2,1)}), bf16[4,48,768]{2,1,0:T(8,128)(2,1)S(1)}, u32[]{:S(2)}, u32[]{:S(2)}) async-start(bf16[4,48,768]{2,1,0:T(8,128)(2,1)} %bitcast.107), calls=%async_computation.4 | async-start | bytes 589824 | tf_op jit(solution)/shard_map/all_to_all | solution.py:1093
  (112 other events, 1331.0 us)

commit v5 on v4

--- a/solution.py
+++ b/solution.py
@@ -539,10 +539,9 @@
     fetched = [[] for _ in range(cores + 2)]
     for i in range(slots):
         at = pl.ds(i * rows, rows)
-        first = width if shape["joined"][i] else 0
         fetched[0].append((x_slots[i].at[:, pl.ds(0, width)], x_ref.at[at, :]))
-        fetched[cores].append((beside[i].at[:, pl.ds(first + width, LANES)], mask_ref.at[at, :]))
-        fetched[cores + 1].append((beside[i].at[:, pl.ds(first, width)], gm_ref.at[at, :]))
+        fetched[cores].append((x_slots[i].at[:, pl.ds(width, LANES)], mask_ref.at[at, :]))
+        fetched[cores + 1].append((beside[i], gm_ref.at[at, :]))
     step = hidden // ys
     for c in range(cores):
         for s in range(ys):
@@ -649,8 +648,7 @@
     outs += [jax.ShapeDtypeStruct((rows, width), BF16) for _ in x_slots]
     outs += [jax.ShapeDtypeStruct((total, own * hidden), BF16) for _ in range(cores)]
     outs += [jax.ShapeDtypeStruct((total, 2 * own * hidden), BF16) for _ in range(cores)]
-    joined = [slot.shape[1] > width for slot in x_slots]
-    shape = dict(shape, slots=len(x_slots), joined=joined)
+    shape = dict(shape, slots=len(x_slots))
     copies = 3 * len(x_slots) + cores * shape["ys"] * (shape["zs"] + own)
     operands = x_slots + beside + gu_parts + dn_parts
     return pl.pallas_call(
@@ -797,20 +795,18 @@
         "packs": 3 if whole else dp_count,
         "copies": micros * members + (3 if whole else dp_count * (2 + members)),
     }
-    def beside_started(value):
-        column = rings.gather(value, "x")
-        ahead = [rings.step(value, "z")] if zn > 1 else []
-        tied = yield ahead + column[1:]
-        return [column[0]] + tied[len(ahead) :], tied[0]
-
     inputs = tokens.astype(F32)
     inv_first = lax.rsqrt(jnp.mean(inputs * inputs, -1, keepdims=True) + EPSILON)
     unit_first = inputs * inv_first
 
-    pack, routes, w_down = tie(pack, routes, w_down)
+    grad_result = cotangent.astype(F32)
+    grad_moe = (RESIDUAL_SCALE * grad_result).astype(BF16).reshape(home_rows, width)
+    pack, routes, w_down, grad_moe = tie(pack, routes, w_down, grad_moe)
     packs = phases.start(rings.gather_two(pack, "z", "y"))
     weights_started.append(True)
+    work = phases.start(make(lambda: grad_moe))
     phases.phase()
+    beside = phases.start(rings.gather_two(work.result, "z", "x"))
     dealt = lax.all_to_all(
         routes.reshape(micros, dp_count, rows // dp_count, routes.shape[2]), "dp", 1, 1
     ).reshape(micros, rows, routes.shape[2])
@@ -821,10 +817,6 @@
     hot = jnp.sum((dealt[:, :, :, None] == lane_ids).astype(F32), 2).astype(BF16)
     place = (shuffle[:, 0, :, None] == jnp.arange(rows, dtype=jnp.int32)).astype(BF16)
     named = jnp.einsum("mir,mix->mrx", place, hot, preferred_element_type=F32).astype(BF16)
-
-    grad_result = cotangent.astype(F32)
-    grad_moe = (RESIDUAL_SCALE * grad_result).astype(BF16)
-    beside = jnp.concatenate([grad_moe, named], 2).reshape(home_rows, width + LANES)
 
     row_at = jnp.concatenate(
         [
@@ -851,10 +843,9 @@
     allowed = segment[:, :, None] == segment[:, None, :]
     bias = jnp.where(allowed & (row_at[None, :] <= row_at[:, None]), 0.0, NEGATIVE)
 
-    tables = phases.start(make(lambda: (cosine, sine, bias, beside, gate_up, w_down)))
+    tables = phases.start(make(lambda: (cosine, sine, bias, named, gate_up, w_down)))
     phases.phase()
-    cosine, sine, bias, beside, gate_up, w_down = tables.result
-    beside = phases.start(beside_started(beside))
+    cosine, sine, bias, named, gate_up, w_down = tables.result
     gate_up = lax.all_to_all(gate_up, "dp", 0, 0, axis_index_groups=rings.z_groups)
     held = phases.start(make(lambda: w_down))
     packs, group_tokens = phases.finish(packs, group_tokens)
@@ -887,7 +878,7 @@
         )
     )
     down_task = phases.start(make(lambda: down))
-    phases.finish(attention)
+    (_, beside) = phases.finish(attention, beside)
     down = phases.start(make(lambda: [rings.gather(part, "c") for part in down_task.result]))
     attn_parts, group_in, n1, router_columns, small_rows, qkv, merged, lse = attention.result
     gain_first = small_rows[experts_all]
@@ -902,27 +893,17 @@
     unit_second = hidden * inv_second
     normed_second = (unit_second * gain_second).astype(BF16).reshape(home_rows, width)
 
-    if zn > 1:
-        first = phases.start(make(lambda: [rings.step(normed_second, "z")] + rings.gather(normed_second, "x")))
-        phases.finish(first)
-        passed, *column = first.result
-        together = jnp.concatenate([passed, beside.result[1]], 1)
-        group = phases.start(rings.gather_two(together, "z", "x", zn - 1))
-    else:
-        first = phases.start(make(lambda: rings.gather(normed_second, "x")))
-        phases.finish(first)
-        column, group = first.result, None
+    together = jnp.concatenate([normed_second, named.reshape(home_rows, LANES)], 1)
+    group_x = phases.start(rings.gather_two(together, "z", "x"))
     gate_up = rings.gather(gate_up, "y")
-    if group is not None:
-        phases.phase()
-        phases.phase()
+    phases.phase()
+    phases.phase()
     mine_too = phases.start(make(lambda: rings.gather(gate_up[0], "c")))
     gate_up = phases.start(make(lambda: gate_up[1:]))
-    phases.finish(mine_too, gate_up, *([] if group is None else [group]))
-    gate_up = [mine_too.result] + [rings.gather(part, "c") for part in gate_up.result]
-    later = [[] for _ in range(xn)] if group is None else group.result
-    group_x = [[column[i]] + later[i] for i in range(xn)]
-    beside = [[beside.result[0][i]] + later[i] for i in range(xn)]
+    phases.finish(mine_too, gate_up)
+    gate_up = phases.start(make(lambda: [rings.gather(part, "c") for part in gate_up.result]))
+    group_x, gate_up = phases.finish(group_x, gate_up)
+    gate_up = [mine_too.result] + gate_up
     gu_parts = [gate_up[s][c] for c in range(cn) for s in range(yn)]
     dn_parts = [down[s][c] for c in range(cn) for s in range(yn)]
 

time: 479 us -> 469 us (0.979)
  starting transfers between devices: 106 us -> 91.7 us
  waiting for transfers between devices: 204 us -> 213 us
  local copies, waits for them, and re-layouts: 21.8 us -> 16.9 us
    ppermute x61 -> x66, starting transfers between devices: 74.9 us -> 61.1 us  [step(): return lax.ppermute(value, axis, pairs)]
    all_to_all x1, waiting for transfers between devices: 5.16 us -> 15.4 us  [per_device(): lax.all_to_all(routes.reshape(micros, dp_count, rows // dp_count, routes....]
    unnamed x141 -> x138, local copies, waits for them, and re-layouts: 11.9 us -> 7.9 us
    ppermute x61 -> x66, waiting for transfers between devices: 176 us -> 173 us  [step(): return lax.ppermute(value, axis, pairs)]
  transfers between devices with their start and end apart: 68 -> 73, of which waited for: 40 -> 40; matrix products, arithmetic and copies ran while one was open for 11% -> 12% of each run, Pallas kernels for 9% -> 9%
where the time goes in v5:
time: 469 us; the launch traced here: 461 us
  waiting for transfers between devices  213 us (45%)
  starting transfers between devices  91.7 us (20%)
  Pallas kernels  81 us (17%)
  other arithmetic  35.5 us (8%)
  matrix products  20.4 us (4%)
  local copies, waits for them, and re-layouts  16.9 us (4%)
    ppermute x66, waiting for transfers between devices, step(): return lax.ppermute(value, axis, pairs)  173 us
    ppermute x66, starting transfers between devices, step(): return lax.ppermute(value, axis, pairs)  61.1 us
    pallas_call x1, Pallas kernels, run_experts(): pl.pallas_call(functools.partial(experts_kernel, shape), in_specs=[pl.Blo...  38.4 us
    dot_general x5, matrix products, dot(): return lax.dot_general(a, b, (dims, ((), ())), preferred_element_type=F32)  20.3 us
    pallas_call x1, Pallas kernels, attention_backward(): pl.pallas_call(functools.partial(attention_backward_kernel, shape), grid_...  19.4 us
    all_to_all x1, waiting for transfers between devices, per_device(): lax.all_to_all(routes.reshape(micros, dp_count, rows // dp_count, routes....  15.4 us
    pallas_call x1, Pallas kernels, attention_forward(): pl.pallas_call(functools.partial(attention_forward_kernel, shape), grid_s...  13.7 us
    all_to_all x1, waiting for transfers between devices, per_device(): lax.all_to_all(grad_gu, 'dp', 0, 0, axis_index_groups=rings.z_groups)  12.8 us
  transfers between devices with their start and end apart: 73, of which 40 were waited for; matrix products, arithmetic and copies ran while one was open for 12% of the time, Pallas kernels for 9%

profile of v5, /device:TPU:3, one launch (start us, length us, event | category | flops | bytes accessed | tf_op | source)
XLA Modules:
  0.0 460.9 jit_solution(13996104829429676080)
XLA Ops:
  24.0 6.2 %collective-permute-done.4.refs_4_ = bf16[192,1152]{1,0:T(8,128)(2,1)S(1)} collective-permute-done((bf16[192,1152]{1,0:T(8,128)(2,1)S(1)}, bf16[192,1152]{1,0:T(8,128)(2,1)S(1)}, u32[]{:S(2)}, u32[]{:S(2)}) %collective-permute-start.4) | collective-permute-done | bytes 442400 | tf_op jit(solution)/shard_map/ppermute | solution.py:67
  45.0 15.4 %all-to-all-done.1 = s32[8,1,128]{2,1,0:T(1,128)S(1)} async-done(((s32[8,1,128]{2,1,0:T(1,128)}), s32[8,1,128]{2,1,0:T(1,128)S(1)}, u32[]{:S(2)}, u32[]{:S(2)}) %all-to-all-start.1) | async-done | bytes 4128 | tf_op jit(solution)/shard_map/all_to_all | solution.py:810
  66.6 5.7 %collective-permute-done.13.refs_13_ = bf16[128,1536]{1,0:T(8,128)(2,1)S(1)} collective-permute-done((bf16[128,1536]{1,0:T(8,128)(2,1)}, bf16[128,1536]{1,0:T(8,128)(2,1)S(1)}, u32[]{:S(2)}, u32[]{:S(2)}) %collective-permute-start.13) | collective-permute-done | bytes 393248 | tf_op jit(solution)/shard_map/ppermute | solution.py:67
  73.8 9.4 %collective-permute-done.10.refs_3_ = bf16[192,1152]{1,0:T(8,128)(2,1)S(1)} collective-permute-done((bf16[192,1152]{1,0:T(8,128)(2,1)S(1)}, bf16[192,1152]{1,0:T(8,128)(2,1)S(1)}, u32[]{:S(2)}, u32[]{:S(2)}) %collective-permute-start.10) | collective-permute-done | bytes 442400 | tf_op jit(solution)/shard_map/ppermute | solution.py:67
  96.9 13.7 %attention_forward.1 = (bf16[2,64,1536]{2,1,0:T(8,128)(2,1)}, bf16[2,64,1536]{2,1,0:T(8,128)(2,1)}, bf16[2,64,1536]{2,1,0:T(8,128)(2,1)}, bf16[2,64,1536]{2,1,0:...) custom-call(s32[8]{0:T(128)} %stack.41.spots_ref, ...), custom_call_target="tpu_custom_call" | custom-call | tf_op jit(solution)/shard_map/attention_forward/pallas_call | solution.py:464
  112.7 7.4 %collective-permute-start.19 = (bf16[5,64,1536]{2,1,0:T(8,128)(2,1)}, bf16[5,64,1536]{2,1,0:T(8,128)(2,1)}, u32[]{:S(2)}, u32[]{:S(2)}) collective-permute-start(bf16[5,64,1536]{2,1,0:T(8,128)(2,1)} %refs_20_), channel_id=1, source_target_pairs={{0,1},{1,0},{2,3},{3,2},{4,5},{5,4},{6,7},{7,6},{8,9},{9,8},{10,11... | collective-permute-start | bytes 2949128 | tf_op jit(solution)/shard_map/ppermute | solution.py:67
  127.4 8.7 %collective-permute-done.22 = bf16[2,64,1536]{2,1,0:T(8,128)(2,1)S(1)} collective-permute-done((bf16[2,64,1536]{2,1,0:T(8,128)(2,1)S(1)}, bf16[2,64,1536]{2,1,0:T(8,128)(2,1)S(1)}, u32[]{:S(2)}, u32[]{:S(2)}) %collective-permute-start.22) | collective-permute-done | bytes 393248 | tf_op jit(solution)/shard_map/ppermute | solution.py:67
  144.0 11.5 %collective-permute-done.25.refs_4_ = bf16[128,1664]{1,0:T(8,128)(2,1)S(1)} collective-permute-done((bf16[128,1664]{1,0:T(8,128)(2,1)S(1)}, bf16[128,1664]{1,0:T(8,128)(2,1)S(1)}, u32[]{:S(2)}, u32[]{:S(2)}) %collective-permute-start.25) | collective-permute-done | bytes 426016 | tf_op jit(solution)/shard_map/ppermute | solution.py:67
  158.3 8.9 %collective-permute-done.27.refs_5_ = bf16[128,1664]{1,0:T(8,128)(2,1)S(1)} collective-permute-done((bf16[128,1664]{1,0:T(8,128)(2,1)S(1)}, bf16[128,1664]{1,0:T(8,128)(2,1)S(1)}, u32[]{:S(2)}, u32[]{:S(2)}) %collective-permute-start.27) | collective-permute-done | bytes 426016 | tf_op jit(solution)/shard_map/ppermute | solution.py:67
  170.6 8.6 %collective-permute-done.29.refs_6_ = bf16[128,1664]{1,0:T(8,128)(2,1)S(1)} collective-permute-done((bf16[128,1664]{1,0:T(8,128)(2,1)S(1)}, bf16[128,1664]{1,0:T(8,128)(2,1)S(1)}, u32[]{:S(2)}, u32[]{:S(2)}) %collective-permute-start.29) | collective-permute-done | bytes 426016 | tf_op jit(solution)/shard_map/ppermute | solution.py:67
  186.9 9.6 %collective-permute-done.32.refs_7_ = bf16[128,1664]{1,0:T(8,128)(2,1)} collective-permute-done((bf16[128,1664]{1,0:T(8,128)(2,1)}, bf16[128,1664]{1,0:T(8,128)(2,1)}, u32[]{:S(2)}, u32[]{:S(2)}) %collective-permute-start.32) | collective-permute-done | bytes 426016 | tf_op jit(solution)/shard_map/ppermute | solution.py:67
  197.8 38.4 %experts.1 = (f32[1024,128]{1,0:T(8,128)}, bf16[1024,1536]{1,0:T(8,128)(2,1)}, bf16[1024,1536]{1,0:T(8,128)(2,1)}, bf16[128,1792]{1,0:T(8,128)(2,1)}, bf16[128,1...) custom-call(s32[12]{0:T(128)} %pad_add_fusion.1.table_ref, ...), custom_call_target="tpu_custom_call" | custom-call | tf_op jit(solution)/shard_map/experts/pallas_call | solution.py:654
  236.6 9.3 %convolution_convert_fusion = bf16[1536,1280]{1,0:T(8,128)(2,1)} fusion(bf16[1024,1536]{1,0:T(8,128)(2,1)} %get-tuple-element.312, bf16[1024,1280]{1,0:T(8,128)(2,1)} %get-tuple-element.304), kind=kOutput, calls=%fused_computation.1 | convolution fusion | flops 4028497920 | bytes 9699328 | tf_op jit(solution)/shard_map/dot_general | solution.py:27
  256.2 6.2 %fusion = bf16[1536,1280]{1,0:T(8,128)(2,1)S(1)} fusion(bf16[1536,1280]{1,0:T(8,128)(2,1)} %collective-permute-done.37, bf16[1024,1536]{1,0:T(8,128)(2,1)S(1)} %copy-done.57, bf16[1024,1280]{1,0:T(8,128)(2,1)S(1)} %copy-done.58), kind=kOutput, calls=%fused_computation.2 | convolution fusion | flops 4032430080 | bytes 13631488 | tf_op jit(solution)/shard_map/dot_general | solution.py:27
  267.5 18.6 %collective-permute-done.40 = bf16[128,1536]{1,0:T(8,128)(2,1)S(1)} collective-permute-done((bf16[128,1536]{1,0:T(8,128)(2,1)S(1)}, bf16[128,1536]{1,0:T(8,128)(2,1)S(1)}, u32[]{:S(2)}, u32[]{:S(2)}) %collective-permute-start.40) | collective-permute-done | bytes 393248 | tf_op jit(solution)/shard_map/ppermute | solution.py:67
  297.9 9.8 %collective-permute-done.43 = bf16[128,1792]{1,0:T(8,128)(2,1)S(1)} collective-permute-done((bf16[128,1792]{1,0:T(8,128)(2,1)S(1)}, bf16[128,1792]{1,0:T(8,128)(2,1)S(1)}, u32[]{:S(2)}, u32[]{:S(2)}) %collective-permute-start.43) | collective-permute-done | bytes 458784 | tf_op jit(solution)/shard_map/ppermute | solution.py:67
  318.1 8.5 %collective-permute-done.48 = bf16[128,1536]{1,0:T(8,128)(2,1)S(1)} collective-permute-done((bf16[128,1536]{1,0:T(8,128)(2,1)S(1)}, bf16[128,1536]{1,0:T(8,128)(2,1)S(1)}, u32[]{:S(2)}, u32[]{:S(2)}) %collective-permute-start.48) | collective-permute-done | bytes 393248 | tf_op jit(solution)/shard_map/ppermute | solution.py:67
  331.0 6.2 %collective-permute-done.53 = bf16[128,1536]{1,0:T(8,128)(2,1)S(1)} collective-permute-done((bf16[128,1536]{1,0:T(8,128)(2,1)S(1)}, bf16[128,1536]{1,0:T(8,128)(2,1)S(1)}, u32[]{:S(2)}, u32[]{:S(2)}) %collective-permute-start.53) | collective-permute-done | bytes 393248 | tf_op jit(solution)/shard_map/ppermute | solution.py:67
  349.4 19.4 %attention_backward.1 = (bf16[2,64,1536]{2,1,0:T(8,128)(2,1)}, bf16[2,64,1536]{2,1,0:T(8,128)(2,1)}, bf16[2,64,1536]{2,1,0:T(8,128)(2,1)}, bf16[2,64,1536]{2,1,0...) custom-call(s32[8]{0:T(128)} %stack.41.spots_ref, ...), custom_call_target="tpu_custom_call" | custom-call | tf_op jit(solution)/shard_map/attention_backward/pallas_call | solution.py:490
  369.7 6.9 %collective-permute-done.57 = bf16[192,1152]{1,0:T(8,128)(2,1)S(1)} collective-permute-done((bf16[192,1152]{1,0:T(8,128)(2,1)}, bf16[192,1152]{1,0:T(8,128)(2,1)S(1)}, u32[]{:S(2)}, u32[]{:S(2)}) %collective-permute-start.57) | collective-permute-done | bytes 442400 | tf_op jit(solution)/shard_map/ppermute | solution.py:67
  380.2 6.5 %collective-permute-start.60 = (bf16[2,64,1536]{2,1,0:T(8,128)(2,1)}, bf16[2,64,1536]{2,1,0:T(8,128)(2,1)S(1)}, u32[]{:S(2)}, u32[]{:S(2)}) collective-permute-start(bf16[2,64,1536]{2,1,0:T(8,128)(2,1)} %get-tuple-element.405), channel_id=1, source_target_pairs={{0,1},{1,0},{2,3},{3,2},{4,5},{5,4},{6,7},{7,6},{8,9},{9,8},{10,11... | collective-permute-start | bytes 1179656 | tf_op jit(solution)/shard_map/ppermute | solution.py:67
  389.8 12.8 %all-to-all-done.3.in_ref = bf16[4,192,1280]{2,1,0:T(8,128)(2,1)S(1)} async-done(((bf16[4,192,1280]{2,1,0:T(8,128)(2,1)}), bf16[4,192,1280]{2,1,0:T(8,128)(2,1)S(1)}, u32[]{:S(2)}, u32[]{:S(2)}) %all-to-all-start.3) | async-done | bytes 1966112 | tf_op jit(solution)/shard_map/all_to_all | solution.py:1022
  413.7 8.2 %collective-permute-done.61 = bf16[192,1152]{1,0:T(8,128)(2,1)S(1)} collective-permute-done((bf16[192,1152]{1,0:T(8,128)(2,1)S(1)}, bf16[192,1152]{1,0:T(8,128)(2,1)S(1)}, u32[]{:S(2)}, u32[]{:S(2)}) %collective-permute-start.61) | collective-permute-done | bytes 442400 | tf_op jit(solution)/shard_map/ppermute | solution.py:67
  438.7 5.9 %all-to-all-start.4 = ((bf16[4,48,768]{2,1,0:T(8,128)(2,1)}), bf16[4,48,768]{2,1,0:T(8,128)(2,1)S(1)}, u32[]{:S(2)}, u32[]{:S(2)}) async-start(bf16[4,48,768]{2,1,0:T(8,128)(2,1)} %bitcast.109), calls=%async_computation.4 | async-start | bytes 589824 | tf_op jit(solution)/shard_map/all_to_all | solution.py:1074
  (361 shorter events, 197.2 us)
Async XLA Ops:
  0.7 20.1 %collective-permute-start = (bf16[2,64,1536]{2,1,0:T(8,128)(2,1)}, bf16[2,64,1536]{2,1,0:T(8,128)(2,1)S(1)}, u32[]{:S(2)}, u32[]{:S(2)}) collective-permute-start(bf16[2,64,1536]{2,1,0:T(8,128)(2,1)} %refs_8_.1), channel_id=1, source_target_pairs={{0,1},{1,0},{2,3},{3,2},{4,5},{5,4},{6,7},{7,6},{8,9},{9,8},{10,11... | collective-permute-start | bytes 1179656 | tf_op jit(solution)/shard_map/ppermute | solution.py:67
  1.4 19.4 %collective-permute-start.1 = (bf16[2,64,1536]{2,1,0:T(8,128)(2,1)}, bf16[2,64,1536]{2,1,0:T(8,128)(2,1)S(1)}, u32[]{:S(2)}, u32[]{:S(2)}) collective-permute-start(bf16[2,64,1536]{2,1,0:T(8,128)(2,1)} %refs_8_.1), channel_id=1, source_target_pairs={{0,2},{1,3},{2,0},{3,1},{4,6},{5,7},{6,4},{7,5},{8,10},{9,11},{10,... | collective-permute-start | bytes 1179656 | tf_op jit(solution)/shard_map/ppermute | solution.py:67
  33.1 28.7 %collective-permute-start.9 = (bf16[128,1536]{1,0:T(8,128)(2,1)S(1)}, bf16[128,1536]{1,0:T(8,128)(2,1)}, u32[]{:S(2)}, u32[]{:S(2)}) collective-permute-start(bf16[128,1536]{1,0:T(8,128)(2,1)S(1)} %bitcast.105), channel_id=1, source_target_pairs={{0,2},{1,3},{2,0},{3,1},{4,6},{5,7},{6,4},{7,5},{8,10},{9,11},{10,... | collective-permute-start | bytes 1179656 | tf_op jit(solution)/shard_map/ppermute | solution.py:67
  37.0 24.8 %collective-permute-start.8 = (bf16[128,1536]{1,0:T(8,128)(2,1)S(1)}, bf16[128,1536]{1,0:T(8,128)(2,1)}, u32[]{:S(2)}, u32[]{:S(2)}) collective-permute-start(bf16[128,1536]{1,0:T(8,128)(2,1)S(1)} %bitcast.106), channel_id=1, source_target_pairs={{0,8},{4,12},{8,16},{12,20},{16,24},{20,28},{24,0},{28,4},{1,9},{5... | collective-permute-start | bytes 1179656 | tf_op jit(solution)/shard_map/ppermute | solution.py:67
  37.4 24.4 %collective-permute-start.7 = (bf16[192,1152]{1,0:T(8,128)(2,1)S(1)}, bf16[192,1152]{1,0:T(8,128)(2,1)S(1)}, u32[]{:S(2)}, u32[]{:S(2)}) collective-permute-start(bf16[192,1152]{1,0:T(8,128)(2,1)S(1)} %collective-permute-done.3.refs_1_), channel_id=1, source_target_pairs={{0,4},{4,0},{8,12},{12,8},{16,20},{20,16},{24,28},{28,24},{1,5},{5... | collective-permute-start | bytes 1327112 | tf_op jit(solution)/shard_map/ppermute | solution.py:67
  38.7 23.1 %collective-permute-start.6 = (bf16[192,1152]{1,0:T(8,128)(2,1)S(1)}, bf16[192,1152]{1,0:T(8,128)(2,1)S(1)}, u32[]{:S(2)}, u32[]{:S(2)}) collective-permute-start(bf16[192,1152]{1,0:T(8,128)(2,1)S(1)} %collective-permute-done.3.refs_1_), channel_id=1, source_target_pairs={{0,8},{4,12},{8,16},{12,20},{16,24},{20,28},{24,0},{28,4},{1,9},{5... | collective-permute-start | bytes 1327112 | tf_op jit(solution)/shard_map/ppermute | solution.py:67
  39.1 22.7 %collective-permute-start.5 = (bf16[2,64,1536]{2,1,0:T(8,128)(2,1)S(1)}, bf16[2,64,1536]{2,1,0:T(8,128)(2,1)S(1)}, u32[]{:S(2)}, u32[]{:S(2)}) collective-permute-start(bf16[2,64,1536]{2,1,0:T(8,128)(2,1)S(1)} %collective-permute-done.refs_9_), channel_id=1, source_target_pairs={{0,2},{1,3},{2,0},{3,1},{4,6},{5,7},{6,4},{7,5},{8,10},{9,11},{10,... | collective-permute-start | bytes 1179656 | tf_op jit(solution)/shard_map/ppermute | solution.py:67
  41.6 18.8 %all-to-all-start.1 = ((s32[8,1,128]{2,1,0:T(1,128)}), s32[8,1,128]{2,1,0:T(1,128)S(1)}, u32[]{:S(2)}, u32[]{:S(2)}) async-start(s32[8,1,128]{2,1,0:T(1,128)} %reshape.272), calls=%async_computation.1 | async-start | bytes 8192 | tf_op jit(solution)/shard_map/all_to_all | solution.py:810
  63.1 20.1 %collective-permute-start.10 = (bf16[192,1152]{1,0:T(8,128)(2,1)S(1)}, bf16[192,1152]{1,0:T(8,128)(2,1)S(1)}, u32[]{:S(2)}, u32[]{:S(2)}) collective-permute-start(bf16[192,1152]{1,0:T(8,128)(2,1)S(1)} %collective-permute-done.6.refs_2_), channel_id=1, source_target_pairs={{0,8},{4,12},{8,16},{12,20},{16,24},{20,28},{24,0},{28,4},{1,9},{5... | collective-permute-start | bytes 1327112 | tf_op jit(solution)/shard_map/ppermute | solution.py:67
  85.3 55.1 %all-to-all-start.2 = ((bf16[4,192,1280]{2,1,0:T(8,128)(2,1)}), bf16[4,192,1280]{2,1,0:T(8,128)(2,1)S(1)}, u32[]{:S(2)}, u32[]{:S(2)}) async-start(bf16[4,192,1280]{2,1,0:T(8,128)(2,1)} %pack_experts.1), calls=%async_computation.2 | async-start | bytes 3932160 | tf_op jit(solution)/shard_map/all_to_all | solution.py:849
  95.6 17.1 %collective-permute-start.18 = (bf16[5,64,1536]{2,1,0:T(8,128)(2,1)}, bf16[5,64,1536]{2,1,0:T(8,128)(2,1)}, u32[]{:S(2)}, u32[]{:S(2)}) collective-permute-start(bf16[5,64,1536]{2,1,0:T(8,128)(2,1)} %refs_20_), channel_id=1, source_target_pairs={{0,4},{4,0},{8,12},{12,8},{16,20},{20,16},{24,28},{28,24},{1,5},{5... | collective-permute-start | bytes 2949128 | tf_op jit(solution)/shard_map/ppermute | solution.py:67
  140.4 44.0 %collective-permute-start.31 = (bf16[4,192,1280]{2,1,0:T(8,128)(2,1)S(1)}, bf16[4,192,1280]{2,1,0:T(8,128)(2,1)}, u32[]{:S(2)}, u32[]{:S(2)}) collective-permute-start(bf16[4,192,1280]{2,1,0:T(8,128)(2,1)S(1)} %all-to-all-done.2.refs_16_), channel_id=1, source_target_pairs={{0,4},{4,0},{8,12},{12,8},{16,20},{20,16},{24,28},{28,24},{1,5},{5... | collective-permute-start | bytes 5898248 | tf_op jit(solution)/shard_map/ppermute | solution.py:67
  141.2 43.2 %collective-permute-start.30 = (bf16[4,192,1280]{2,1,0:T(8,128)(2,1)S(1)}, bf16[4,192,1280]{2,1,0:T(8,128)(2,1)S(1)}, u32[]{:S(2)}, u32[]{:S(2)}) collective-permute-start(bf16[4,192,1280]{2,1,0:T(8,128)(2,1)S(1)} %all-to-all-done.2.refs_16_), channel_id=1, source_target_pairs={{0,1},{1,0},{2,3},{3,2},{4,5},{5,4},{6,7},{7,6},{8,9},{9,8},{10,11... | collective-permute-start | bytes 5898248 | tf_op jit(solution)/shard_map/ppermute | solution.py:67
  263.6 22.5 %collective-permute-start.42 = (bf16[640,1536]{1,0:T(8,128)(2,1)S(1)}, bf16[640,1536]{1,0:T(8,128)(2,1)S(1)}, u32[]{:S(2)}, u32[]{:S(2)}) collective-permute-start(bf16[640,1536]{1,0:T(8,128)(2,1)S(1)} %convolution_convert_fusion.1), channel_id=1, source_target_pairs={{0,1},{1,0},{2,3},{3,2},{4,5},{5,4},{6,7},{7,6},{8,9},{9,8},{10,11... | collective-permute-start | bytes 5898248 | tf_op jit(solution)/shard_map/ppermute | solution.py:67
  264.6 21.5 %collective-permute-start.41 = (bf16[4,192,512]{2,1,0:T(8,128)(2,1)S(1)}, bf16[4,192,512]{2,1,0:T(8,128)(2,1)S(1)}, u32[]{:S(2)}, u32[]{:S(2)}) collective-permute-start(bf16[4,192,512]{2,1,0:T(8,128)(2,1)S(1)} %get-tuple-element.487), channel_id=1, source_target_pairs={{0,4},{4,0},{8,12},{12,8},{16,20},{20,16},{24,28},{28,24},{1,5},{5... | collective-permute-start | bytes 2359304 | tf_op jit(solution)/shard_map/ppermute | solution.py:67
  265.7 20.4 %collective-permute-start.38 = (bf16[128,1792]{1,0:T(8,128)(2,1)S(1)}, bf16[128,1792]{1,0:T(8,128)(2,1)S(1)}, u32[]{:S(2)}, u32[]{:S(2)}) collective-permute-start(bf16[128,1792]{1,0:T(8,128)(2,1)S(1)} %pad_maximum_fusion.2), channel_id=1, source_target_pairs={{0,8},{4,12},{8,16},{12,20},{16,24},{20,28},{24,0},{28,4},{1,9},{5... | collective-permute-start | bytes 1376264 | tf_op jit(solution)/shard_map/ppermute | solution.py:67
  265.8 20.3 %collective-permute-start.39 = (bf16[128,1792]{1,0:T(8,128)(2,1)S(1)}, bf16[128,1792]{1,0:T(8,128)(2,1)S(1)}, u32[]{:S(2)}, u32[]{:S(2)}) collective-permute-start(bf16[128,1792]{1,0:T(8,128)(2,1)S(1)} %copy-done.61), channel_id=1, source_target_pairs={{0,2},{1,3},{2,0},{3,1},{4,6},{5,7},{6,4},{7,5},{8,10},{9,11},{10,... | collective-permute-start | bytes 1376264 | tf_op jit(solution)/shard_map/ppermute | solution.py:67
  266.0 20.0 %collective-permute-start.40 = (bf16[128,1536]{1,0:T(8,128)(2,1)S(1)}, bf16[128,1536]{1,0:T(8,128)(2,1)S(1)}, u32[]{:S(2)}, u32[]{:S(2)}) collective-permute-start(bf16[128,1536]{1,0:T(8,128)(2,1)S(1)} %copy-done.66), channel_id=1, source_target_pairs={{0,2},{1,3},{2,0},{3,1},{4,6},{5,7},{6,4},{7,5},{8,10},{9,11},{10,... | collective-permute-start | bytes 1179656 | tf_op jit(solution)/shard_map/ppermute | solution.py:67
  287.4 20.3 %collective-permute-start.43 = (bf16[128,1792]{1,0:T(8,128)(2,1)S(1)}, bf16[128,1792]{1,0:T(8,128)(2,1)S(1)}, u32[]{:S(2)}, u32[]{:S(2)}) collective-permute-start(bf16[128,1792]{1,0:T(8,128)(2,1)S(1)} %pad_maximum_fusion.3), channel_id=1, source_target_pairs={{0,8},{4,12},{8,16},{12,20},{16,24},{20,28},{24,0},{28,4},{1,9},{5... | collective-permute-start | bytes 1376264 | tf_op jit(solution)/shard_map/ppermute | solution.py:67
  288.7 19.0 %collective-permute-start.44 = (bf16[128,1792]{1,0:T(8,128)(2,1)S(1)}, bf16[128,1792]{1,0:T(8,128)(2,1)S(1)}, u32[]{:S(2)}, u32[]{:S(2)}) collective-permute-start(bf16[128,1792]{1,0:T(8,128)(2,1)S(1)} %copy-done.60), channel_id=1, source_target_pairs={{0,2},{1,3},{2,0},{3,1},{4,6},{5,7},{6,4},{7,5},{8,10},{9,11},{10,... | collective-permute-start | bytes 1376264 | tf_op jit(solution)/shard_map/ppermute | solution.py:67
  290.0 17.7 %collective-permute-start.47 = (bf16[4,192,512]{2,1,0:T(8,128)(2,1)S(1)}, bf16[4,192,512]{2,1,0:T(8,128)(2,1)S(1)}, u32[]{:S(2)}, u32[]{:S(2)}) collective-permute-start(bf16[4,192,512]{2,1,0:T(8,128)(2,1)S(1)} %get-tuple-element.342), channel_id=1, source_target_pairs={{0,4},{4,0},{8,12},{12,8},{16,20},{20,16},{24,28},{28,24},{1,5},{5... | collective-permute-start | bytes 2359304 | tf_op jit(solution)/shard_map/ppermute | solution.py:67
  343.5 59.1 %all-to-all-start.3 = ((bf16[4,192,1280]{2,1,0:T(8,128)(2,1)}), bf16[4,192,1280]{2,1,0:T(8,128)(2,1)S(1)}, u32[]{:S(2)}, u32[]{:S(2)}) async-start(bf16[4,192,1280]{2,1,0:T(8,128)(2,1)} %pad_maximum_fusion), calls=%async_computation.3 | async-start | bytes 3932160 | tf_op jit(solution)/shard_map/all_to_all | solution.py:1022
  348.2 20.6 %collective-permute-start.56 = (bf16[5,64,1536]{2,1,0:T(8,128)(2,1)}, bf16[5,64,1536]{2,1,0:T(8,128)(2,1)}, u32[]{:S(2)}, u32[]{:S(2)}) collective-permute-start(bf16[5,64,1536]{2,1,0:T(8,128)(2,1)} %get-tuple-element.376), channel_id=1, source_target_pairs={{0,4},{4,0},{8,12},{12,8},{16,20},{20,16},{24,28},{28,24},{1,5},{5... | collective-permute-start | bytes 2949128 | tf_op jit(solution)/shard_map/ppermute | solution.py:67
  438.7 18.2 %all-to-all-start.4 = ((bf16[4,48,768]{2,1,0:T(8,128)(2,1)}), bf16[4,48,768]{2,1,0:T(8,128)(2,1)S(1)}, u32[]{:S(2)}, u32[]{:S(2)}) async-start(bf16[4,48,768]{2,1,0:T(8,128)(2,1)} %bitcast.109), calls=%async_computation.4 | async-start | bytes 589824 | tf_op jit(solution)/shard_map/all_to_all | solution.py:1074
  (116 other events, 1557.6 us)

commit v6 on v5

--- a/solution.py
+++ b/solution.py
@@ -804,15 +804,16 @@
     pack, routes, w_down, grad_moe = tie(pack, routes, w_down, grad_moe)
     packs = phases.start(rings.gather_two(pack, "z", "y"))
     weights_started.append(True)
-    work = phases.start(make(lambda: grad_moe))
-    phases.phase()
-    beside = phases.start(rings.gather_two(work.result, "z", "x"))
     dealt = lax.all_to_all(
         routes.reshape(micros, dp_count, rows // dp_count, routes.shape[2]), "dp", 1, 1
     ).reshape(micros, rows, routes.shape[2])
-    held = phases.start(make(lambda: dealt))
+    work = phases.start(make(lambda: (grad_moe, dealt)))
     phases.phase()
-    dealt = held.result
+    grad_moe, dealt = work.result
+    beside = phases.start(rings.gather_two(grad_moe, "z", "x"))
+    work = phases.start(make(lambda: dealt))
+    phases.phase()
+    dealt = work.result
     lane_ids = jnp.arange(LANES, dtype=jnp.int32)
     hot = jnp.sum((dealt[:, :, :, None] == lane_ids).astype(F32), 2).astype(BF16)
     place = (shuffle[:, 0, :, None] == jnp.arange(rows, dtype=jnp.int32)).astype(BF16)

time: 469 us -> 463 us (0.987)
  waiting for transfers between devices: 213 us -> 199 us
  starting transfers between devices: 91.7 us -> 99.8 us
    all_to_all x1, waiting for transfers between devices: 15.4 us -> 5.34 us  [per_device(): lax.all_to_all(routes.reshape(micros, dp_count, rows // dp_count, routes....]
    ppermute x66, starting transfers between devices: 61.1 us -> 67.2 us  [step(): return lax.ppermute(value, axis, pairs)]
  transfers between devices with their start and end apart: 73 -> 73, of which waited for: 40 -> 39; matrix products, arithmetic and copies ran while one was open for 12% -> 12% of each run, Pallas kernels for 9% -> 9%
where the time goes in v6:
time: 463 us; the launch traced here: 455 us
  waiting for transfers between devices  199 us (43%)
  starting transfers between devices  99.8 us (22%)
  Pallas kernels  81 us (17%)
  other arithmetic  33.2 us (7%)
  matrix products  21.7 us (5%)
  local copies, waits for them, and re-layouts  17.8 us (4%)
    ppermute x66, waiting for transfers between devices, step(): return lax.ppermute(value, axis, pairs)  171 us
    ppermute x66, starting transfers between devices, step(): return lax.ppermute(value, axis, pairs)  67.2 us
    pallas_call x1, Pallas kernels, run_experts(): pl.pallas_call(functools.partial(experts_kernel, shape), in_specs=[pl.Blo...  38.4 us
    dot_general x5, matrix products, dot(): return lax.dot_general(a, b, (dims, ((), ())), preferred_element_type=F32)  21.6 us
    pallas_call x1, Pallas kernels, attention_backward(): pl.pallas_call(functools.partial(attention_backward_kernel, shape), grid_...  19.3 us
    pallas_call x1, Pallas kernels, attention_forward(): pl.pallas_call(functools.partial(attention_forward_kernel, shape), grid_s...  13.7 us
    all_to_all x1, waiting for transfers between devices, per_device(): lax.all_to_all(grad_gu, 'dp', 0, 0, axis_index_groups=rings.z_groups)  12.8 us
  transfers between devices with their start and end apart: 73, of which 39 were waited for; matrix products, arithmetic and copies ran while one was open for 12% of the time, Pallas kernels for 9%

profile of v6, /device:TPU:3, one launch (start us, length us, event | category | flops | bytes accessed | tf_op | source)
XLA Modules:
  0.0 454.9 jit_solution(13974559317938649201)
XLA Ops:
  4.8 5.2 %all-to-all-start = ((bf16[4,48,768]{2,1,0:T(8,128)(2,1)}), bf16[4,48,768]{2,1,0:T(8,128)(2,1)S(1)}, u32[]{:S(2)}, u32[]{:S(2)}) async-start(bf16[4,48,768]{2,1,0:T(8,128)(2,1)} %maximum_bitcast_fusion), calls=%async_computation | async-start | bytes 589824 | tf_op jit(solution)/shard_map/all_to_all | solution.py:765
  29.3 5.3 %all-to-all-done.1 = s32[8,1,128]{2,1,0:T(1,128)S(1)} async-done(((s32[8,1,128]{2,1,0:T(1,128)}), s32[8,1,128]{2,1,0:T(1,128)S(1)}, u32[]{:S(2)}, u32[]{:S(2)}) %all-to-all-start.1) | async-done | bytes 4128 | tf_op jit(solution)/shard_map/all_to_all | solution.py:807
  41.8 12.3 %collective-permute-done.5.refs_11_ = bf16[2,64,1536]{2,1,0:T(8,128)(2,1)S(1)} collective-permute-done((bf16[2,64,1536]{2,1,0:T(8,128)(2,1)S(1)}, bf16[2,64,1536]{2,1,0:T(8,128)(2,1)S(1)}, u32[]{:S(2)}, u32[]{:S(2)}) %collective-permute-start.5) | collective-permute-done | bytes 393248 | tf_op jit(solution)/shard_map/ppermute | solution.py:67
  68.2 9.4 %collective-permute-done.10.refs_3_ = bf16[192,1152]{1,0:T(8,128)(2,1)S(1)} collective-permute-done((bf16[192,1152]{1,0:T(8,128)(2,1)S(1)}, bf16[192,1152]{1,0:T(8,128)(2,1)S(1)}, u32[]{:S(2)}, u32[]{:S(2)}) %collective-permute-start.10) | collective-permute-done | bytes 442400 | tf_op jit(solution)/shard_map/ppermute | solution.py:67
  90.0 13.7 %attention_forward.1 = (bf16[2,64,1536]{2,1,0:T(8,128)(2,1)}, bf16[2,64,1536]{2,1,0:T(8,128)(2,1)}, bf16[2,64,1536]{2,1,0:T(8,128)(2,1)}, bf16[2,64,1536]{2,1,0:...) custom-call(s32[8]{0:T(128)} %stack.41.spots_ref, ...), custom_call_target="tpu_custom_call" | custom-call | tf_op jit(solution)/shard_map/attention_forward/pallas_call | solution.py:464
  103.7 11.1 %collective-permute-start.19 = (bf16[5,64,1536]{2,1,0:T(8,128)(2,1)}, bf16[5,64,1536]{2,1,0:T(8,128)(2,1)}, u32[]{:S(2)}, u32[]{:S(2)}) collective-permute-start(bf16[5,64,1536]{2,1,0:T(8,128)(2,1)} %refs_20_), channel_id=1, source_target_pairs={{0,1},{1,0},{2,3},{3,2},{4,5},{5,4},{6,7},{7,6},{8,9},{9,8},{10,11... | collective-permute-start | bytes 2949128 | tf_op jit(solution)/shard_map/ppermute | solution.py:67
  123.4 7.4 %collective-permute-done.22 = bf16[2,64,1536]{2,1,0:T(8,128)(2,1)S(1)} collective-permute-done((bf16[2,64,1536]{2,1,0:T(8,128)(2,1)S(1)}, bf16[2,64,1536]{2,1,0:T(8,128)(2,1)S(1)}, u32[]{:S(2)}, u32[]{:S(2)}) %collective-permute-start.22) | collective-permute-done | bytes 393248 | tf_op jit(solution)/shard_map/ppermute | solution.py:67
  138.4 11.5 %collective-permute-done.25.refs_4_ = bf16[128,1664]{1,0:T(8,128)(2,1)S(1)} collective-permute-done((bf16[128,1664]{1,0:T(8,128)(2,1)S(1)}, bf16[128,1664]{1,0:T(8,128)(2,1)S(1)}, u32[]{:S(2)}, u32[]{:S(2)}) %collective-permute-start.25) | collective-permute-done | bytes 426016 | tf_op jit(solution)/shard_map/ppermute | solution.py:67
  152.7 8.9 %collective-permute-done.27.refs_5_ = bf16[128,1664]{1,0:T(8,128)(2,1)S(1)} collective-permute-done((bf16[128,1664]{1,0:T(8,128)(2,1)S(1)}, bf16[128,1664]{1,0:T(8,128)(2,1)S(1)}, u32[]{:S(2)}, u32[]{:S(2)}) %collective-permute-start.27) | collective-permute-done | bytes 426016 | tf_op jit(solution)/shard_map/ppermute | solution.py:67
  165.0 8.6 %collective-permute-done.29.refs_6_ = bf16[128,1664]{1,0:T(8,128)(2,1)S(1)} collective-permute-done((bf16[128,1664]{1,0:T(8,128)(2,1)S(1)}, bf16[128,1664]{1,0:T(8,128)(2,1)S(1)}, u32[]{:S(2)}, u32[]{:S(2)}) %collective-permute-start.29) | collective-permute-done | bytes 426016 | tf_op jit(solution)/shard_map/ppermute | solution.py:67
  181.3 9.1 %collective-permute-done.32.refs_7_ = bf16[128,1664]{1,0:T(8,128)(2,1)} collective-permute-done((bf16[128,1664]{1,0:T(8,128)(2,1)}, bf16[128,1664]{1,0:T(8,128)(2,1)}, u32[]{:S(2)}, u32[]{:S(2)}) %collective-permute-start.32) | collective-permute-done | bytes 426016 | tf_op jit(solution)/shard_map/ppermute | solution.py:67
  191.7 38.4 %experts.1 = (f32[1024,128]{1,0:T(8,128)}, bf16[1024,1536]{1,0:T(8,128)(2,1)}, bf16[1024,1536]{1,0:T(8,128)(2,1)}, bf16[128,1792]{1,0:T(8,128)(2,1)}, bf16[128,1...) custom-call(s32[12]{0:T(128)} %pad_add_fusion.1.table_ref, ...), custom_call_target="tpu_custom_call" | custom-call | tf_op jit(solution)/shard_map/experts/pallas_call | solution.py:654
  231.0 9.2 %convolution_convert_fusion = bf16[1536,1280]{1,0:T(8,128)(2,1)} fusion(bf16[1024,1536]{1,0:T(8,128)(2,1)} %get-tuple-element.314, bf16[1024,1280]{1,0:T(8,128)(2,1)} %get-tuple-element.306), kind=kOutput, calls=%fused_computation.1 | convolution fusion | flops 4028497920 | bytes 9699328 | tf_op jit(solution)/shard_map/dot_general | solution.py:27
  250.1 6.1 %fusion = bf16[1536,1280]{1,0:T(8,128)(2,1)S(1)} fusion(bf16[1536,1280]{1,0:T(8,128)(2,1)} %collective-permute-done.37, bf16[1024,1536]{1,0:T(8,128)(2,1)S(1)} %copy-done.62, bf16[1024,1280]{1,0:T(8,128)(2,1)S(1)} %copy-done.63), kind=kOutput, calls=%fused_computation.2 | convolution fusion | flops 4032430080 | bytes 13631488 | tf_op jit(solution)/shard_map/dot_general | solution.py:27
  261.6 18.6 %collective-permute-done.40 = bf16[128,1536]{1,0:T(8,128)(2,1)S(1)} collective-permute-done((bf16[128,1536]{1,0:T(8,128)(2,1)S(1)}, bf16[128,1536]{1,0:T(8,128)(2,1)S(1)}, u32[]{:S(2)}, u32[]{:S(2)}) %collective-permute-start.40) | collective-permute-done | bytes 393248 | tf_op jit(solution)/shard_map/ppermute | solution.py:67
  291.9 9.8 %collective-permute-done.43 = bf16[128,1792]{1,0:T(8,128)(2,1)S(1)} collective-permute-done((bf16[128,1792]{1,0:T(8,128)(2,1)S(1)}, bf16[128,1792]{1,0:T(8,128)(2,1)S(1)}, u32[]{:S(2)}, u32[]{:S(2)}) %collective-permute-start.43) | collective-permute-done | bytes 458784 | tf_op jit(solution)/shard_map/ppermute | solution.py:67
  311.9 8.9 %collective-permute-done.48 = bf16[128,1536]{1,0:T(8,128)(2,1)S(1)} collective-permute-done((bf16[128,1536]{1,0:T(8,128)(2,1)S(1)}, bf16[128,1536]{1,0:T(8,128)(2,1)S(1)}, u32[]{:S(2)}, u32[]{:S(2)}) %collective-permute-start.48) | collective-permute-done | bytes 393248 | tf_op jit(solution)/shard_map/ppermute | solution.py:67
  325.0 6.2 %collective-permute-done.53 = bf16[128,1536]{1,0:T(8,128)(2,1)S(1)} collective-permute-done((bf16[128,1536]{1,0:T(8,128)(2,1)S(1)}, bf16[128,1536]{1,0:T(8,128)(2,1)S(1)}, u32[]{:S(2)}, u32[]{:S(2)}) %collective-permute-start.53) | collective-permute-done | bytes 393248 | tf_op jit(solution)/shard_map/ppermute | solution.py:67
  343.3 19.3 %attention_backward.1 = (bf16[2,64,1536]{2,1,0:T(8,128)(2,1)}, bf16[2,64,1536]{2,1,0:T(8,128)(2,1)}, bf16[2,64,1536]{2,1,0:T(8,128)(2,1)}, bf16[2,64,1536]{2,1,0...) custom-call(s32[8]{0:T(128)} %stack.41.spots_ref, ...), custom_call_target="tpu_custom_call" | custom-call | tf_op jit(solution)/shard_map/attention_backward/pallas_call | solution.py:490
  363.6 7.0 %collective-permute-done.57 = bf16[192,1152]{1,0:T(8,128)(2,1)S(1)} collective-permute-done((bf16[192,1152]{1,0:T(8,128)(2,1)}, bf16[192,1152]{1,0:T(8,128)(2,1)S(1)}, u32[]{:S(2)}, u32[]{:S(2)}) %collective-permute-start.57) | collective-permute-done | bytes 442400 | tf_op jit(solution)/shard_map/ppermute | solution.py:67
  374.1 6.5 %collective-permute-start.60 = (bf16[2,64,1536]{2,1,0:T(8,128)(2,1)}, bf16[2,64,1536]{2,1,0:T(8,128)(2,1)S(1)}, u32[]{:S(2)}, u32[]{:S(2)}) collective-permute-start(bf16[2,64,1536]{2,1,0:T(8,128)(2,1)} %get-tuple-element.407), channel_id=1, source_target_pairs={{0,1},{1,0},{2,3},{3,2},{4,5},{5,4},{6,7},{7,6},{8,9},{9,8},{10,11... | collective-permute-start | bytes 1179656 | tf_op jit(solution)/shard_map/ppermute | solution.py:67
  383.8 12.8 %all-to-all-done.3.in_ref = bf16[4,192,1280]{2,1,0:T(8,128)(2,1)S(1)} async-done(((bf16[4,192,1280]{2,1,0:T(8,128)(2,1)}), bf16[4,192,1280]{2,1,0:T(8,128)(2,1)S(1)}, u32[]{:S(2)}, u32[]{:S(2)}) %all-to-all-start.3) | async-done | bytes 1966112 | tf_op jit(solution)/shard_map/all_to_all | solution.py:1023
  409.1 6.7 %collective-permute-done.61 = bf16[192,1152]{1,0:T(8,128)(2,1)S(1)} collective-permute-done((bf16[192,1152]{1,0:T(8,128)(2,1)S(1)}, bf16[192,1152]{1,0:T(8,128)(2,1)S(1)}, u32[]{:S(2)}, u32[]{:S(2)}) %collective-permute-start.61) | collective-permute-done | bytes 442400 | tf_op jit(solution)/shard_map/ppermute | solution.py:67
  432.6 6.0 %all-to-all-start.4 = ((bf16[4,48,768]{2,1,0:T(8,128)(2,1)}), bf16[4,48,768]{2,1,0:T(8,128)(2,1)S(1)}, u32[]{:S(2)}, u32[]{:S(2)}) async-start(bf16[4,48,768]{2,1,0:T(8,128)(2,1)} %bitcast.109), calls=%async_computation.4 | async-start | bytes 589824 | tf_op jit(solution)/shard_map/all_to_all | solution.py:1075
  (369 shorter events, 194.8 us)
Async XLA Ops:
  0.7 20.1 %collective-permute-start = (bf16[2,64,1536]{2,1,0:T(8,128)(2,1)}, bf16[2,64,1536]{2,1,0:T(8,128)(2,1)S(1)}, u32[]{:S(2)}, u32[]{:S(2)}) collective-permute-start(bf16[2,64,1536]{2,1,0:T(8,128)(2,1)} %refs_8_.1), channel_id=1, source_target_pairs={{0,1},{1,0},{2,3},{3,2},{4,5},{5,4},{6,7},{7,6},{8,9},{9,8},{10,11... | collective-permute-start | bytes 1179656 | tf_op jit(solution)/shard_map/ppermute | solution.py:67
  1.4 19.4 %collective-permute-start.1 = (bf16[2,64,1536]{2,1,0:T(8,128)(2,1)}, bf16[2,64,1536]{2,1,0:T(8,128)(2,1)S(1)}, u32[]{:S(2)}, u32[]{:S(2)}) collective-permute-start(bf16[2,64,1536]{2,1,0:T(8,128)(2,1)} %refs_8_.1), channel_id=1, source_target_pairs={{0,2},{1,3},{2,0},{3,1},{4,6},{5,7},{6,4},{7,5},{8,10},{9,11},{10,... | collective-permute-start | bytes 1179656 | tf_op jit(solution)/shard_map/ppermute | solution.py:67
  4.8 16.0 %all-to-all-start = ((bf16[4,48,768]{2,1,0:T(8,128)(2,1)}), bf16[4,48,768]{2,1,0:T(8,128)(2,1)S(1)}, u32[]{:S(2)}, u32[]{:S(2)}) async-start(bf16[4,48,768]{2,1,0:T(8,128)(2,1)} %maximum_bitcast_fusion), calls=%async_computation | async-start | bytes 589824 | tf_op jit(solution)/shard_map/all_to_all | solution.py:765
  20.9 15.1 %collective-permute-start.4 = (bf16[192,1152]{1,0:T(8,128)(2,1)S(1)}, bf16[192,1152]{1,0:T(8,128)(2,1)S(1)}, u32[]{:S(2)}, u32[]{:S(2)}) collective-permute-start(bf16[192,1152]{1,0:T(8,128)(2,1)S(1)} %maximum_maximum_fusion.refs_0_), channel_id=1, source_target_pairs={{0,4},{4,0},{8,12},{12,8},{16,20},{20,16},{24,28},{28,24},{1,5},{5... | collective-permute-start | bytes 1327112 | tf_op jit(solution)/shard_map/ppermute | solution.py:67
  36.1 18.0 %collective-permute-start.9 = (bf16[128,1536]{1,0:T(8,128)(2,1)S(1)}, bf16[128,1536]{1,0:T(8,128)(2,1)S(1)}, u32[]{:S(2)}, u32[]{:S(2)}) collective-permute-start(bf16[128,1536]{1,0:T(8,128)(2,1)S(1)} %bitcast.105), channel_id=1, source_target_pairs={{0,2},{1,3},{2,0},{3,1},{4,6},{5,7},{6,4},{7,5},{8,10},{9,11},{10,... | collective-permute-start | bytes 1179656 | tf_op jit(solution)/shard_map/ppermute | solution.py:67
  39.9 18.9 %collective-permute-start.6 = (bf16[192,1152]{1,0:T(8,128)(2,1)S(1)}, bf16[192,1152]{1,0:T(8,128)(2,1)S(1)}, u32[]{:S(2)}, u32[]{:S(2)}) collective-permute-start(bf16[192,1152]{1,0:T(8,128)(2,1)S(1)} %collective-permute-done.3.refs_1_), channel_id=1, source_target_pairs={{0,8},{4,12},{8,16},{12,20},{16,24},{20,28},{24,0},{28,4},{1,9},{5... | collective-permute-start | bytes 1327112 | tf_op jit(solution)/shard_map/ppermute | solution.py:67
  59.7 17.9 %collective-permute-start.10 = (bf16[192,1152]{1,0:T(8,128)(2,1)S(1)}, bf16[192,1152]{1,0:T(8,128)(2,1)S(1)}, u32[]{:S(2)}, u32[]{:S(2)}) collective-permute-start(bf16[192,1152]{1,0:T(8,128)(2,1)S(1)} %collective-permute-done.6.refs_2_), channel_id=1, source_target_pairs={{0,8},{4,12},{8,16},{12,20},{16,24},{20,28},{24,0},{28,4},{1,9},{5... | collective-permute-start | bytes 1327112 | tf_op jit(solution)/shard_map/ppermute | solution.py:67
  79.6 54.7 %all-to-all-start.2 = ((bf16[4,192,1280]{2,1,0:T(8,128)(2,1)}), bf16[4,192,1280]{2,1,0:T(8,128)(2,1)S(1)}, u32[]{:S(2)}, u32[]{:S(2)}) async-start(bf16[4,192,1280]{2,1,0:T(8,128)(2,1)} %pack_experts.1), calls=%async_computation.2 | async-start | bytes 3932160 | tf_op jit(solution)/shard_map/all_to_all | solution.py:850
  88.4 15.3 %collective-permute-start.18 = (bf16[5,64,1536]{2,1,0:T(8,128)(2,1)}, bf16[5,64,1536]{2,1,0:T(8,128)(2,1)}, u32[]{:S(2)}, u32[]{:S(2)}) collective-permute-start(bf16[5,64,1536]{2,1,0:T(8,128)(2,1)} %refs_20_), channel_id=1, source_target_pairs={{0,4},{4,0},{8,12},{12,8},{16,20},{20,16},{24,28},{28,24},{1,5},{5... | collective-permute-start | bytes 2949128 | tf_op jit(solution)/shard_map/ppermute | solution.py:67
  134.4 43.6 %collective-permute-start.31 = (bf16[4,192,1280]{2,1,0:T(8,128)(2,1)S(1)}, bf16[4,192,1280]{2,1,0:T(8,128)(2,1)}, u32[]{:S(2)}, u32[]{:S(2)}) collective-permute-start(bf16[4,192,1280]{2,1,0:T(8,128)(2,1)S(1)} %all-to-all-done.2.refs_16_), channel_id=1, source_target_pairs={{0,4},{4,0},{8,12},{12,8},{16,20},{20,16},{24,28},{28,24},{1,5},{5... | collective-permute-start | bytes 5898248 | tf_op jit(solution)/shard_map/ppermute | solution.py:67
  135.3 42.6 %collective-permute-start.30 = (bf16[4,192,1280]{2,1,0:T(8,128)(2,1)S(1)}, bf16[4,192,1280]{2,1,0:T(8,128)(2,1)S(1)}, u32[]{:S(2)}, u32[]{:S(2)}) collective-permute-start(bf16[4,192,1280]{2,1,0:T(8,128)(2,1)S(1)} %all-to-all-done.2.refs_16_), channel_id=1, source_target_pairs={{0,1},{1,0},{2,3},{3,2},{4,5},{5,4},{6,7},{7,6},{8,9},{9,8},{10,11... | collective-permute-start | bytes 5898248 | tf_op jit(solution)/shard_map/ppermute | solution.py:67
  257.6 22.6 %collective-permute-start.42 = (bf16[640,1536]{1,0:T(8,128)(2,1)S(1)}, bf16[640,1536]{1,0:T(8,128)(2,1)S(1)}, u32[]{:S(2)}, u32[]{:S(2)}) collective-permute-start(bf16[640,1536]{1,0:T(8,128)(2,1)S(1)} %convolution_convert_fusion.1), channel_id=1, source_target_pairs={{0,1},{1,0},{2,3},{3,2},{4,5},{5,4},{6,7},{7,6},{8,9},{9,8},{10,11... | collective-permute-start | bytes 5898248 | tf_op jit(solution)/shard_map/ppermute | solution.py:67
  258.5 21.7 %collective-permute-start.41 = (bf16[4,192,512]{2,1,0:T(8,128)(2,1)S(1)}, bf16[4,192,512]{2,1,0:T(8,128)(2,1)S(1)}, u32[]{:S(2)}, u32[]{:S(2)}) collective-permute-start(bf16[4,192,512]{2,1,0:T(8,128)(2,1)S(1)} %get-tuple-element.489), channel_id=1, source_target_pairs={{0,4},{4,0},{8,12},{12,8},{16,20},{20,16},{24,28},{28,24},{1,5},{5... | collective-permute-start | bytes 2359304 | tf_op jit(solution)/shard_map/ppermute | solution.py:67
  259.7 20.4 %collective-permute-start.38 = (bf16[128,1792]{1,0:T(8,128)(2,1)S(1)}, bf16[128,1792]{1,0:T(8,128)(2,1)S(1)}, u32[]{:S(2)}, u32[]{:S(2)}) collective-permute-start(bf16[128,1792]{1,0:T(8,128)(2,1)S(1)} %pad_maximum_fusion.2), channel_id=1, source_target_pairs={{0,8},{4,12},{8,16},{12,20},{16,24},{20,28},{24,0},{28,4},{1,9},{5... | collective-permute-start | bytes 1376264 | tf_op jit(solution)/shard_map/ppermute | solution.py:67
  259.8 20.3 %collective-permute-start.39 = (bf16[128,1792]{1,0:T(8,128)(2,1)S(1)}, bf16[128,1792]{1,0:T(8,128)(2,1)S(1)}, u32[]{:S(2)}, u32[]{:S(2)}) collective-permute-start(bf16[128,1792]{1,0:T(8,128)(2,1)S(1)} %copy-done.65), channel_id=1, source_target_pairs={{0,2},{1,3},{2,0},{3,1},{4,6},{5,7},{6,4},{7,5},{8,10},{9,11},{10,... | collective-permute-start | bytes 1376264 | tf_op jit(solution)/shard_map/ppermute | solution.py:67
  260.3 19.8 %collective-permute-start.40 = (bf16[128,1536]{1,0:T(8,128)(2,1)S(1)}, bf16[128,1536]{1,0:T(8,128)(2,1)S(1)}, u32[]{:S(2)}, u32[]{:S(2)}) collective-permute-start(bf16[128,1536]{1,0:T(8,128)(2,1)S(1)} %copy-done.70), channel_id=1, source_target_pairs={{0,2},{1,3},{2,0},{3,1},{4,6},{5,7},{6,4},{7,5},{8,10},{9,11},{10,... | collective-permute-start | bytes 1179656 | tf_op jit(solution)/shard_map/ppermute | solution.py:67
  281.7 20.1 %collective-permute-start.43 = (bf16[128,1792]{1,0:T(8,128)(2,1)S(1)}, bf16[128,1792]{1,0:T(8,128)(2,1)S(1)}, u32[]{:S(2)}, u32[]{:S(2)}) collective-permute-start(bf16[128,1792]{1,0:T(8,128)(2,1)S(1)} %pad_maximum_fusion.3), channel_id=1, source_target_pairs={{0,8},{4,12},{8,16},{12,20},{16,24},{20,28},{24,0},{28,4},{1,9},{5... | collective-permute-start | bytes 1376264 | tf_op jit(solution)/shard_map/ppermute | solution.py:67
  283.0 18.7 %collective-permute-start.44 = (bf16[128,1792]{1,0:T(8,128)(2,1)S(1)}, bf16[128,1792]{1,0:T(8,128)(2,1)S(1)}, u32[]{:S(2)}, u32[]{:S(2)}) collective-permute-start(bf16[128,1792]{1,0:T(8,128)(2,1)S(1)} %copy-done.64), channel_id=1, source_target_pairs={{0,2},{1,3},{2,0},{3,1},{4,6},{5,7},{6,4},{7,5},{8,10},{9,11},{10,... | collective-permute-start | bytes 1376264 | tf_op jit(solution)/shard_map/ppermute | solution.py:67
  284.0 17.7 %collective-permute-start.47 = (bf16[4,192,512]{2,1,0:T(8,128)(2,1)S(1)}, bf16[4,192,512]{2,1,0:T(8,128)(2,1)S(1)}, u32[]{:S(2)}, u32[]{:S(2)}) collective-permute-start(bf16[4,192,512]{2,1,0:T(8,128)(2,1)S(1)} %get-tuple-element.344), channel_id=1, source_target_pairs={{0,4},{4,0},{8,12},{12,8},{16,20},{20,16},{24,28},{28,24},{1,5},{5... | collective-permute-start | bytes 2359304 | tf_op jit(solution)/shard_map/ppermute | solution.py:67
  304.8 16.9 %collective-permute-start.51 = (bf16[2,64,1536]{2,1,0:T(8,128)(2,1)S(1)}, bf16[2,64,1536]{2,1,0:T(8,128)(2,1)S(1)}, u32[]{:S(2)}, u32[]{:S(2)}) collective-permute-start(bf16[2,64,1536]{2,1,0:T(8,128)(2,1)S(1)} %multiply_convert_fusion.refs_8_), channel_id=1, source_target_pairs={{0,2},{1,3},{2,0},{3,1},{4,6},{5,7},{6,4},{7,5},{8,10},{9,11},{10,... | collective-permute-start | bytes 1179656 | tf_op jit(solution)/shard_map/ppermute | solution.py:67
  305.3 16.4 %collective-permute-start.50 = (bf16[2,64,1536]{2,1,0:T(8,128)(2,1)S(1)}, bf16[2,64,1536]{2,1,0:T(8,128)(2,1)S(1)}, u32[]{:S(2)}, u32[]{:S(2)}) collective-permute-start(bf16[2,64,1536]{2,1,0:T(8,128)(2,1)S(1)} %multiply_convert_fusion.refs_8_), channel_id=1, source_target_pairs={{0,1},{1,0},{2,3},{3,2},{4,5},{5,4},{6,7},{7,6},{8,9},{9,8},{10,11... | collective-permute-start | bytes 1179656 | tf_op jit(solution)/shard_map/ppermute | solution.py:67
  337.5 59.1 %all-to-all-start.3 = ((bf16[4,192,1280]{2,1,0:T(8,128)(2,1)}), bf16[4,192,1280]{2,1,0:T(8,128)(2,1)S(1)}, u32[]{:S(2)}, u32[]{:S(2)}) async-start(bf16[4,192,1280]{2,1,0:T(8,128)(2,1)} %pad_maximum_fusion), calls=%async_computation.3 | async-start | bytes 3932160 | tf_op jit(solution)/shard_map/all_to_all | solution.py:1023
  342.2 20.5 %collective-permute-start.56 = (bf16[5,64,1536]{2,1,0:T(8,128)(2,1)}, bf16[5,64,1536]{2,1,0:T(8,128)(2,1)}, u32[]{:S(2)}, u32[]{:S(2)}) collective-permute-start(bf16[5,64,1536]{2,1,0:T(8,128)(2,1)} %get-tuple-element.378), channel_id=1, source_target_pairs={{0,4},{4,0},{8,12},{12,8},{16,20},{20,16},{24,28},{28,24},{1,5},{5... | collective-permute-start | bytes 2949128 | tf_op jit(solution)/shard_map/ppermute | solution.py:67
  432.6 18.3 %all-to-all-start.4 = ((bf16[4,48,768]{2,1,0:T(8,128)(2,1)}), bf16[4,48,768]{2,1,0:T(8,128)(2,1)S(1)}, u32[]{:S(2)}, u32[]{:S(2)}) async-start(bf16[4,48,768]{2,1,0:T(8,128)(2,1)} %bitcast.109), calls=%async_computation.4 | async-start | bytes 589824 | tf_op jit(solution)/shard_map/all_to_all | solution.py:1075
  (120 other events, 1481.9 us)
